TPU v7x, 32 devices: a whole 2x2x4 slice. The times are simulated.
32 devices in a mesh: gx: 2 (over x), gz: 4 (over y, core), ta: 4 (over z).
Axes of the slice: x: 2, y: 2, z: 4, core: 2. Of those that a mesh axis runs over, the one named last changes fastest.
Arguments:
- velocity: bfloat16 [3, 32, 64, 4096], P(None, 'ta', 'gx', 'gz'), may hold values from -6 to 6
- offsets: int32 [7], replicated, may hold values from 0 to 16, as said below
- owner: int32 [7], replicated, may hold values from 0 to 7, as said below
Outputs:
- cross_spectra: float32 [4, 2, 7, 64, 4096], P(None, None, None, 'gx', ('gz', 'ta'))
Inputs may be any that keep to these rules, and one draw needn't show every extreme that they name: `offsets`: each segment of 16 snapshots lies inside the window. owner o names the block of streamwise index o // 4 and spanwise index o mod 4.
All inputs are finite; a program needn't handle non-finite values.
Results may differ from a plain program's by a relative error of at most 0.0062.
Values may be sent and summed in bfloat16 or wider, within the bound.
No kernel may reach another device: no remote copies, remote signals or barrier semaphores. Data moves between devices by JAX's collectives and lax.ppermute only.
A program may use at most 64 MiB of HBM per device.

v0:
```python
import math

import jax
import jax.numpy as jnp
from jax import lax
from jax.sharding import PartitionSpec as P

SEG = 16
NSEG = 7
F = 7


def from_root(shard, axis, root):
    mine = lax.axis_index(axis) == root
    return lax.psum(jnp.where(mine, shard, jnp.zeros_like(shard)), axis)


def padded_2(shard, sides, width):
    for axis, dim in sides:
        devices, length = (lax.axis_size(axis), shard.shape[dim])
        up = [(i, (i + 1) % devices) for i in range(devices)]
        down = [(j, i) for i, j in up]
        last = lax.slice_in_dim(shard, length - width, length, axis=dim)
        first = lax.slice_in_dim(shard, 0, width, axis=dim)
        before = lax.ppermute(last, axis, up)
        after = lax.ppermute(first, axis, down)
        shard = jnp.concatenate([before, shard, after], axis=dim)
    return shard


def dft_table(offsets, step_count_total):
    sample_times = jnp.arange(step_count_total, dtype=jnp.int32)
    temporal_delay = sample_times[None, :] - offsets[:, None]
    inside = (temporal_delay >= 0) & (temporal_delay < SEG)
    window = 0.5 - 0.5 * jnp.cos(2.0 * math.pi / SEG * temporal_delay.astype(jnp.float32))
    frequency = jnp.arange(1, F + 1, dtype=jnp.int32)
    turns = frequency[None, :, None] * temporal_delay[:, None, :] % SEG
    phase_angle = 2.0 * math.pi / SEG * turns.astype(jnp.float32)
    weight = jnp.where(inside, window, jnp.float32(0.0))[:, None, :]
    rows = jnp.stack([weight * jnp.cos(phase_angle), -weight * jnp.sin(phase_angle)], axis=1)
    return rows.reshape(offsets.shape[0] * 2 * F, step_count_total).astype(jnp.bfloat16)


def fourth_order(padded, which_axis, length_cells):

    def shifted(first):
        return lax.slice_in_dim(padded, first, first + length_cells, axis=which_axis)

    return (8.0 * (shifted(3) - shifted(1)) - (shifted(4) - shifted(0))) / 12.0


def spread_series(block_data, root_index):
    return from_root(block_data, ("gx", "gz"), root_index)


def shards(velocity, offsets, owner):
    block_rows = velocity.shape[2]
    block_cols = velocity.shape[3]
    stream_span = jnp.stack([velocity[0], velocity[2]])
    padded = padded_2(stream_span, (("gx", 2), ("gz", 3)), 2).astype(jnp.float32)
    streamwise = padded[0, :, 2 : 2 + block_rows, :]
    spanwise = padded[1, :, :, 2 : 2 + block_cols]
    vorticity = (
        fourth_order(streamwise, 2, block_cols) - fourth_order(spanwise, 1, block_rows)
    ).astype(jnp.bfloat16)
    fields = jnp.concatenate([velocity, vorticity[None]], axis=0)
    step_count_total = velocity.shape[1] * lax.axis_size("ta")
    segment_rows = dft_table(offsets, step_count_total)
    series = lax.all_to_all(fields, "ta", split_axis=3, concat_axis=1, tiled=True)
    flat_series = series.reshape(series.shape[0], series.shape[1], -1)
    power_spectra = jnp.einsum(
        "rt,qtn->qrn", segment_rows, flat_series, preferred_element_type=jnp.float32
    )
    flat_series, power_spectra = (flat_series, power_spectra)
    quantities = flat_series.shape[0]
    cells_here = flat_series.shape[2]
    slab_cols = cells_here // block_rows
    window_rows = dft_table(jnp.zeros((1,), jnp.int32), SEG)
    cospectrum = jnp.zeros((quantities, F, cells_here), jnp.float32)
    quadrature_spectrum = jnp.zeros((quantities, F, cells_here), jnp.float32)
    for segment in range(NSEG):
        local_spec = power_spectra[:, segment * 2 * F : (segment + 1) * 2 * F, :]
        window_piece = lax.dynamic_slice_in_dim(flat_series, offsets[segment], SEG, 1)
        arrived = spread_series(window_piece, owner[segment])
        remote = jnp.einsum("rt,qtn->qrn", window_rows, arrived, preferred_element_type=jnp.float32)
        remote_cos = remote[:, :F]
        remote_sin = remote[:, F:]
        cosine_part_here = local_spec[:, :F]
        local_sin = local_spec[:, F:]
        cospectrum = cospectrum + (remote_cos * cosine_part_here + remote_sin * local_sin)
        quadrature_spectrum = quadrature_spectrum + (
            remote_cos * local_sin - remote_sin * cosine_part_here
        )
    scaling = 8.0 / (3.0 * SEG * NSEG)
    result = jnp.stack([cospectrum, quadrature_spectrum], axis=1) * scaling
    return result.reshape(quantities, 2, F, block_rows, slab_cols)


def solution(mesh):
    in_specs = (P(None, "ta", "gx", "gz"), P(), P())
    out_specs = P(None, None, None, "gx", ("gz", "ta"))
    return jax.shard_map(shards, mesh=mesh, in_specs=in_specs, out_specs=out_specs, check_vma=False)
```

profile of v0, /device:TPU:0, one launch (start us, length us, event | category | flops | bytes accessed | tf_op | source)
XLA Modules:
  0.0 293.2 jit_solution(14867775583435725023)
XLA Ops:
  6.5 1.3 fusion.28
  8.1 3.0 %collective-permute-start = (bf16[2,8,2,1024]{3,1,2,0:T(8,128)(2,1)S(1)}, bf16[2,8,2,1024]{3,1,2,0:T(8,128)(2,1)S(1)}, u32[]{:S(2)}, u32[]{:S(2)}) collective-permute-start(bf16[2,8,2,1024]{3,1,2,0:T(8,128)(2,1)S(1)} %copy.47), channel_id=1, source_target_pairs={{0,16},{16,0},{1,17},{17,1},{2,18},{18,2},{3,19},{19,3},{4,20},{20... | collective-permute-start | bytes 196616 | tf_op jit(solution)/shard_map/ppermute | solution.py:25
  11.2 2.2 collective-permute-done
  14.0 1.5 collective-permute-done.1
  15.7 1.7 collective-permute-start.3
  17.4 6.1 %copy.34 = bf16[3,8,32,1024]{2,1,0,3:T(8,128)(2,1)} copy(bf16[3,8,32,1024]{3,2,1,0:T(8,128)(2,1)S(1)} %copy-done) | data formatting | bytes 3145728 | tf_op args[0]
  23.5 1.4 concatenate.11
  24.8 4.7 %copy.33 = bf16[2,8,36,1028]{2,1,3,0:T(8,128)(2,1)} copy(bf16[2,8,36,1028]{3,1,2,0:T(8,128)(2,1)S(1)} %concatenate.11) | data formatting | bytes 2368512 | tf_op jit(solution)/shard_map/concatenate | solution.py:27
  29.5 2.5 convert_element_type.78
  32.4 1.2 slice_bitcast_fusion
  33.6 4.4 %fusion.8 = bf16[1,8,32,1024]{2,1,0,3:T(8,128)(2,1)} fusion(f32[8,36,1024]{1,0,2:T(8,128)S(1)} %slice_bitcast_fusion.1, f32[8,32,1028]{1,0,2:T(8,128)S(1)} %slice_bitcast_fusion), kind=kLoop, calls=%fused_computation.23 | loop fusion | flops 3145728 | bytes 8912896 | tf_op jit(solution)/shard_map/broadcast_in_dim | solution.py:66
  38.1 6.7 %fusion.33 = bf16[1024,4,8,32]{3,2,1,0:T(8,128)(2,1)} fusion(bf16[1,8,32,1024]{2,1,0,3:T(8,128)(2,1)} %fusion.8, bf16[3,8,32,1024]{2,1,0,3:T(8,128)(2,1)S(1)} %bitcast.65), kind=kLoop, calls=%fused_computation.82 | loop fusion | flops 1048576 | bytes 4194304
  44.8 10.6 %reshape.340 = bf16[4,2,131072]{2,1,0:T(2,128)(2,1)} reshape(bf16[1024,4,8,32]{3,2,1,0:T(8,128)(2,1)} %fusion.33) | data formatting | bytes 4194304
  55.4 5.0 %all-to-all-start = ((bf16[4,2,131072]{2,1,0:T(2,128)(2,1)}), bf16[4,2,131072]{2,1,0:T(2,128)(2,1)S(1)}, u32[]{:S(2)}, u32[]{:S(2)}) async-start(bf16[4,2,131072]{2,1,0:T(2,128)(2,1)} %reshape.340), calls=%async_computation | async-start | bytes 4194304 | tf_op jit(solution)/shard_map/all_to_all | solution.py:69
  60.4 0.7 fusion.32
  69.8 0.7 fusion.31
  79.1 29.5 %all-to-all-done = bf16[4,2,131072]{2,1,0:T(2,128)(2,1)S(1)} async-done(((bf16[4,2,131072]{2,1,0:T(2,128)(2,1)}), bf16[4,2,131072]{2,1,0:T(2,128)(2,1)S(1)}, u32[]{:S(2)}, u32[]{:S(2)}) %all-to-all-start) | async-done | bytes 2097184 | tf_op jit(solution)/shard_map/all_to_all | solution.py:69
  108.6 5.6 %reshape.341 = bf16[1024,4,8,32]{3,2,1,0:T(8,128)(2,1)} reshape(bf16[4,2,131072]{2,1,0:T(2,128)(2,1)S(1)} %all-to-all-done) | data formatting | bytes 4194304
  114.3 8.8 %copy.35 = bf16[4,8,32,4,256]{4,1,2,3,0:T(8,128)(2,1)S(1)} copy(bf16[4,8,32,4,256]{2,1,0,4,3:T(8,128)(2,1)} %bitcast.63) | data formatting | bytes 4194304 | tf_op jit(solution)/shard_map/all_to_all | solution.py:69
  123.1 4.5 %dynamic-slice_select_fusion.6 = (bf16[4,16,8192]{2,1,0:T(8,128)(2,1)}, bf16[4,16,8192]{2,1,0:T(8,128)(2,1)}, bf16[4,16,8192]{2,1,0:T(8,128)(2,1)}, bf16[4,16,81...) fusion(bf16[4,32,8192]{2,1,0:T(8,128)(2,1)S(1)} %bitcast.61, ...), kind=kLoop, calls=%fused_computation.35 | loop fusion | flops 3670016 | bytes 14680099 | tf_op jit(solution)/shard_map/jit(_where)/select_n | solution.py:15
  128.3 7.6 %convolution_bitcast_fusion = f32[4,98,8192]{2,1,0:T(8,128)} fusion(bf16[4,32,8192]{2,1,0:T(8,128)(2,1)S(1)} %bitcast.62, bf16[98,32]{1,0:T(8,128)(2,1)S(1)} %convert_element_type.85), kind=kOutput, calls=%fused_computation | convolution fusion | flops 205520896 | bytes 14948480 | tf_op jit(solution)/shard_map/rt,qtn->qrn/dot_general | solution.py:71
  135.9 105.2 %all-reduce.3.cloned.1.call-done = (bf16[4,16,8192]{2,1,0:T(8,128)(2,1)}, bf16[4,16,8192]{2,1,0:T(8,128)(2,1)}, bf16[4,16,8192]{2,1,0:T(8,128)(2,1)}, bf16[4,16,...) async-done(((bf16[4,16,8192]{2,1,0:T(8,128)(2,1)}, bf16[4,16,8192]{2,1,0:T(8,128)(2,1)}, ...) | async-done | bytes 7340048 | tf_op jit(solution)/shard_map/psum | solution.py:15
  241.1 1.7 convolution_bitcast_fusion.1
  243.3 0.8 copy-done.6
  244.6 1.7 convolution_bitcast_fusion.4
  246.3 1.7 convolution_bitcast_fusion.5
  248.1 1.7 convolution_bitcast_fusion.6
  249.8 1.8 convolution_bitcast_fusion.7
  251.6 15.3 %subtract_add_fusion = f32[4,7,8192]{2,1,0:T(8,128)} fusion(f32[4,98,8192]{2,1,0:T(8,128)} %convolution_bitcast_fusion, f32[4,14,8192]{2,1,0:T(8,128)S(1)} %convolution_bitcast_fusion.1, f32[4,14,8192]{2,1,0:T(8,128)S(1)} %convolution_bitcast_fusion.2, f32[4,14,8192]{2,1,0:T(8,128)S(1)} %convolution_bitcast_fusion.3, ...), kind=kLoop, calls=%fused_computation.27 | loop fusion | flops 6193152 | bytes 26607616 | tf_op jit(solution)/shard_map/add | solution.py:91
  266.9 15.6 %add_add_fusion = f32[4,7,8192]{2,1,0:T(8,128)} fusion(f32[4,98,8192]{2,1,0:T(8,128)} %convolution_bitcast_fusion, f32[4,14,8192]{2,1,0:T(8,128)S(1)} %convolution_bitcast_fusion.1, f32[4,14,8192]{2,1,0:T(8,128)S(1)} %convolution_bitcast_fusion.2, f32[4,14,8192]{2,1,0:T(8,128)S(1)} %convolution_bitcast_fusion.3, ...), kind=kLoop, calls=%fused_computation.28 | loop fusion | flops 6193152 | bytes 26607616 | tf_op jit(solution)/shard_map/add | solution.py:90
  282.6 1.8 reshape.339
  285.1 1.3 copy.39
  (53 shorter events, 3.6 us)
Async XLA Ops:
  7.9 9.5 %copy-start = (bf16[3,8,32,1024]{3,2,1,0:T(8,128)(2,1)S(1)}, bf16[3,8,32,1024]{3,2,1,0:T(8,128)(2,1)}, u32[]{:S(2)}) copy-start(bf16[3,8,32,1024]{3,2,1,0:T(8,128)(2,1)} %param.3) | copy-start | bytes 4718596
  8.1 5.3 %collective-permute-start = (bf16[2,8,2,1024]{3,1,2,0:T(8,128)(2,1)S(1)}, bf16[2,8,2,1024]{3,1,2,0:T(8,128)(2,1)S(1)}, u32[]{:S(2)}, u32[]{:S(2)}) collective-permute-start(bf16[2,8,2,1024]{3,1,2,0:T(8,128)(2,1)S(1)} %copy.47), channel_id=1, source_target_pairs={{0,16},{16,0},{1,17},{17,1},{2,18},{18,2},{3,19},{19,3},{4,20},{20... | collective-permute-start | bytes 196616 | tf_op jit(solution)/shard_map/ppermute | solution.py:25
  11.1 4.3 %collective-permute-start.1 = (bf16[2,8,2,1024]{3,1,2,0:T(8,128)(2,1)S(1)}, bf16[2,8,2,1024]{3,1,2,0:T(8,128)(2,1)S(1)}, u32[]{:S(2)}, u32[]{:S(2)}) collective-permute-start(bf16[2,8,2,1024]{3,1,2,0:T(8,128)(2,1)S(1)} %copy.48), channel_id=1, source_target_pairs={{16,0},{0,16},{17,1},{1,17},{18,2},{2,18},{19,3},{3,19},{20,4},{4,... | collective-permute-start | bytes 196616 | tf_op jit(solution)/shard_map/ppermute | solution.py:26
  15.6 7.9 %collective-permute-start.2 = (bf16[2,8,36,2]{3,1,2,0:T(8,128)(2,1)S(1)}, bf16[2,8,36,2]{3,1,2,0:T(8,128)(2,1)S(1)}, u32[]{:S(2)}, u32[]{:S(2)}) collective-permute-start(bf16[2,8,36,2]{3,1,2,0:T(8,128)(2,1)S(1)} %get-tuple-element.22), channel_id=1, source_target_pairs={{0,4},{4,8},{8,12},{12,0},{1,5},{5,9},{9,13},{13,1},{2,6},{6,10},{... | collective-permute-start | bytes 6920 | tf_op jit(solution)/shard_map/ppermute | solution.py:25
  15.7 7.8 %collective-permute-start.3 = (bf16[2,8,36,2]{3,1,2,0:T(8,128)(2,1)S(1)}, bf16[2,8,36,2]{3,1,2,0:T(8,128)(2,1)S(1)}, u32[]{:S(2)}, u32[]{:S(2)}) collective-permute-start(bf16[2,8,36,2]{3,1,2,0:T(8,128)(2,1)S(1)} %get-tuple-element.21), channel_id=1, source_target_pairs={{4,0},{8,4},{12,8},{0,12},{5,1},{9,5},{13,9},{1,13},{6,2},{10,6},{... | collective-permute-start | bytes 6920 | tf_op jit(solution)/shard_map/ppermute | solution.py:26
  32.3 5.7 %slice-start = ((s8[6291456]{0:T(1024)(128)(4,1)}), s8[4194304]{0:T(1024)(128)(4,1)S(1)}, s32[]{:S(2)}) async-start(s8[6291456]{0:T(1024)(128)(4,1)} %bitcast.64), calls=%async_computation.2 | async-start | bytes 8388608
  33.6 4.5 %slice-start.1 = ((s8[6291456]{0:T(1024)(128)(4,1)}), s8[2097152]{0:T(1024)(128)(4,1)S(1)}, s32[]{:S(2)}) async-start(s8[6291456]{0:T(1024)(128)(4,1)} %bitcast.64), calls=%async_computation.3 | async-start | bytes 4194304
  55.4 5.0 %copy-start.8 = (s32[7]{0:T(128)S(1)}, s32[7]{0:T(128)}, u32[]{:S(2)}) copy-start(s32[7]{0:T(128)} %param.4) | copy-start | bytes 88
  55.4 14.4 %copy-start.9 = (s32[7]{0:T(128)S(1)}, s32[7]{0:T(128)}, u32[]{:S(2)}) copy-start(s32[7]{0:T(128)} %param.5) | copy-start | bytes 88
  55.4 53.3 %all-to-all-start = ((bf16[4,2,131072]{2,1,0:T(2,128)(2,1)}), bf16[4,2,131072]{2,1,0:T(2,128)(2,1)S(1)}, u32[]{:S(2)}, u32[]{:S(2)}) async-start(bf16[4,2,131072]{2,1,0:T(2,128)(2,1)} %reshape.340), calls=%async_computation | async-start | bytes 4194304 | tf_op jit(solution)/shard_map/all_to_all | solution.py:69
  60.4 180.7 %all-reduce.3.cloned.1.call-start = ((), (), s32[]{:S(2)}) async-start(), calls=%async_computation.1 | async-start | bytes 14680064 | tf_op jit(solution)/shard_map/psum | solution.py:15
  241.1 1.7 copy-start.7
  242.9 1.2 copy-start.6
  243.3 1.3 copy-start.5
  244.5 1.8 copy-start.4
  246.3 1.8 copy-start.3
  248.1 1.7 copy-start.2
  282.6 1.8 copy-start.1
Sparse Core Ops, SparseCore 0:
  127.8 113.3 all-reduce.2
where the time goes:
time: 294 us; the launch traced here: 293 us
  waiting for transfers between devices  138 us (47%)
  other arithmetic  50.1 us (17%)
  local copies, waits for them, and re-layouts  46.7 us (16%)
  between operations  31 us (11%)
  matrix products  17.1 us (6%)
  starting transfers between devices  9.91 us (3%)
    psum x1, waiting for transfers between devices, from_root(): return lax.psum(jnp.where(mine, shard, jnp.zeros_like(shard)), axis)  105 us
    all_to_all x1, waiting for transfers between devices, shards(): lax.all_to_all(fields, 'ta', split_axis=3, concat_axis=1, tiled=True)  29.5 us
    unnamed x31, local copies, waits for them, and re-layouts  23.8 us
    add x1, other arithmetic, shards(): cospectrum + (remote_cos * cosine_part_here + remote_sin * local_sin)  15.6 us
    add x1, other arithmetic, shards(): quadrature_spectrum + (remote_cos * local_sin - remote_sin * cosine_part_...  15.3 us
    dot_general x7, matrix products, shards(): jnp.einsum('rt,qtn->qrn', window_rows, arrived, preferred_element_type=jn...  9.5 us
    all_to_all x1, local copies, waits for them, and re-layouts, shards(): lax.all_to_all(fields, 'ta', split_axis=3, concat_axis=1, tiled=True)  8.82 us
    dot_general x1, matrix products, shards(): jnp.einsum('rt,qtn->qrn', segment_rows, flat_series, preferred_element_ty...  7.59 us
  transfers between devices with their start and end apart: 6, of which 4 were waited for; matrix products, arithmetic and copies ran while one was open for 6% of the time, Pallas kernels for 0%

commit v1 on v0

v1 whole, which is shorter than its diff:
```python
import math

import jax
import jax.numpy as jnp
import numpy as np
from jax import lax
from jax.experimental import pallas as pl
from jax.experimental.pallas import tpu as pltpu
from jax.sharding import PartitionSpec as P

SEG = 16
NSEG = 7
F = 7
ROWS = 16
LANES = 128
PARTNERS = 8


class Plan:
    def __init__(self, velocity):
        _, self.tl, self.xb, self.zb = velocity.shape
        self.gx, self.gz, self.ta = (lax.axis_size(a) for a in ("gx", "gz", "ta"))
        self.blocks = self.gx * self.gz
        self.nt = self.tl * self.ta
        self.cs = self.zb // self.ta
        self.cc = self.cs // self.blocks
        self.groups = LANES // self.cc
        self.rg = self.xb // self.groups
        self.chunks = self.zb // self.cc
        assert self.groups * self.rg == self.xb and self.xb * 4 == LANES and self.cc >= 2
        assert self.ta & (self.ta - 1) == 0 and self.blocks & (self.blocks - 1) == 0
        self.by_partner = self.blocks <= PARTNERS
        self.fast = self.rg == 8 and self.tl == 8 and self.cs % LANES == 0


def on_chip(body, inputs, outs, scratch, scalars=(), in_hbm=0, **params):
    count = len(inputs) - in_hbm
    arrays = [pltpu.with_memory_space_constraint(x, pltpu.VMEM) for x in inputs[:count]]
    if not params:
        arrays += [pltpu.with_memory_space_constraint(x, pltpu.HBM) for x in inputs[count:]]
    else:
        arrays += inputs[count:]
    vmem = pl.BlockSpec(memory_space=pltpu.VMEM)
    smem = pl.BlockSpec(memory_space=pltpu.SMEM)
    hbm = pl.BlockSpec(memory_space=pl.ANY)
    return pl.pallas_call(
        body,
        in_specs=[smem] * len(scalars) + [vmem] * count + [hbm] * in_hbm,
        out_specs=jax.tree.map(lambda x: hbm if isinstance(x, jax.ShapeDtypeStruct) else vmem, outs),
        out_shape=outs,
        scratch_shapes=scratch,
        compiler_params=pltpu.CompilerParams(vmem_limit_bytes=24 << 20),
        **params,
    )(*scalars, *arrays)


def dft_rows(offsets, times):
    lag = times[None, :] - offsets[:, None]
    inside = (lag >= 0) & (lag < SEG)
    window = 0.5 - 0.5 * jnp.cos((2.0 * math.pi / SEG) * lag.astype(jnp.float32))
    frequency = jnp.arange(1, 9, dtype=jnp.int32)
    turns = (frequency[None, :, None] * lag[:, None, :]) % SEG
    angle = (2.0 * math.pi / SEG) * turns.astype(jnp.float32)
    keep = inside[:, None, :] & (frequency <= F)[None, :, None]
    weight = jnp.where(keep, window[:, None, :], jnp.float32(0.0))
    rows = jnp.stack([weight * jnp.cos(angle), -weight * jnp.sin(angle)], axis=1)
    return rows.reshape(offsets.shape[0] * ROWS, times.shape[0]).astype(jnp.bfloat16)


def trade(x, axis, step, count):
    return lax.ppermute(x, axis, [(i, i ^ step) for i in range(count)])


def group_swap(plan):
    p = plan
    size = p.groups * p.groups * p.cc
    at = np.arange(size).reshape(p.groups, p.groups, p.cc)
    matrix = np.zeros((size, size), np.float32)
    matrix[at.reshape(-1), at.transpose(1, 0, 2).reshape(-1)] = 1.0
    return jnp.asarray(matrix, jnp.bfloat16)


def side_picks(plan):
    p = plan
    matrix = np.zeros((p.rg, p.groups, p.cc, 2, p.groups, p.rg, 4), np.float32)
    for r in range(p.rg):
        for g in range(p.groups):
            for n in range(2):
                matrix[r, g, p.cc - 2 + n, 0, g, r, n] = 1.0
                matrix[r, g, n, 1, g, r, 2 + n] = 1.0
    return jnp.asarray(matrix.reshape(p.rg * LANES, 2 * LANES), jnp.bfloat16)


def split_slabs(plan, velocity, quantity, place):
    p = plan

    def body(place_ref, velocity_ref, *rest):
        outs, sems = rest[:-1], rest[-1]
        copies = []
        for n, out in enumerate(outs):
            slab = place_ref[0] ^ (n + 1)
            columns = pl.ds(pl.multiple_of(slab * p.cs, LANES), p.cs)
            copies.append(pltpu.make_async_copy(velocity_ref.at[quantity, :, :, columns], out, sems.at[n]))
            copies[-1].start()
        for copy in copies:
            copy.wait()

    outs = [pltpu.VMEM((p.tl, p.xb, p.cs), velocity.dtype) for _ in range(1, p.ta)]
    scratch = [pltpu.SemaphoreType.DMA((p.ta - 1,))]
    return on_chip(body, [velocity], outs, scratch, (place,), in_hbm=1)


def rows_by_snapshot(plan, wide, tiles):
    p = plan
    lhs = []
    for g in range(p.groups):
        rows = [
            wide[tile, pl.ds(g * p.rg + r, p.tl, stride=p.xb), :] for tile in tiles for r in range(p.rg)
        ]
        lhs.append(jnp.concatenate(rows, axis=0).astype(jnp.bfloat16))
    return jnp.concatenate(lhs, axis=1)


def pack_slab(plan, velocity, quantity, arrived, place):
    p = plan
    shape = (p.ta, p.rg, p.tl, LANES)
    if not p.fast:
        own = lax.dynamic_slice_in_dim(velocity[quantity], place[0] * p.cs, p.cs, axis=2)
        x = jnp.stack([own] + list(arrived)).reshape(p.ta, p.tl, p.groups, p.rg, p.blocks, p.cc)
        x = x.transpose(4, 0, 3, 1, 2, 5).reshape((p.blocks,) + shape)
        return [jnp.take(x, place[1] ^ n, axis=0) for n in range(p.blocks)] if p.by_partner else [x]
    assert p.by_partner
    per_slab = p.cs // LANES

    def body(place_ref, swap, *rest):
        others, velocity_ref = rest[: p.ta - 1], rest[p.ta - 1]
        outs = rest[p.ta : p.ta + p.blocks]
        own, sem, wide, chunks = rest[p.ta + p.blocks :]
        columns = pl.ds(pl.multiple_of(place_ref[0] * p.cs, LANES), p.cs)
        copy = pltpu.make_async_copy(velocity_ref.at[quantity, :, :, columns], own, sem.at[0])
        copy.start()
        for m in list(range(1, p.ta)) + [0]:
            if m == 0:
                copy.wait()
            x = own if m == 0 else others[m - 1]
            for i in range(per_slab):
                rows = x[:, :, i * LANES : (i + 1) * LANES].astype(jnp.float32)
                wide[m * per_slab + i] = rows.reshape(p.tl * p.xb, LANES)
        tiles = range(p.ta * per_slab)
        swapped = jnp.dot(
            rows_by_snapshot(p, wide, tiles), swap[...], preferred_element_type=jnp.float32
        ).astype(jnp.bfloat16)
        count = p.rg * p.tl
        for tile in tiles:
            m, i = divmod(tile, per_slab)
            for g in range(p.groups):
                mine = swapped[tile * count : (tile + 1) * count, g * LANES : (g + 1) * LANES]
                chunks[i * p.groups + g, m] = mine.reshape(p.rg, p.tl, LANES)
        for n in range(p.blocks):
            outs[n][...] = chunks[place_ref[1] ^ n]

    outs = [pltpu.VMEM(shape, velocity.dtype) for _ in range(p.blocks)]
    scratch = [
        pltpu.VMEM((p.tl, p.xb, p.cs), velocity.dtype),
        pltpu.SemaphoreType.DMA((1,)),
        pltpu.VMEM((p.zb // LANES, p.tl * p.xb, LANES), jnp.float32),
        pltpu.VMEM((p.blocks,) + shape, velocity.dtype),
    ]
    return on_chip(body, [group_swap(p), *arrived, velocity], outs, scratch, (place,), in_hbm=1)


def pack_all(plan, velocity):
    p = plan
    shape = (p.blocks, p.ta, 2 * p.rg + 1, p.tl, LANES)
    if not p.fast:
        out = []
        for quantity in (2, 0):
            x = velocity[quantity].reshape(p.tl, p.groups, p.rg, p.ta, p.blocks, p.cc)
            out.append(x.transpose(4, 3, 2, 0, 1, 5).reshape(p.blocks, p.ta, p.rg, p.tl, LANES))
        x = velocity[0].reshape(p.tl, p.xb, p.chunks, p.cc)
        before = jnp.roll(x[..., p.cc - 2 :], 1, axis=2)
        after = jnp.roll(x[..., :2], -1, axis=2)
        side = jnp.concatenate([before, after], axis=3).transpose(2, 0, 1, 3)
        out.append(side.reshape(p.ta, p.blocks, 1, p.tl, LANES).swapaxes(0, 1))
        return jnp.concatenate(out, axis=2)
    per_slab = p.cs // LANES
    half = max(p.ta // 2, 1)

    def body(swap_hbm, picks_hbm, velocity_ref, out, x, sems, table_sems, wide, swap, picks, chunks):
        tables = [
            pltpu.make_async_copy(swap_hbm, swap, table_sems.at[0]),
            pltpu.make_async_copy(picks_hbm, picks, table_sems.at[1]),
        ]
        tables[0].start()
        copies = {}
        for n, quantity in enumerate((2, 0)):
            for start in range(0, p.ta, half):
                columns = slice(start * p.cs, (start + half) * p.cs)
                copies[n, start] = pltpu.make_async_copy(
                    velocity_ref.at[quantity, :, :, columns], x.at[n, :, :, columns], sems.at[n, start]
                )
                copies[n, start].start()
        tables[1].start()
        tables[0].wait()
        count = p.rg * p.tl
        for n in range(2):
            for start in range(0, p.ta, half):
                copies[n, start].wait()
                tiles = range(start * per_slab, (start + half) * per_slab)
                for tile in tiles:
                    rows = x[n, :, :, tile * LANES : (tile + 1) * LANES].astype(jnp.float32)
                    wide[tile] = rows.reshape(p.tl * p.xb, LANES)
                swapped = jnp.dot(
                    rows_by_snapshot(p, wide, tiles), swap[...], preferred_element_type=jnp.float32
                )
                for tile in tiles:
                    at = (tile - tiles[0]) * count
                    m, i = divmod(tile, per_slab)
                    for g in range(p.groups):
                        mine = swapped[at : at + count, g * LANES : (g + 1) * LANES]
                        if n == 1:
                            chunks[tile * p.groups + g] = mine
                        out[i * p.groups + g, m, n * p.rg : (n + 1) * p.rg] = mine.reshape(
                            p.rg, p.tl, LANES
                        ).astype(jnp.bfloat16)
        tables[1].wait()
        acc = jnp.zeros((p.chunks * p.tl, 2 * LANES), jnp.float32)
        for r in range(p.rg):
            rows = [chunks[c, r * p.tl : (r + 1) * p.tl, :] for c in range(p.chunks)]
            acc = acc + jnp.dot(
                jnp.concatenate(rows, axis=0).astype(jnp.bfloat16),
                picks[r * LANES : (r + 1) * LANES, :],
                preferred_element_type=jnp.float32,
            )
        for c in range(p.chunks):
            before, after = (c + p.chunks - 1) % p.chunks, (c + 1) % p.chunks
            both = (
                acc[before * p.tl : (before + 1) * p.tl, :LANES]
                + acc[after * p.tl : (after + 1) * p.tl, LANES:]
            )
            out[c % p.blocks, c // p.blocks, 2 * p.rg] = both.astype(jnp.bfloat16)

    swap, picks = group_swap(p), side_picks(p)
    scratch = [
        pltpu.VMEM((2, p.tl, p.xb, p.zb), velocity.dtype),
        pltpu.SemaphoreType.DMA((2, p.ta)),
        pltpu.SemaphoreType.DMA((2,)),
        pltpu.VMEM((p.zb // LANES, p.tl * p.xb, LANES), jnp.float32),
        pltpu.VMEM(swap.shape, swap.dtype),
        pltpu.VMEM(picks.shape, picks.dtype),
        pltpu.VMEM((p.chunks, p.rg * p.tl, LANES), jnp.float32),
    ]
    outs = pltpu.VMEM(shape, velocity.dtype)
    return on_chip(body, [swap, picks, velocity], outs, scratch, in_hbm=3)


def slope_taps(plan):
    p = plan
    tap = {1: 8.0, -1: -8.0, 2: -1.0, -2: 1.0}
    inner = np.zeros((LANES, LANES), np.float32)
    outer = np.zeros((LANES, p.rg, LANES), np.float32)
    for g in range(p.groups):
        for c in range(p.cc):
            to = g * p.cc + c
            for ahead, weight in tap.items():
                at = c + ahead
                if 0 <= at < p.cc:
                    inner[g * p.cc + at, to] = weight
                else:
                    side = at + 2 if at < 0 else at - p.cc + 2
                    for r in range(p.rg):
                        outer[(g * p.rg + r) * 4 + side, r, to] = weight
    return jnp.asarray(inner, jnp.bfloat16), jnp.asarray(outer.reshape(LANES, -1), jnp.bfloat16)


def series_of(ref, b, r):
    x = [ref[b, m, r].astype(jnp.float32) for m in range(ref.shape[1])]
    return jnp.concatenate(x, axis=0)


def vorticity(plan, both, place):
    p = plan
    inner, outer = slope_taps(p)

    def body(place_ref, x, inner_ref, outer_ref, out, sides, slope):
        chunk = place_ref[0] * p.blocks + place_ref[1]
        first = (chunk == 0).astype(jnp.int32)
        last = (chunk == p.chunks - 1).astype(jnp.int32)
        lane = lax.broadcasted_iota(jnp.int32, (p.nt, LANES), 1)
        for a in range(p.gx):
            for z in range(p.gz):
                before = a * p.gz + lax.rem(z + p.gz - first, p.gz)
                after = a * p.gz + lax.rem(z + last, p.gz)
                left = series_of(x, before, 2 * p.rg)
                right = series_of(x, after, 2 * p.rg)
                b = a * p.gz + z
                side = jnp.where(lane % 4 < 2, left, right).astype(jnp.bfloat16)
                sides[b * p.nt : (b + 1) * p.nt, :] = side
        slope[...] = jnp.dot(sides[...], outer_ref[...], preferred_element_type=jnp.float32)

        def row_of(a, z, r):
            shift, r = divmod(r, p.rg)
            own = series_of(x, (a % p.gx) * p.gz + z, r)
            if shift == 0:
                return own
            other = series_of(x, ((a + (1 if shift > 0 else -1)) % p.gx) * p.gz + z, r)
            width = shift * p.cc
            if shift > 0:
                return pltpu.roll(jnp.where(lane < width, other, own), LANES - width, 1)
            return pltpu.roll(jnp.where(lane >= LANES + width, other, own), -width, 1)

        for a in range(p.gx):
            for z in range(p.gz):
                b = a * p.gz + z
                rows = {r: row_of(a, z, r) for r in range(-2, p.rg + 2)}
                for r in range(p.rg):
                    across = 8.0 * (rows[r + 1] - rows[r - 1]) - (rows[r + 2] - rows[r - 2])
                    mine = series_of(x, b, p.rg + r).astype(jnp.bfloat16)
                    along = jnp.dot(mine, inner_ref[...], preferred_element_type=jnp.float32)
                    along = along + slope[b * p.nt : (b + 1) * p.nt, r * LANES : (r + 1) * LANES]
                    spin = (along - across) / 12.0
                    for m in range(p.ta):
                        out[b, m, r] = spin[m * p.tl : (m + 1) * p.tl].astype(jnp.bfloat16)

    outs = pltpu.VMEM((p.blocks, p.ta, p.rg, p.tl, LANES), jnp.bfloat16)
    scratch = [
        pltpu.VMEM((p.blocks * p.nt, LANES), jnp.bfloat16),
        pltpu.VMEM((p.blocks * p.nt, p.rg * LANES), jnp.float32),
    ]
    return on_chip(body, [both, inner, outer], outs, scratch, (place,))


def cross(plan, series, starts, table, owner, place, by_partner):
    p = plan
    scaling = 8.0 / (3.0 * SEG * NSEG)
    pair = 2 if p.rg % 2 == 0 else 1
    width = pair * LANES
    split = len(series) > 1

    def body(owner_ref, place_ref, *refs):
        xs, table_ref = refs[: len(series)], refs[len(series)]
        outs, (spec, ref_spec) = refs[len(series) + 1 : -2], refs[-2:]
        turn = 0
        for q, start in enumerate(starts):
            for r in range(0, p.rg, pair):
                slot = turn % 2
                turn += 1
                for n in range(p.blocks):
                    rows = []
                    for i in range(pair):
                        at = start + r + i
                        if split:
                            x = [xs[n][m, at].astype(jnp.float32) for m in range(p.ta)]
                            rows.append(jnp.concatenate(x, axis=0))
                        else:
                            rows.append(series_of(xs[0], n, at))
                    b = place_ref[1] ^ n if split else n
                    spec[slot, b] = jnp.dot(
                        table_ref[...],
                        jnp.concatenate(rows, axis=1).astype(jnp.bfloat16),
                        preferred_element_type=jnp.float32,
                    )
                for s in range(NSEG):
                    at = s * ROWS
                    ref_spec[slot, at : at + ROWS, :] = spec[slot, owner_ref[s], at : at + ROWS, :]
                for n in range(p.blocks):
                    b = place_ref[1] ^ n if by_partner else n
                    co = jnp.zeros((8, width), jnp.float32)
                    quad = jnp.zeros((8, width), jnp.float32)
                    for s in range(NSEG):
                        at = s * ROWS
                        rc, rs = ref_spec[slot, at : at + 8, :], ref_spec[slot, at + 8 : at + 16, :]
                        qc, qs = spec[slot, b, at : at + 8, :], spec[slot, b, at + 8 : at + 16, :]
                        co = co + (rc * qc + rs * qs)
                        quad = quad + (rc * qs - rs * qc)
                    both = (jnp.concatenate([co, quad], axis=0) * scaling).astype(jnp.bfloat16)
                    for i in range(pair):
                        mine = both[:, i * LANES : (i + 1) * LANES]
                        if by_partner:
                            outs[n][q, r + i] = mine
                        else:
                            outs[0][n, q, r + i] = mine

    shape = (len(starts), p.rg, ROWS, LANES)
    if by_partner:
        outs = [pltpu.VMEM(shape, jnp.bfloat16) for _ in range(p.blocks)]
    else:
        outs = [pltpu.VMEM((p.blocks,) + shape, jnp.bfloat16)]
    scratch = [
        pltpu.VMEM((2, p.blocks, NSEG * ROWS, width), jnp.float32),
        pltpu.VMEM((2, NSEG * ROWS, width), jnp.float32),
    ]
    return on_chip(body, [*series, table], outs, scratch, (owner, place))


def assemble(plan, so_far, quantities, pieces, place):
    p = plan
    shape = (4, 2, F, p.xb, p.cs)
    if not p.fast:
        if len(pieces) > 1:
            x = jnp.stack(pieces)
            x = jnp.take(x, jnp.arange(p.blocks, dtype=jnp.int32) ^ place[1], axis=0)
        else:
            x = pieces[0]
        out = jnp.zeros(shape, jnp.float32) if so_far is None else so_far
        x = x.reshape(p.blocks, len(quantities), p.rg, 2, 8, p.groups, p.cc)[:, :, :, :, :F]
        x = x.transpose(1, 3, 4, 5, 2, 0, 6).reshape((-1,) + shape[1:]).astype(jnp.float32)
        for n, quantity in enumerate(quantities):
            out = out.at[quantity].set(x[n])
        return out

    def body(place_ref, *refs):
        xs, swap = refs[: len(pieces)], refs[len(pieces)]
        out, by_chunk, wide, held, sems = refs[-5:]
        copies = []
        for n, quantity in enumerate(quantities):
            for j in range(p.blocks):
                if len(pieces) > 1:
                    by_chunk[place_ref[1] ^ j] = xs[j][n].reshape(p.rg * ROWS, LANES)
                else:
                    by_chunk[j] = xs[0][j, n].reshape(p.rg * ROWS, LANES)
            for tile in range(p.cs // LANES):
                lhs = [by_chunk[tile * p.groups + i] for i in range(p.groups)]
                swapped = jnp.dot(
                    jnp.concatenate(lhs, axis=1), swap[...], preferred_element_type=jnp.float32
                )
                for g in range(p.groups):
                    wide[tile, g] = swapped[:, g * LANES : (g + 1) * LANES]
            for part in range(2):
                for k in range(F):
                    for tile in range(p.cs // LANES):
                        for g in range(p.groups):
                            block = wide[tile, g, pl.ds(part * 8 + k, p.rg, stride=ROWS), :]
                            rows = slice(g * p.rg, (g + 1) * p.rg)
                            held[n, part, k, rows, tile * LANES : (tile + 1) * LANES] = block
                copies.append(
                    pltpu.make_async_copy(held.at[n, part], out.at[quantity, part], sems.at[n, part])
                )
                copies[-1].start()
        for copy in copies:
            copy.wait()

    before = [] if so_far is None else [so_far]
    scratch = [
        pltpu.VMEM((p.blocks, p.rg * ROWS, LANES), jnp.bfloat16),
        pltpu.VMEM((p.cs // LANES, p.groups, p.rg * ROWS, LANES), jnp.float32),
        pltpu.VMEM((len(quantities),) + shape[1:], jnp.float32),
        pltpu.SemaphoreType.DMA((len(quantities), 2)),
    ]
    return on_chip(
        body,
        [*pieces, group_swap(p)] + before,
        jax.ShapeDtypeStruct(shape, jnp.float32),
        scratch,
        (place,),
        in_hbm=len(before),
        **({"input_output_aliases": {len(pieces) + 2: 0}} if before else {}),
    )


def shards(velocity, offsets, owner):
    plan = Plan(velocity)
    block_axes = ("gx", "gz")
    time = lax.axis_index("ta").astype(jnp.int32)
    place = jnp.stack([time, lax.axis_index(block_axes).astype(jnp.int32)])

    slabs = split_slabs(plan, velocity, 1, place)
    slabs = [trade(x, "ta", n + 1, plan.ta) for n, x in enumerate(slabs)]
    both = pack_all(plan, velocity)
    both = both.reshape((-1,) + both.shape[2:])
    both = lax.all_to_all(both, block_axes + ("ta",), split_axis=0, concat_axis=0, tiled=True)
    both = both.reshape((plan.blocks, plan.ta) + both.shape[1:])

    def over_blocks(arrays):
        if len(arrays) == 1:
            return [lax.all_to_all(arrays[0], block_axes, split_axis=0, concat_axis=0, tiled=True)]
        return [arrays[0]] + [trade(arrays[n], block_axes, n, plan.blocks) for n in range(1, plan.blocks)]

    wall = pack_slab(plan, velocity, 1, slabs, place)
    wall = over_blocks(wall)
    times = jnp.arange(plan.tl, dtype=jnp.int32)[None, :]
    turn = jnp.arange(plan.ta, dtype=jnp.int32)[:, None]
    table_wall = dft_rows(offsets, ((turn ^ time) * plan.tl + times).reshape(-1))
    table = dft_rows(offsets, (turn * plan.tl + times).reshape(-1))
    wall = cross(plan, wall, (0,), table_wall, owner, place, plan.by_partner)
    wall = over_blocks(wall)
    out = assemble(plan, None, (1,), wall, place)

    pieces = cross(plan, [both], (0, plan.rg), table, owner, place, False)
    pieces = over_blocks(pieces)
    spin = vorticity(plan, both, place)
    spin = cross(plan, [spin], (0,), table, owner, place, plan.by_partner)
    spin = over_blocks(spin)
    out = assemble(plan, out, (2, 0), pieces, place)
    return assemble(plan, out, (3,), spin, place)


def solution(mesh):
    in_specs = (P(None, "ta", "gx", "gz"), P(), P())
    out_specs = P(None, None, None, "gx", ("gz", "ta"))

    return jax.shard_map(shards, mesh=mesh, in_specs=in_specs, out_specs=out_specs, check_vma=False)
```

time: 294 us -> 100 us (0.34)
  waiting for transfers between devices: 138 us -> 40.8 us
  other arithmetic: 50.1 us -> 0.86 us
  local copies, waits for them, and re-layouts: 46.7 us -> 0.2 us
  between operations: 31 us -> 0.23 us
  starting transfers between devices: 9.91 us -> 35.4 us
  Pallas kernels: 0 us -> 22.2 us
  matrix products: 17.1 us -> 0 us
    psum x1 -> x0, waiting for transfers between devices: 105 us -> none  [from_root(): return lax.psum(jnp.where(mine, shard, jnp.zeros_like(shard)), axis)]
    add x3, other arithmetic: 31 us -> 0.15 us  [the longest x1 0.07 us: shards(): (turn ^ time) * plan.tl + times]
    unnamed x31 -> x10, local copies, waits for them, and re-layouts: 23.8 us -> 0.03 us
    pallas_call x0 -> x10, Pallas kernels: none -> 22.2 us  [on_chip(): pl.pallas_call(body, in_specs=[smem] * len(scalars) + [vmem] * count + [h...]
    ppermute x4 -> x24, starting transfers between devices: 4.91 us -> 24.1 us  [trade(): return lax.ppermute(x, axis, [(i, i ^ step) for i in range(count)])]
    dot_general x8 -> x0, matrix products: 17.1 us -> none  [the longest x7 9.5 us: shards(): jnp.einsum('rt,qtn->qrn', window_rows, arrived, preferred_element_type=jn...]
    ppermute x4 -> x24, waiting for transfers between devices: 3.66 us -> 15.6 us  [trade(): return lax.ppermute(x, axis, [(i, i ^ step) for i in range(count)])]
    all_to_all x1 -> x0, local copies, waits for them, and re-layouts: 8.82 us -> none  [shards(): lax.all_to_all(fields, 'ta', split_axis=3, concat_axis=1, tiled=True)]
  transfers between devices with their start and end apart: 6 -> 26, of which waited for: 4 -> 7; matrix products, arithmetic and copies ran while one was open for 6% -> 1% of each run, Pallas kernels for 0% -> 12%
where the time goes in v1:
time: 100 us; the launch traced here: 99.8 us
  waiting for transfers between devices  40.8 us (41%)
  starting transfers between devices  35.4 us (35%)
  Pallas kernels  22.2 us (22%)
    all_to_all x1, waiting for transfers between devices, shards(): lax.all_to_all(both, block_axes + ('ta',), split_axis=0, concat_axis=0, t...  25.2 us
    ppermute x24, starting transfers between devices, trade(): return lax.ppermute(x, axis, [(i, i ^ step) for i in range(count)])  24.1 us
    pallas_call x10, Pallas kernels, on_chip(): pl.pallas_call(body, in_specs=[smem] * len(scalars) + [vmem] * count + [h...  22.2 us
    ppermute x24, waiting for transfers between devices, trade(): return lax.ppermute(x, axis, [(i, i ^ step) for i in range(count)])  15.6 us
    all_to_all x1, starting transfers between devices, shards(): lax.all_to_all(both, block_axes + ('ta',), split_axis=0, concat_axis=0, t...  7.33 us
    all_to_all x1, starting transfers between devices, over_blocks(): lax.all_to_all(arrays[0], block_axes, split_axis=0, concat_axis=0, tiled=...  4.05 us
  transfers between devices with their start and end apart: 26, of which 7 were waited for; matrix products, arithmetic and copies ran while one was open for 1% of the time, Pallas kernels for 12%

profile of v1, /device:TPU:0, one launch (start us, length us, event | category | flops | bytes accessed | tf_op | source)
XLA Modules:
  0.0 99.8 jit_solution(8953591359072243748)
XLA Ops:
  0.0 5.2 %shard_map.109 = bf16[8,4,17,8,128]{4,3,2,1,0:T(8,128)(2,1)} custom-call(bf16[512,512]{1,0:T(8,128)(2,1)} %constant.58.clone.swap_hbm.swap.refs_8_.refs_1_, bf16[1024,256]{1,0:T(8,128)(2,1)} %constant.59.clone.picks_hbm, bf16[3,8,32,1024]{3,2,1,0:T(8,128)(2,1)} %rest_3_.1), custom_call_target="tpu_custom_call" | custom-call | tf_op jit(solution)/shard_map/pallas_call | solution.py:46
  5.2 7.3 %all-to-all-start = ((bf16[32,17,8,128]{3,2,1,0:T(8,128)(2,1)}), bf16[32,17,8,128]{3,2,1,0:T(8,128)(2,1)S(1)}, u32[]{:S(2)}, u32[]{:S(2)}) async-start(bf16[32,17,8,128]{3,2,1,0:T(8,128)(2,1)} %bitcast.2), calls=%async_computation | async-start | bytes 2228224 | tf_op jit(solution)/shard_map/all_to_all | solution.py:471
  13.6 25.2 %all-to-all-done = bf16[32,17,8,128]{3,2,1,0:T(8,128)(2,1)S(1)} async-done(((bf16[32,17,8,128]{3,2,1,0:T(8,128)(2,1)}), bf16[32,17,8,128]{3,2,1,0:T(8,128)(2,1)S(1)}, u32[]{:S(2)}, u32[]{:S(2)}) %all-to-all-start) | async-done | bytes 1114144 | tf_op jit(solution)/shard_map/all_to_all | solution.py:471
  38.9 3.1 %shard_map.112 = bf16[8,2,8,16,128]{4,3,2,1,0:T(8,128)(2,1)} custom-call(s32[7]{0:T(128)S(1)} %copy-done.3, s32[2]{0:T(128)S(1)} %pad_add_fusion.place_ref, bf16[8,4,17,8,128]{4,3,2,1,0:T(8,128)(2,1)S(1)} %bitcast.6, bf16[112,32]{1,0:T(8,128)(2,1)S(1)} %bitcast.8), custom_call_target="tpu_custom_call" | custom-call | tf_op jit(solution)/shard_map/pallas_call | solution.py:46
  41.9 4.1 %all-to-all-start.1 = ((bf16[8,2,8,16,128]{4,3,2,1,0:T(8,128)(2,1)}), bf16[8,2,8,16,128]{4,3,2,1,0:T(8,128)(2,1)S(1)}, u32[]{:S(2)}, u32[]{:S(2)}) async-start(bf16[8,2,8,16,128]{4,3,2,1,0:T(8,128)(2,1)} %shard_map.112), calls=%async_computation.1 | async-start | bytes 1048576 | tf_op jit(solution)/shard_map/all_to_all | solution.py:476
  46.0 1.6 %shard_map.113 = (bf16[8,32,256]{2,1,0:T(8,128)(2,1)S(1)}, bf16[8,32,256]{2,1,0:T(8,128)(2,1)S(1)}, bf16[8,32,256]{2,1,0:T(8,128)(2,1)S(1)}) custom-call(s32[2]{0:T(128)S(1)} %pad_add_fusion.place_ref, bf16[3,8,32,1024]{3,2,1,0:T(8,128)(2,1)} %rest_3_.1), custom_call_target="tpu_custom_call" | custom-call | tf_op jit(solution)/shard_map/pallas_call | solution.py:46
  47.6 2.7 %collective-permute-start.7 = (bf16[8,32,256]{2,1,0:T(8,128)(2,1)S(1)}, bf16[8,32,256]{2,1,0:T(8,128)(2,1)S(1)}, u32[]{:S(2)}, u32[]{:S(2)}) collective-permute-start(bf16[8,32,256]{2,1,0:T(8,128)(2,1)S(1)} %get-tuple-element.40), channel_id=1, source_target_pairs={{0,1},{1,0},{2,3},{3,2},{4,5},{5,4},{6,7},{7,6},{8,9},{9,8},{10,11... | collective-permute-start | bytes 393224 | tf_op jit(solution)/shard_map/ppermute | solution.py:71
  51.0 1.7 %collective-permute-start.9 = (bf16[8,32,256]{2,1,0:T(8,128)(2,1)S(1)}, bf16[8,32,256]{2,1,0:T(8,128)(2,1)S(1)}, u32[]{:S(2)}, u32[]{:S(2)}) collective-permute-start(bf16[8,32,256]{2,1,0:T(8,128)(2,1)S(1)} %get-tuple-element.42), channel_id=1, source_target_pairs={{0,3},{1,2},{2,1},{3,0},{4,7},{5,6},{6,5},{7,4},{8,11},{9,10},{10,... | collective-permute-start | bytes 393224 | tf_op jit(solution)/shard_map/ppermute | solution.py:71
  52.7 2.3 %collective-permute-done.7.rest_0_ = bf16[8,32,256]{2,1,0:T(8,128)(2,1)S(1)} collective-permute-done((bf16[8,32,256]{2,1,0:T(8,128)(2,1)S(1)}, bf16[8,32,256]{2,1,0:T(8,128)(2,1)S(1)}, u32[]{:S(2)}, u32[]{:S(2)}) %collective-permute-start.7) | collective-permute-done | bytes 131104 | tf_op jit(solution)/shard_map/ppermute | solution.py:71
  55.0 7.9 %collective-permute-done.8.rest_1_ = bf16[8,32,256]{2,1,0:T(8,128)(2,1)S(1)} collective-permute-done((bf16[8,32,256]{2,1,0:T(8,128)(2,1)S(1)}, bf16[8,32,256]{2,1,0:T(8,128)(2,1)S(1)}, u32[]{:S(2)}, u32[]{:S(2)}) %collective-permute-start.8) | collective-permute-done | bytes 131104 | tf_op jit(solution)/shard_map/ppermute | solution.py:71
  62.9 2.2 %shard_map.114 = (bf16[4,8,8,128]{3,2,1,0:T(8,128)(2,1)S(1)}, bf16[4,8,8,128]{3,2,1,0:T(8,128)(2,1)S(1)}, bf16[4,8,8,128]{3,2,1,0:T(8,128)(2,1)S(1)}, bf16[4,8,8...) custom-call(s32[2]{0:T(128)S(1)} %pad_add_fusion.place_ref, ...), custom_call_target="tpu_custom_call" | custom-call | tf_op jit(solution)/shard_map/pallas_call | solution.py:46
  65.2 1.7 %collective-permute-start.11 = (bf16[4,8,8,128]{3,2,1,0:T(8,128)(2,1)S(1)}, bf16[4,8,8,128]{3,2,1,0:T(8,128)(2,1)S(1)}, u32[]{:S(2)}, u32[]{:S(2)}) collective-permute-start(bf16[4,8,8,128]{3,2,1,0:T(8,128)(2,1)S(1)} %get-tuple-element.45), channel_id=1, source_target_pairs={{0,8},{4,12},{8,0},{12,4},{16,24},{20,28},{24,16},{28,20},{1,9},{5... | collective-permute-start | bytes 196616 | tf_op jit(solution)/shard_map/ppermute | solution.py:71
  67.0 1.7 %collective-permute-start.13 = (bf16[4,8,8,128]{3,2,1,0:T(8,128)(2,1)S(1)}, bf16[4,8,8,128]{3,2,1,0:T(8,128)(2,1)S(1)}, u32[]{:S(2)}, u32[]{:S(2)}) collective-permute-start(bf16[4,8,8,128]{3,2,1,0:T(8,128)(2,1)S(1)} %get-tuple-element.47), channel_id=1, source_target_pairs={{0,16},{4,20},{8,24},{12,28},{16,0},{20,4},{24,8},{28,12},{1,17},{... | collective-permute-start | bytes 196616 | tf_op jit(solution)/shard_map/ppermute | solution.py:71
  68.7 2.6 %collective-permute-start.15 = (bf16[4,8,8,128]{3,2,1,0:T(8,128)(2,1)S(1)}, bf16[4,8,8,128]{3,2,1,0:T(8,128)(2,1)S(1)}, u32[]{:S(2)}, u32[]{:S(2)}) collective-permute-start(bf16[4,8,8,128]{3,2,1,0:T(8,128)(2,1)S(1)} %get-tuple-element.49), channel_id=1, source_target_pairs={{0,24},{4,28},{8,16},{12,20},{16,8},{20,12},{24,0},{28,4},{1,25},{... | collective-permute-start | bytes 196616 | tf_op jit(solution)/shard_map/ppermute | solution.py:71
  71.5 1.4 %collective-permute-done.14.refs_5_ = bf16[4,8,8,128]{3,2,1,0:T(8,128)(2,1)S(1)} collective-permute-done((bf16[4,8,8,128]{3,2,1,0:T(8,128)(2,1)S(1)}, bf16[4,8,8,128]{3,2,1,0:T(8,128)(2,1)S(1)}, u32[]{:S(2)}, u32[]{:S(2)}) %collective-permute-start.14) | collective-permute-done | bytes 65568 | tf_op jit(solution)/shard_map/ppermute | solution.py:71
  72.8 2.8 %collective-permute-done.15.refs_6_ = bf16[4,8,8,128]{3,2,1,0:T(8,128)(2,1)S(1)} collective-permute-done((bf16[4,8,8,128]{3,2,1,0:T(8,128)(2,1)S(1)}, bf16[4,8,8,128]{3,2,1,0:T(8,128)(2,1)S(1)}, u32[]{:S(2)}, u32[]{:S(2)}) %collective-permute-start.15) | collective-permute-done | bytes 65568 | tf_op jit(solution)/shard_map/ppermute | solution.py:71
  75.6 1.0 %collective-permute-done.16.refs_7_ = bf16[4,8,8,128]{3,2,1,0:T(8,128)(2,1)S(1)} collective-permute-done((bf16[4,8,8,128]{3,2,1,0:T(8,128)(2,1)S(1)}, bf16[4,8,8,128]{3,2,1,0:T(8,128)(2,1)S(1)}, u32[]{:S(2)}, u32[]{:S(2)}) %collective-permute-start.16) | collective-permute-done | bytes 65568 | tf_op jit(solution)/shard_map/ppermute | solution.py:71
  76.6 1.6 %shard_map.115 = (bf16[1,8,16,128]{3,2,1,0:T(8,128)(2,1)S(1)}, bf16[1,8,16,128]{3,2,1,0:T(8,128)(2,1)S(1)}, bf16[1,8,16,128]{3,2,1,0:T(8,128)(2,1)S(1)}, bf16[1,...) custom-call(s32[7]{0:T(128)S(1)} %copy-done.3, ...), custom_call_target="tpu_custom_call" | custom-call | tf_op jit(solution)/shard_map/pallas_call | solution.py:46
  79.0 1.2 %collective-permute-start.19 = (bf16[1,8,16,128]{3,2,1,0:T(8,128)(2,1)S(1)}, bf16[1,8,16,128]{3,2,1,0:T(8,128)(2,1)S(1)}, u32[]{:S(2)}, u32[]{:S(2)}) collective-permute-start(bf16[1,8,16,128]{3,2,1,0:T(8,128)(2,1)S(1)} %get-tuple-element.54), channel_id=1, source_target_pairs={{0,12},{4,8},{8,4},{12,0},{16,28},{20,24},{24,20},{28,16},{1,13},{... | collective-permute-start | bytes 98312 | tf_op jit(solution)/shard_map/ppermute | solution.py:71
  80.2 0.9 collective-permute-start.20
  81.1 0.8 collective-permute-start.21
  81.9 1.4 %shard_map.110.refs_0_ = bf16[8,4,8,8,128]{4,3,2,1,0:T(8,128)(2,1)S(1)} custom-call(s32[2]{0:T(128)S(1)} %pad_add_fusion.place_ref, bf16[8,4,17,8,128]{4,3,2,1,0:T(8,128)(2,1)S(1)} %bitcast.7, bf16[128,128]{1,0:T(8,128)(2,1)S(1)} %copy-done.2, bf16[128,1024]{1,0:T(8,128)(2,1)S(1)} %copy-done.1), custom_call_target="tpu_custom_call" | custom-call | tf_op jit(solution)/shard_map/pallas_call | solution.py:46
  83.3 1.6 %shard_map.111 = (bf16[1,8,16,128]{3,2,1,0:T(8,128)(2,1)S(1)}, bf16[1,8,16,128]{3,2,1,0:T(8,128)(2,1)S(1)}, bf16[1,8,16,128]{3,2,1,0:T(8,128)(2,1)S(1)}, bf16[1,...) custom-call(s32[7]{0:T(128)S(1)} %copy-done.3, ...), custom_call_target="tpu_custom_call" | custom-call | tf_op jit(solution)/shard_map/pallas_call | solution.py:46
  84.9 1.5 %collective-permute-start.22 = (bf16[1,8,16,128]{3,2,1,0:T(8,128)(2,1)S(1)}, bf16[1,8,16,128]{3,2,1,0:T(8,128)(2,1)S(1)}, u32[]{:S(2)}, u32[]{:S(2)}) collective-permute-start(bf16[1,8,16,128]{3,2,1,0:T(8,128)(2,1)S(1)} %get-tuple-element.57), channel_id=1, source_target_pairs={{0,24},{4,28},{8,16},{12,20},{16,8},{20,12},{24,0},{28,4},{1,25},{... | collective-permute-start | bytes 98312 | tf_op jit(solution)/shard_map/ppermute | solution.py:71
  86.5 1.2 %collective-permute-start.23 = (bf16[1,8,16,128]{3,2,1,0:T(8,128)(2,1)S(1)}, bf16[1,8,16,128]{3,2,1,0:T(8,128)(2,1)S(1)}, u32[]{:S(2)}, u32[]{:S(2)}) collective-permute-start(bf16[1,8,16,128]{3,2,1,0:T(8,128)(2,1)S(1)} %get-tuple-element.58), channel_id=1, source_target_pairs={{0,28},{4,24},{8,20},{12,16},{16,12},{20,8},{24,4},{28,0},{1,29},{... | collective-permute-start | bytes 98312 | tf_op jit(solution)/shard_map/ppermute | solution.py:71
  88.6 0.9 collective-permute-start.2
  89.8 1.4 %collective-permute-start.3 = (bf16[1,8,16,128]{3,2,1,0:T(8,128)(2,1)S(1)}, bf16[1,8,16,128]{3,2,1,0:T(8,128)(2,1)S(1)}, u32[]{:S(2)}, u32[]{:S(2)}) collective-permute-start(bf16[1,8,16,128]{3,2,1,0:T(8,128)(2,1)S(1)} %get-tuple-element.36), channel_id=1, source_target_pairs={{0,16},{4,20},{8,24},{12,28},{16,0},{20,4},{24,8},{28,12},{1,17},{... | collective-permute-start | bytes 98312 | tf_op jit(solution)/shard_map/ppermute | solution.py:71
  91.6 1.9 %collective-permute-start.5 = (bf16[1,8,16,128]{3,2,1,0:T(8,128)(2,1)S(1)}, bf16[1,8,16,128]{3,2,1,0:T(8,128)(2,1)S(1)}, u32[]{:S(2)}, u32[]{:S(2)}) collective-permute-start(bf16[1,8,16,128]{3,2,1,0:T(8,128)(2,1)S(1)} %get-tuple-element.38), channel_id=1, source_target_pairs={{0,24},{4,28},{8,16},{12,20},{16,8},{20,12},{24,0},{28,4},{1,25},{... | collective-permute-start | bytes 98312 | tf_op jit(solution)/shard_map/ppermute | solution.py:71
  93.5 0.7 collective-permute-start.6
  94.2 1.7 %shard_map.116.refs_2_ = f32[4,2,7,32,256]{4,3,2,1,0:T(8,128)} custom-call(s32[2]{0:T(128)S(1)} %pad_add_fusion.place_ref, bf16[1,8,16,128]{3,2,1,0:T(8,128)(2,1)S(1)} %get-tuple-element.51.refs_0_, bf16[1,8,16,128]{3,2,1,0:T(8,128)(2,1)S(1)} %collective-permute-done.17.refs_1_, bf16[1,8,16,128]{3,2,1,0:T(8,128)(2,1)S(1)} %collective-permute-done.18.refs_2_, ...), custom_call_target="tpu_custom_call" | custom-call | tf_op jit(solution)/shard_map/pallas_call | solution.py:46
  96.0 2.1 %shard_map.117.refs_9_ = f32[4,2,7,32,256]{4,3,2,1,0:T(8,128)} custom-call(s32[2]{0:T(128)S(1)} %pad_add_fusion.place_ref, bf16[8,2,8,16,128]{4,3,2,1,0:T(8,128)(2,1)S(1)} %all-to-all-done.1.refs_0_, bf16[512,512]{1,0:T(8,128)(2,1)S(1)} %copy-done, f32[4,2,7,32,256]{4,3,2,1,0:T(8,128)} %shard_map.116.refs_2_), custom_call_target="tpu_custom_call", output_to_operand_aliasing={{}: (3, {})} | custom-call | tf_op jit(solution)/shard_map/pallas_call | solution.py:46
  98.1 1.7 %shard_map.118 = f32[4,2,7,32,256]{4,3,2,1,0:T(8,128)} custom-call(s32[2]{0:T(128)S(1)} %pad_add_fusion.place_ref, bf16[1,8,16,128]{3,2,1,0:T(8,128)(2,1)S(1)} %get-tuple-element.32.refs_0_, bf16[1,8,16,128]{3,2,1,0:T(8,128)(2,1)S(1)} %collective-permute-done.refs_1_, ...), custom_call_target="tpu_custom_call", output_to_operand_aliasing={{}: (10, {})} | custom-call | tf_op jit(solution)/shard_map/pallas_call | solution.py:46
  (55 shorter events, 4.5 us)
Async XLA Ops:
  5.2 7.8 %copy-start.4 = (s32[7]{0:T(128)S(1)}, s32[7]{0:T(128)}, u32[]{:S(2)}) copy-start(s32[7]{0:T(128)} %param.12) | copy-start | bytes 88
  5.2 33.6 %copy-start.3 = (s32[7]{0:T(128)S(1)}, s32[7]{0:T(128)}, u32[]{:S(2)}) copy-start(s32[7]{0:T(128)} %owner_ref.5) | copy-start | bytes 88
  5.2 33.6 %all-to-all-start = ((bf16[32,17,8,128]{3,2,1,0:T(8,128)(2,1)}), bf16[32,17,8,128]{3,2,1,0:T(8,128)(2,1)S(1)}, u32[]{:S(2)}, u32[]{:S(2)}) async-start(bf16[32,17,8,128]{3,2,1,0:T(8,128)(2,1)} %bitcast.2), calls=%async_computation | async-start | bytes 2228224 | tf_op jit(solution)/shard_map/all_to_all | solution.py:471
  38.9 24.0 %copy-start = (bf16[512,512]{1,0:T(8,128)(2,1)S(1)}, bf16[512,512]{1,0:T(8,128)(2,1)}, u32[]{:S(2)}) copy-start(bf16[512,512]{1,0:T(8,128)(2,1)} %constant.58.clone.swap_hbm.swap.refs_8_.refs_1_) | copy-start | bytes 1572868
  41.9 54.0 %all-to-all-start.1 = ((bf16[8,2,8,16,128]{4,3,2,1,0:T(8,128)(2,1)}), bf16[8,2,8,16,128]{4,3,2,1,0:T(8,128)(2,1)S(1)}, u32[]{:S(2)}, u32[]{:S(2)}) async-start(bf16[8,2,8,16,128]{4,3,2,1,0:T(8,128)(2,1)} %shard_map.112), calls=%async_computation.1 | async-start | bytes 1048576 | tf_op jit(solution)/shard_map/all_to_all | solution.py:476
  47.6 34.3 %copy-start.1 = (bf16[128,1024]{1,0:T(8,128)(2,1)S(1)}, bf16[128,1024]{1,0:T(8,128)(2,1)}, u32[]{:S(2)}) copy-start(bf16[128,1024]{1,0:T(8,128)(2,1)} %constant.61.clone.outer_ref) | copy-start | bytes 786436
  47.6 34.3 %copy-start.2 = (bf16[128,128]{1,0:T(8,128)(2,1)S(1)}, bf16[128,128]{1,0:T(8,128)(2,1)}, u32[]{:S(2)}) copy-start(bf16[128,128]{1,0:T(8,128)(2,1)} %constant.60.clone.inner_ref) | copy-start | bytes 98308
  47.6 7.4 %collective-permute-start.7 = (bf16[8,32,256]{2,1,0:T(8,128)(2,1)S(1)}, bf16[8,32,256]{2,1,0:T(8,128)(2,1)S(1)}, u32[]{:S(2)}, u32[]{:S(2)}) collective-permute-start(bf16[8,32,256]{2,1,0:T(8,128)(2,1)S(1)} %get-tuple-element.40), channel_id=1, source_target_pairs={{0,1},{1,0},{2,3},{3,2},{4,5},{5,4},{6,7},{7,6},{8,9},{9,8},{10,11... | collective-permute-start | bytes 393224 | tf_op jit(solution)/shard_map/ppermute | solution.py:71
  50.3 12.6 %collective-permute-start.8 = (bf16[8,32,256]{2,1,0:T(8,128)(2,1)S(1)}, bf16[8,32,256]{2,1,0:T(8,128)(2,1)S(1)}, u32[]{:S(2)}, u32[]{:S(2)}) collective-permute-start(bf16[8,32,256]{2,1,0:T(8,128)(2,1)S(1)} %get-tuple-element.41), channel_id=1, source_target_pairs={{0,2},{1,3},{2,0},{3,1},{4,6},{5,7},{6,4},{7,5},{8,10},{9,11},{10,... | collective-permute-start | bytes 393224 | tf_op jit(solution)/shard_map/ppermute | solution.py:71
  51.0 11.9 %collective-permute-start.9 = (bf16[8,32,256]{2,1,0:T(8,128)(2,1)S(1)}, bf16[8,32,256]{2,1,0:T(8,128)(2,1)S(1)}, u32[]{:S(2)}, u32[]{:S(2)}) collective-permute-start(bf16[8,32,256]{2,1,0:T(8,128)(2,1)S(1)} %get-tuple-element.42), channel_id=1, source_target_pairs={{0,3},{1,2},{2,1},{3,0},{4,7},{5,6},{6,5},{7,4},{8,11},{9,10},{10,... | collective-permute-start | bytes 393224 | tf_op jit(solution)/shard_map/ppermute | solution.py:71
  65.1 3.6 %collective-permute-start.10 = (bf16[4,8,8,128]{3,2,1,0:T(8,128)(2,1)S(1)}, bf16[4,8,8,128]{3,2,1,0:T(8,128)(2,1)S(1)}, u32[]{:S(2)}, u32[]{:S(2)}) collective-permute-start(bf16[4,8,8,128]{3,2,1,0:T(8,128)(2,1)S(1)} %get-tuple-element.44), channel_id=1, source_target_pairs={{0,4},{4,0},{8,12},{12,8},{16,20},{20,16},{24,28},{28,24},{1,5},{5... | collective-permute-start | bytes 196616 | tf_op jit(solution)/shard_map/ppermute | solution.py:71
  65.2 6.1 %collective-permute-start.11 = (bf16[4,8,8,128]{3,2,1,0:T(8,128)(2,1)S(1)}, bf16[4,8,8,128]{3,2,1,0:T(8,128)(2,1)S(1)}, u32[]{:S(2)}, u32[]{:S(2)}) collective-permute-start(bf16[4,8,8,128]{3,2,1,0:T(8,128)(2,1)S(1)} %get-tuple-element.45), channel_id=1, source_target_pairs={{0,8},{4,12},{8,0},{12,4},{16,24},{20,28},{24,16},{28,20},{1,9},{5... | collective-permute-start | bytes 196616 | tf_op jit(solution)/shard_map/ppermute | solution.py:71
  66.9 4.6 %collective-permute-start.12 = (bf16[4,8,8,128]{3,2,1,0:T(8,128)(2,1)S(1)}, bf16[4,8,8,128]{3,2,1,0:T(8,128)(2,1)S(1)}, u32[]{:S(2)}, u32[]{:S(2)}) collective-permute-start(bf16[4,8,8,128]{3,2,1,0:T(8,128)(2,1)S(1)} %get-tuple-element.46), channel_id=1, source_target_pairs={{0,12},{4,8},{8,4},{12,0},{16,28},{20,24},{24,20},{28,16},{1,13},{... | collective-permute-start | bytes 196616 | tf_op jit(solution)/shard_map/ppermute | solution.py:71
  67.0 4.4 %collective-permute-start.13 = (bf16[4,8,8,128]{3,2,1,0:T(8,128)(2,1)S(1)}, bf16[4,8,8,128]{3,2,1,0:T(8,128)(2,1)S(1)}, u32[]{:S(2)}, u32[]{:S(2)}) collective-permute-start(bf16[4,8,8,128]{3,2,1,0:T(8,128)(2,1)S(1)} %get-tuple-element.47), channel_id=1, source_target_pairs={{0,16},{4,20},{8,24},{12,28},{16,0},{20,4},{24,8},{28,12},{1,17},{... | collective-permute-start | bytes 196616 | tf_op jit(solution)/shard_map/ppermute | solution.py:71
  68.7 4.1 %collective-permute-start.14 = (bf16[4,8,8,128]{3,2,1,0:T(8,128)(2,1)S(1)}, bf16[4,8,8,128]{3,2,1,0:T(8,128)(2,1)S(1)}, u32[]{:S(2)}, u32[]{:S(2)}) collective-permute-start(bf16[4,8,8,128]{3,2,1,0:T(8,128)(2,1)S(1)} %get-tuple-element.48), channel_id=1, source_target_pairs={{0,20},{4,16},{8,28},{12,24},{16,4},{20,0},{24,12},{28,8},{1,21},{... | collective-permute-start | bytes 196616 | tf_op jit(solution)/shard_map/ppermute | solution.py:71
  68.7 6.8 %collective-permute-start.15 = (bf16[4,8,8,128]{3,2,1,0:T(8,128)(2,1)S(1)}, bf16[4,8,8,128]{3,2,1,0:T(8,128)(2,1)S(1)}, u32[]{:S(2)}, u32[]{:S(2)}) collective-permute-start(bf16[4,8,8,128]{3,2,1,0:T(8,128)(2,1)S(1)} %get-tuple-element.49), channel_id=1, source_target_pairs={{0,24},{4,28},{8,16},{12,20},{16,8},{20,12},{24,0},{28,4},{1,25},{... | collective-permute-start | bytes 196616 | tf_op jit(solution)/shard_map/ppermute | solution.py:71
  71.3 5.3 %collective-permute-start.16 = (bf16[4,8,8,128]{3,2,1,0:T(8,128)(2,1)S(1)}, bf16[4,8,8,128]{3,2,1,0:T(8,128)(2,1)S(1)}, u32[]{:S(2)}, u32[]{:S(2)}) collective-permute-start(bf16[4,8,8,128]{3,2,1,0:T(8,128)(2,1)S(1)} %get-tuple-element.50), channel_id=1, source_target_pairs={{0,28},{4,24},{8,20},{12,16},{16,12},{20,8},{24,4},{28,0},{1,29},{... | collective-permute-start | bytes 196616 | tf_op jit(solution)/shard_map/ppermute | solution.py:71
  78.3 6.7 %collective-permute-start.17 = (bf16[1,8,16,128]{3,2,1,0:T(8,128)(2,1)S(1)}, bf16[1,8,16,128]{3,2,1,0:T(8,128)(2,1)S(1)}, u32[]{:S(2)}, u32[]{:S(2)}) collective-permute-start(bf16[1,8,16,128]{3,2,1,0:T(8,128)(2,1)S(1)} %get-tuple-element.52), channel_id=1, source_target_pairs={{0,4},{4,0},{8,12},{12,8},{16,20},{20,16},{24,28},{28,24},{1,5},{5... | collective-permute-start | bytes 98312 | tf_op jit(solution)/shard_map/ppermute | solution.py:71
  78.4 8.1 %collective-permute-start.18 = (bf16[1,8,16,128]{3,2,1,0:T(8,128)(2,1)S(1)}, bf16[1,8,16,128]{3,2,1,0:T(8,128)(2,1)S(1)}, u32[]{:S(2)}, u32[]{:S(2)}) collective-permute-start(bf16[1,8,16,128]{3,2,1,0:T(8,128)(2,1)S(1)} %get-tuple-element.53), channel_id=1, source_target_pairs={{0,8},{4,12},{8,0},{12,4},{16,24},{20,28},{24,16},{28,20},{1,9},{5... | collective-permute-start | bytes 98312 | tf_op jit(solution)/shard_map/ppermute | solution.py:71
  79.0 8.7 %collective-permute-start.19 = (bf16[1,8,16,128]{3,2,1,0:T(8,128)(2,1)S(1)}, bf16[1,8,16,128]{3,2,1,0:T(8,128)(2,1)S(1)}, u32[]{:S(2)}, u32[]{:S(2)}) collective-permute-start(bf16[1,8,16,128]{3,2,1,0:T(8,128)(2,1)S(1)} %get-tuple-element.54), channel_id=1, source_target_pairs={{0,12},{4,8},{8,4},{12,0},{16,28},{20,24},{24,20},{28,16},{1,13},{... | collective-permute-start | bytes 98312 | tf_op jit(solution)/shard_map/ppermute | solution.py:71
  80.2 7.9 %collective-permute-start.20 = (bf16[1,8,16,128]{3,2,1,0:T(8,128)(2,1)S(1)}, bf16[1,8,16,128]{3,2,1,0:T(8,128)(2,1)S(1)}, u32[]{:S(2)}, u32[]{:S(2)}) collective-permute-start(bf16[1,8,16,128]{3,2,1,0:T(8,128)(2,1)S(1)} %get-tuple-element.55), channel_id=1, source_target_pairs={{0,16},{4,20},{8,24},{12,28},{16,0},{20,4},{24,8},{28,12},{1,17},{... | collective-permute-start | bytes 98312 | tf_op jit(solution)/shard_map/ppermute | solution.py:71
  81.1 7.5 %collective-permute-start.21 = (bf16[1,8,16,128]{3,2,1,0:T(8,128)(2,1)S(1)}, bf16[1,8,16,128]{3,2,1,0:T(8,128)(2,1)S(1)}, u32[]{:S(2)}, u32[]{:S(2)}) collective-permute-start(bf16[1,8,16,128]{3,2,1,0:T(8,128)(2,1)S(1)} %get-tuple-element.56), channel_id=1, source_target_pairs={{0,20},{4,16},{8,28},{12,24},{16,4},{20,0},{24,12},{28,8},{1,21},{... | collective-permute-start | bytes 98312 | tf_op jit(solution)/shard_map/ppermute | solution.py:71
  84.9 4.9 %collective-permute-start.22 = (bf16[1,8,16,128]{3,2,1,0:T(8,128)(2,1)S(1)}, bf16[1,8,16,128]{3,2,1,0:T(8,128)(2,1)S(1)}, u32[]{:S(2)}, u32[]{:S(2)}) collective-permute-start(bf16[1,8,16,128]{3,2,1,0:T(8,128)(2,1)S(1)} %get-tuple-element.57), channel_id=1, source_target_pairs={{0,24},{4,28},{8,16},{12,20},{16,8},{20,12},{24,0},{28,4},{1,25},{... | collective-permute-start | bytes 98312 | tf_op jit(solution)/shard_map/ppermute | solution.py:71
  86.5 4.8 %collective-permute-start.23 = (bf16[1,8,16,128]{3,2,1,0:T(8,128)(2,1)S(1)}, bf16[1,8,16,128]{3,2,1,0:T(8,128)(2,1)S(1)}, u32[]{:S(2)}, u32[]{:S(2)}) collective-permute-start(bf16[1,8,16,128]{3,2,1,0:T(8,128)(2,1)S(1)} %get-tuple-element.58), channel_id=1, source_target_pairs={{0,28},{4,24},{8,20},{12,16},{16,12},{20,8},{24,4},{28,0},{1,29},{... | collective-permute-start | bytes 98312 | tf_op jit(solution)/shard_map/ppermute | solution.py:71
  87.7 3.9 %collective-permute-start = (bf16[1,8,16,128]{3,2,1,0:T(8,128)(2,1)S(1)}, bf16[1,8,16,128]{3,2,1,0:T(8,128)(2,1)S(1)}, u32[]{:S(2)}, u32[]{:S(2)}) collective-permute-start(bf16[1,8,16,128]{3,2,1,0:T(8,128)(2,1)S(1)} %get-tuple-element.33), channel_id=1, source_target_pairs={{0,4},{4,0},{8,12},{12,8},{16,20},{20,16},{24,28},{28,24},{1,5},{5... | collective-permute-start | bytes 98312 | tf_op jit(solution)/shard_map/ppermute | solution.py:71
  88.1 5.4 %collective-permute-start.1 = (bf16[1,8,16,128]{3,2,1,0:T(8,128)(2,1)S(1)}, bf16[1,8,16,128]{3,2,1,0:T(8,128)(2,1)S(1)}, u32[]{:S(2)}, u32[]{:S(2)}) collective-permute-start(bf16[1,8,16,128]{3,2,1,0:T(8,128)(2,1)S(1)} %get-tuple-element.34), channel_id=1, source_target_pairs={{0,8},{4,12},{8,0},{12,4},{16,24},{20,28},{24,16},{28,20},{1,9},{5... | collective-permute-start | bytes 98312 | tf_op jit(solution)/shard_map/ppermute | solution.py:71
  88.6 9.4 %collective-permute-start.2 = (bf16[1,8,16,128]{3,2,1,0:T(8,128)(2,1)S(1)}, bf16[1,8,16,128]{3,2,1,0:T(8,128)(2,1)S(1)}, u32[]{:S(2)}, u32[]{:S(2)}) collective-permute-start(bf16[1,8,16,128]{3,2,1,0:T(8,128)(2,1)S(1)} %get-tuple-element.35), channel_id=1, source_target_pairs={{0,12},{4,8},{8,4},{12,0},{16,28},{20,24},{24,20},{28,16},{1,13},{... | collective-permute-start | bytes 98312 | tf_op jit(solution)/shard_map/ppermute | solution.py:71
  89.8 8.2 %collective-permute-start.3 = (bf16[1,8,16,128]{3,2,1,0:T(8,128)(2,1)S(1)}, bf16[1,8,16,128]{3,2,1,0:T(8,128)(2,1)S(1)}, u32[]{:S(2)}, u32[]{:S(2)}) collective-permute-start(bf16[1,8,16,128]{3,2,1,0:T(8,128)(2,1)S(1)} %get-tuple-element.36), channel_id=1, source_target_pairs={{0,16},{4,20},{8,24},{12,28},{16,0},{20,4},{24,8},{28,12},{1,17},{... | collective-permute-start | bytes 98312 | tf_op jit(solution)/shard_map/ppermute | solution.py:71
  91.2 6.8 %collective-permute-start.4 = (bf16[1,8,16,128]{3,2,1,0:T(8,128)(2,1)S(1)}, bf16[1,8,16,128]{3,2,1,0:T(8,128)(2,1)S(1)}, u32[]{:S(2)}, u32[]{:S(2)}) collective-permute-start(bf16[1,8,16,128]{3,2,1,0:T(8,128)(2,1)S(1)} %get-tuple-element.37), channel_id=1, source_target_pairs={{0,20},{4,16},{8,28},{12,24},{16,4},{20,0},{24,12},{28,8},{1,21},{... | collective-permute-start | bytes 98312 | tf_op jit(solution)/shard_map/ppermute | solution.py:71
  91.6 6.5 %collective-permute-start.5 = (bf16[1,8,16,128]{3,2,1,0:T(8,128)(2,1)S(1)}, bf16[1,8,16,128]{3,2,1,0:T(8,128)(2,1)S(1)}, u32[]{:S(2)}, u32[]{:S(2)}) collective-permute-start(bf16[1,8,16,128]{3,2,1,0:T(8,128)(2,1)S(1)} %get-tuple-element.38), channel_id=1, source_target_pairs={{0,24},{4,28},{8,16},{12,20},{16,8},{20,12},{24,0},{28,4},{1,25},{... | collective-permute-start | bytes 98312 | tf_op jit(solution)/shard_map/ppermute | solution.py:71
  93.5 4.6 %collective-permute-start.6 = (bf16[1,8,16,128]{3,2,1,0:T(8,128)(2,1)S(1)}, bf16[1,8,16,128]{3,2,1,0:T(8,128)(2,1)S(1)}, u32[]{:S(2)}, u32[]{:S(2)}) collective-permute-start(bf16[1,8,16,128]{3,2,1,0:T(8,128)(2,1)S(1)} %get-tuple-element.39), channel_id=1, source_target_pairs={{0,28},{4,24},{8,20},{12,16},{16,12},{20,8},{24,4},{28,0},{1,29},{... | collective-permute-start | bytes 98312 | tf_op jit(solution)/shard_map/ppermute | solution.py:71

commit v2 on v1

--- a/solution.py
+++ b/solution.py
@@ -91,61 +91,46 @@
     return jnp.asarray(matrix.reshape(p.rg * LANES, 2 * LANES), jnp.bfloat16)
 
 
-def split_slabs(plan, velocity, quantity, place):
-    p = plan
-
-    def body(place_ref, velocity_ref, *rest):
-        outs, sems = rest[:-1], rest[-1]
-        copies = []
-        for n, out in enumerate(outs):
-            slab = place_ref[0] ^ (n + 1)
-            columns = pl.ds(pl.multiple_of(slab * p.cs, LANES), p.cs)
-            copies.append(pltpu.make_async_copy(velocity_ref.at[quantity, :, :, columns], out, sems.at[n]))
-            copies[-1].start()
-        for copy in copies:
-            copy.wait()
-
-    outs = [pltpu.VMEM((p.tl, p.xb, p.cs), velocity.dtype) for _ in range(1, p.ta)]
-    scratch = [pltpu.SemaphoreType.DMA((p.ta - 1,))]
-    return on_chip(body, [velocity], outs, scratch, (place,), in_hbm=1)
+def spread_rows(plan, wide, tile, rows):
+    p = plan
+    rows = rows.astype(jnp.float32)
+    for g in range(p.groups):
+        wide[tile, g] = rows[:, g * p.rg : (g + 1) * p.rg].reshape(p.tl * p.rg, LANES)
 
 
 def rows_by_snapshot(plan, wide, tiles):
     p = plan
     lhs = []
     for g in range(p.groups):
-        rows = [
-            wide[tile, pl.ds(g * p.rg + r, p.tl, stride=p.xb), :] for tile in tiles for r in range(p.rg)
-        ]
+        rows = [wide[tile, g, pl.ds(r, p.tl, stride=p.rg), :] for tile in tiles for r in range(p.rg)]
         lhs.append(jnp.concatenate(rows, axis=0).astype(jnp.bfloat16))
     return jnp.concatenate(lhs, axis=1)
 
 
-def pack_slab(plan, velocity, quantity, arrived, place):
+def pack_one(plan, velocity, quantity, place):
     p = plan
     shape = (p.ta, p.rg, p.tl, LANES)
-    if not p.fast:
-        own = lax.dynamic_slice_in_dim(velocity[quantity], place[0] * p.cs, p.cs, axis=2)
-        x = jnp.stack([own] + list(arrived)).reshape(p.ta, p.tl, p.groups, p.rg, p.blocks, p.cc)
-        x = x.transpose(4, 0, 3, 1, 2, 5).reshape((p.blocks,) + shape)
+    if not p.by_partner or not p.fast:
+        x = velocity[quantity].reshape(p.tl, p.groups, p.rg, p.ta, p.blocks, p.cc)
+        x = x.transpose(4, 3, 2, 0, 1, 5).reshape((p.blocks,) + shape)
+        x = jnp.take(x, jnp.arange(p.ta, dtype=jnp.int32) ^ place[0], axis=1)
         return [jnp.take(x, place[1] ^ n, axis=0) for n in range(p.blocks)] if p.by_partner else [x]
-    assert p.by_partner
     per_slab = p.cs // LANES
 
-    def body(place_ref, swap, *rest):
-        others, velocity_ref = rest[: p.ta - 1], rest[p.ta - 1]
-        outs = rest[p.ta : p.ta + p.blocks]
-        own, sem, wide, chunks = rest[p.ta + p.blocks :]
-        columns = pl.ds(pl.multiple_of(place_ref[0] * p.cs, LANES), p.cs)
-        copy = pltpu.make_async_copy(velocity_ref.at[quantity, :, :, columns], own, sem.at[0])
-        copy.start()
-        for m in list(range(1, p.ta)) + [0]:
-            if m == 0:
-                copy.wait()
-            x = own if m == 0 else others[m - 1]
+    def body(place_ref, swap, velocity_ref, *rest):
+        outs = rest[: p.blocks]
+        x, sems, wide, chunks = rest[p.blocks :]
+        copies = []
+        for m in range(p.ta):
+            columns = pl.ds(pl.multiple_of((place_ref[0] ^ m) * p.cs, LANES), p.cs)
+            copies.append(
+                pltpu.make_async_copy(velocity_ref.at[quantity, :, :, columns], x.at[m], sems.at[m])
+            )
+            copies[-1].start()
+        for m in range(p.ta):
+            copies[m].wait()
             for i in range(per_slab):
-                rows = x[:, :, i * LANES : (i + 1) * LANES].astype(jnp.float32)
-                wide[m * per_slab + i] = rows.reshape(p.tl * p.xb, LANES)
+                spread_rows(p, wide, m * per_slab + i, x[m, :, :, i * LANES : (i + 1) * LANES])
         tiles = range(p.ta * per_slab)
         swapped = jnp.dot(
             rows_by_snapshot(p, wide, tiles), swap[...], preferred_element_type=jnp.float32
@@ -161,12 +146,26 @@
 
     outs = [pltpu.VMEM(shape, velocity.dtype) for _ in range(p.blocks)]
     scratch = [
-        pltpu.VMEM((p.tl, p.xb, p.cs), velocity.dtype),
-        pltpu.SemaphoreType.DMA((1,)),
-        pltpu.VMEM((p.zb // LANES, p.tl * p.xb, LANES), jnp.float32),
+        pltpu.VMEM((p.ta, p.tl, p.xb, p.cs), velocity.dtype),
+        pltpu.SemaphoreType.DMA((p.ta,)),
+        pltpu.VMEM((p.zb // LANES, p.groups, p.tl * p.rg, LANES), jnp.float32),
         pltpu.VMEM((p.blocks,) + shape, velocity.dtype),
     ]
-    return on_chip(body, [group_swap(p), *arrived, velocity], outs, scratch, (place,), in_hbm=1)
+    return on_chip(body, [group_swap(p), velocity], outs, scratch, (place,), in_hbm=1)
+
+
+def regroup(plan, arrays):
+    p = plan
+    if len(arrays) == 1:
+        return [arrays[0][:, m] for m in range(p.ta)]
+
+    def body(*refs):
+        for n in range(p.blocks):
+            for m in range(p.ta):
+                refs[p.blocks + m][n] = refs[n][m]
+
+    outs = [pltpu.VMEM((p.blocks, p.rg, p.tl, LANES), arrays[0].dtype) for _ in range(p.ta)]
+    return on_chip(body, list(arrays), outs, [])
 
 
 def pack_all(plan, velocity):
@@ -208,8 +207,7 @@
                 copies[n, start].wait()
                 tiles = range(start * per_slab, (start + half) * per_slab)
                 for tile in tiles:
-                    rows = x[n, :, :, tile * LANES : (tile + 1) * LANES].astype(jnp.float32)
-                    wide[tile] = rows.reshape(p.tl * p.xb, LANES)
+                    spread_rows(p, wide, tile, x[n, :, :, tile * LANES : (tile + 1) * LANES])
                 swapped = jnp.dot(
                     rows_by_snapshot(p, wide, tiles), swap[...], preferred_element_type=jnp.float32
                 )
@@ -245,7 +243,7 @@
         pltpu.VMEM((2, p.tl, p.xb, p.zb), velocity.dtype),
         pltpu.SemaphoreType.DMA((2, p.ta)),
         pltpu.SemaphoreType.DMA((2,)),
-        pltpu.VMEM((p.zb // LANES, p.tl * p.xb, LANES), jnp.float32),
+        pltpu.VMEM((p.zb // LANES, p.groups, p.tl * p.rg, LANES), jnp.float32),
         pltpu.VMEM(swap.shape, swap.dtype),
         pltpu.VMEM(picks.shape, picks.dtype),
         pltpu.VMEM((p.chunks, p.rg * p.tl, LANES), jnp.float32),
@@ -330,18 +328,24 @@
     return on_chip(body, [both, inner, outer], outs, scratch, (place,))
 
 
-def cross(plan, series, starts, table, owner, place, by_partner):
+def cross(plan, jobs, owner, place, by_partner):
     p = plan
     scaling = 8.0 / (3.0 * SEG * NSEG)
     pair = 2 if p.rg % 2 == 0 else 1
     width = pair * LANES
-    split = len(series) > 1
+    inputs, where = [], []
+    for series, start, table in jobs:
+        if not any(x is series[0] for x in inputs):
+            inputs.extend(series)
+        if not any(x is table for x in inputs):
+            inputs.append(table)
+        first = next(i for i, x in enumerate(inputs) if x is series[0])
+        where.append((first, len(series), start, next(i for i, x in enumerate(inputs) if x is table)))
 
     def body(owner_ref, place_ref, *refs):
-        xs, table_ref = refs[: len(series)], refs[len(series)]
-        outs, (spec, ref_spec) = refs[len(series) + 1 : -2], refs[-2:]
+        outs, (spec, ref_spec) = refs[len(inputs) : -2], refs[-2:]
         turn = 0
-        for q, start in enumerate(starts):
+        for q, (first, count, start, table) in enumerate(where):
             for r in range(0, p.rg, pair):
                 slot = turn % 2
                 turn += 1
@@ -349,14 +353,14 @@
                     rows = []
                     for i in range(pair):
                         at = start + r + i
-                        if split:
-                            x = [xs[n][m, at].astype(jnp.float32) for m in range(p.ta)]
+                        if count > 1:
+                            x = [refs[first + m][n, at].astype(jnp.float32) for m in range(count)]
                             rows.append(jnp.concatenate(x, axis=0))
                         else:
-                            rows.append(series_of(xs[0], n, at))
-                    b = place_ref[1] ^ n if split else n
+                            rows.append(series_of(refs[first], n, at))
+                    b = place_ref[1] ^ n if count > 1 and p.by_partner else n
                     spec[slot, b] = jnp.dot(
-                        table_ref[...],
+                        refs[table][...],
                         jnp.concatenate(rows, axis=1).astype(jnp.bfloat16),
                         preferred_element_type=jnp.float32,
                     )
@@ -381,7 +385,7 @@
                         else:
                             outs[0][n, q, r + i] = mine
 
-    shape = (len(starts), p.rg, ROWS, LANES)
+    shape = (len(jobs), p.rg, ROWS, LANES)
     if by_partner:
         outs = [pltpu.VMEM(shape, jnp.bfloat16) for _ in range(p.blocks)]
     else:
@@ -390,7 +394,7 @@
         pltpu.VMEM((2, p.blocks, NSEG * ROWS, width), jnp.float32),
         pltpu.VMEM((2, NSEG * ROWS, width), jnp.float32),
     ]
-    return on_chip(body, [*series, table], outs, scratch, (owner, place))
+    return on_chip(body, inputs, outs, scratch, (owner, place))
 
 
 def assemble(plan, so_far, quantities, pieces, place):
@@ -464,8 +468,6 @@
     time = lax.axis_index("ta").astype(jnp.int32)
     place = jnp.stack([time, lax.axis_index(block_axes).astype(jnp.int32)])
 
-    slabs = split_slabs(plan, velocity, 1, place)
-    slabs = [trade(x, "ta", n + 1, plan.ta) for n, x in enumerate(slabs)]
     both = pack_all(plan, velocity)
     both = both.reshape((-1,) + both.shape[2:])
     both = lax.all_to_all(both, block_axes + ("ta",), split_axis=0, concat_axis=0, tiled=True)
@@ -476,23 +478,22 @@
             return [lax.all_to_all(arrays[0], block_axes, split_axis=0, concat_axis=0, tiled=True)]
         return [arrays[0]] + [trade(arrays[n], block_axes, n, plan.blocks) for n in range(1, plan.blocks)]
 
-    wall = pack_slab(plan, velocity, 1, slabs, place)
+    wall = pack_one(plan, velocity, 1, place)
     wall = over_blocks(wall)
+    wall = regroup(plan, wall)
+    wall = [wall[0]] + [trade(wall[m], "ta", m, plan.ta) for m in range(1, plan.ta)]
+
     times = jnp.arange(plan.tl, dtype=jnp.int32)[None, :]
     turn = jnp.arange(plan.ta, dtype=jnp.int32)[:, None]
     table_wall = dft_rows(offsets, ((turn ^ time) * plan.tl + times).reshape(-1))
     table = dft_rows(offsets, (turn * plan.tl + times).reshape(-1))
-    wall = cross(plan, wall, (0,), table_wall, owner, place, plan.by_partner)
-    wall = over_blocks(wall)
-    out = assemble(plan, None, (1,), wall, place)
-
-    pieces = cross(plan, [both], (0, plan.rg), table, owner, place, False)
-    pieces = over_blocks(pieces)
+    early = cross(plan, [([both], 0, table), ([both], plan.rg, table)], owner, place, False)
+    early = over_blocks(early)
     spin = vorticity(plan, both, place)
-    spin = cross(plan, [spin], (0,), table, owner, place, plan.by_partner)
-    spin = over_blocks(spin)
-    out = assemble(plan, out, (2, 0), pieces, place)
-    return assemble(plan, out, (3,), spin, place)
+    late = cross(plan, [([spin], 0, table), (wall, 0, table_wall)], owner, place, plan.by_partner)
+    late = over_blocks(late)
+    out = assemble(plan, None, (2, 0), early, place)
+    return assemble(plan, out, (3, 1), late, place)
 
 
 def solution(mesh):

time: 100 us -> 90.8 us (0.908)
  starting transfers between devices: 35.4 us -> 29.3 us
  Pallas kernels: 22.2 us -> 17.8 us
  waiting for transfers between devices: 40.8 us -> 42.1 us
    ppermute x24 -> x17, starting transfers between devices: 24.1 us -> 17.9 us  [trade(): return lax.ppermute(x, axis, [(i, i ^ step) for i in range(count)])]
    pallas_call x10 -> x8, Pallas kernels: 22.2 us -> 17.8 us  [on_chip(): pl.pallas_call(body, in_specs=[smem] * len(scalars) + [vmem] * count + [h...]
    ppermute x24 -> x17, waiting for transfers between devices: 15.6 us -> 16.9 us  [trade(): return lax.ppermute(x, axis, [(i, i ^ step) for i in range(count)])]
  transfers between devices with their start and end apart: 26 -> 19, of which waited for: 7 -> 10; matrix products, arithmetic and copies ran while one was open for 1% -> 1% of each run, Pallas kernels for 12% -> 9%
where the time goes in v2:
time: 90.8 us; the launch traced here: 90.4 us
  waiting for transfers between devices  42.1 us (46%)
  starting transfers between devices  29.3 us (32%)
  Pallas kernels  17.8 us (20%)
    all_to_all x1, waiting for transfers between devices, shards(): lax.all_to_all(both, block_axes + ('ta',), split_axis=0, concat_axis=0, t...  25.2 us
    ppermute x17, starting transfers between devices, trade(): return lax.ppermute(x, axis, [(i, i ^ step) for i in range(count)])  17.9 us
    pallas_call x8, Pallas kernels, on_chip(): pl.pallas_call(body, in_specs=[smem] * len(scalars) + [vmem] * count + [h...  17.8 us
    ppermute x17, waiting for transfers between devices, trade(): return lax.ppermute(x, axis, [(i, i ^ step) for i in range(count)])  16.9 us
    all_to_all x1, starting transfers between devices, shards(): lax.all_to_all(both, block_axes + ('ta',), split_axis=0, concat_axis=0, t...  7.33 us
    all_to_all x1, starting transfers between devices, over_blocks(): lax.all_to_all(arrays[0], block_axes, split_axis=0, concat_axis=0, tiled=...  4.05 us
  transfers between devices with their start and end apart: 19, of which 10 were waited for; matrix products, arithmetic and copies ran while one was open for 1% of the time, Pallas kernels for 9%

profile of v2, /device:TPU:0, one launch (start us, length us, event | category | flops | bytes accessed | tf_op | source)
XLA Modules:
  0.0 90.4 jit_solution(6102525873117904633)
XLA Ops:
  0.0 4.4 %shard_map.100 = bf16[8,4,17,8,128]{4,3,2,1,0:T(8,128)(2,1)} custom-call(bf16[512,512]{1,0:T(8,128)(2,1)} %constant.58.clone.swap_hbm.swap.refs_1_.refs_8_, bf16[1024,256]{1,0:T(8,128)(2,1)} %constant.59.clone.picks_hbm, bf16[3,8,32,1024]{3,2,1,0:T(8,128)(2,1)} %velocity_ref.3), custom_call_target="tpu_custom_call" | custom-call | tf_op jit(solution)/shard_map/pallas_call | solution.py:46
  4.5 7.3 %all-to-all-start = ((bf16[32,17,8,128]{3,2,1,0:T(8,128)(2,1)}), bf16[32,17,8,128]{3,2,1,0:T(8,128)(2,1)S(1)}, u32[]{:S(2)}, u32[]{:S(2)}) async-start(bf16[32,17,8,128]{3,2,1,0:T(8,128)(2,1)} %bitcast.2), calls=%async_computation | async-start | bytes 2228224 | tf_op jit(solution)/shard_map/all_to_all | solution.py:473
  12.9 25.2 %all-to-all-done = bf16[32,17,8,128]{3,2,1,0:T(8,128)(2,1)S(1)} async-done(((bf16[32,17,8,128]{3,2,1,0:T(8,128)(2,1)}), bf16[32,17,8,128]{3,2,1,0:T(8,128)(2,1)S(1)}, u32[]{:S(2)}, u32[]{:S(2)}) %all-to-all-start) | async-done | bytes 1114144 | tf_op jit(solution)/shard_map/all_to_all | solution.py:473
  38.1 3.1 %shard_map.105 = bf16[8,2,8,16,128]{4,3,2,1,0:T(8,128)(2,1)} custom-call(s32[7]{0:T(128)S(1)} %copy-done.3, s32[2]{0:T(128)S(1)} %pad_add_fusion.place_ref, bf16[8,4,17,8,128]{4,3,2,1,0:T(8,128)(2,1)S(1)} %bitcast.6, bf16[112,32]{1,0:T(8,128)(2,1)S(1)} %bitcast.8), custom_call_target="tpu_custom_call" | custom-call | tf_op jit(solution)/shard_map/pallas_call | solution.py:46
  41.2 4.1 %all-to-all-start.1 = ((bf16[8,2,8,16,128]{4,3,2,1,0:T(8,128)(2,1)}), bf16[8,2,8,16,128]{4,3,2,1,0:T(8,128)(2,1)S(1)}, u32[]{:S(2)}, u32[]{:S(2)}) async-start(bf16[8,2,8,16,128]{4,3,2,1,0:T(8,128)(2,1)} %shard_map.105), calls=%async_computation.1 | async-start | bytes 1048576 | tf_op jit(solution)/shard_map/all_to_all | solution.py:478
  45.2 2.2 %shard_map.102 = (bf16[4,8,8,128]{3,2,1,0:T(8,128)(2,1)S(1)}, bf16[4,8,8,128]{3,2,1,0:T(8,128)(2,1)S(1)}, bf16[4,8,8,128]{3,2,1,0:T(8,128)(2,1)S(1)}, bf16[4,8,8...) custom-call(s32[2]{0:T(128)S(1)} %pad_add_fusion.place_ref, ...), custom_call_target="tpu_custom_call" | custom-call | tf_op jit(solution)/shard_map/pallas_call | solution.py:46
  47.4 1.2 %collective-permute-start = (bf16[4,8,8,128]{3,2,1,0:T(8,128)(2,1)S(1)}, bf16[4,8,8,128]{3,2,1,0:T(8,128)(2,1)S(1)}, u32[]{:S(2)}, u32[]{:S(2)}) collective-permute-start(bf16[4,8,8,128]{3,2,1,0:T(8,128)(2,1)S(1)} %get-tuple-element.26), channel_id=1, source_target_pairs={{0,4},{4,0},{8,12},{12,8},{16,20},{20,16},{24,28},{28,24},{1,5},{5... | collective-permute-start | bytes 196616 | tf_op jit(solution)/shard_map/ppermute | solution.py:71
  48.6 1.4 %collective-permute-start.1 = (bf16[4,8,8,128]{3,2,1,0:T(8,128)(2,1)S(1)}, bf16[4,8,8,128]{3,2,1,0:T(8,128)(2,1)S(1)}, u32[]{:S(2)}, u32[]{:S(2)}) collective-permute-start(bf16[4,8,8,128]{3,2,1,0:T(8,128)(2,1)S(1)} %get-tuple-element.27), channel_id=1, source_target_pairs={{0,8},{4,12},{8,0},{12,4},{16,24},{20,28},{24,16},{28,20},{1,9},{5... | collective-permute-start | bytes 196616 | tf_op jit(solution)/shard_map/ppermute | solution.py:71
  50.0 1.5 %collective-permute-start.3 = (bf16[4,8,8,128]{3,2,1,0:T(8,128)(2,1)S(1)}, bf16[4,8,8,128]{3,2,1,0:T(8,128)(2,1)S(1)}, u32[]{:S(2)}, u32[]{:S(2)}) collective-permute-start(bf16[4,8,8,128]{3,2,1,0:T(8,128)(2,1)S(1)} %get-tuple-element.29), channel_id=1, source_target_pairs={{0,16},{4,20},{8,24},{12,28},{16,0},{20,4},{24,8},{28,12},{1,17},{... | collective-permute-start | bytes 196616 | tf_op jit(solution)/shard_map/ppermute | solution.py:71
  51.5 0.6 collective-permute-start.4
  52.1 1.9 %collective-permute-start.5 = (bf16[4,8,8,128]{3,2,1,0:T(8,128)(2,1)S(1)}, bf16[4,8,8,128]{3,2,1,0:T(8,128)(2,1)S(1)}, u32[]{:S(2)}, u32[]{:S(2)}) collective-permute-start(bf16[4,8,8,128]{3,2,1,0:T(8,128)(2,1)S(1)} %get-tuple-element.31), channel_id=1, source_target_pairs={{0,24},{4,28},{8,16},{12,20},{16,8},{20,12},{24,0},{28,4},{1,25},{... | collective-permute-start | bytes 196616 | tf_op jit(solution)/shard_map/ppermute | solution.py:71
  54.0 2.0 %collective-permute-done.1.refs_2_ = bf16[4,8,8,128]{3,2,1,0:T(8,128)(2,1)S(1)} collective-permute-done((bf16[4,8,8,128]{3,2,1,0:T(8,128)(2,1)S(1)}, bf16[4,8,8,128]{3,2,1,0:T(8,128)(2,1)S(1)}, u32[]{:S(2)}, u32[]{:S(2)}) %collective-permute-start.1) | collective-permute-done | bytes 65568 | tf_op jit(solution)/shard_map/ppermute | solution.py:71
  56.0 0.5 collective-permute-start.6
  56.5 0.4 collective-permute-done.2.refs_3_
  57.1 2.1 %collective-permute-done.5.refs_6_ = bf16[4,8,8,128]{3,2,1,0:T(8,128)(2,1)S(1)} collective-permute-done((bf16[4,8,8,128]{3,2,1,0:T(8,128)(2,1)S(1)}, bf16[4,8,8,128]{3,2,1,0:T(8,128)(2,1)S(1)}, u32[]{:S(2)}, u32[]{:S(2)}) %collective-permute-start.5) | collective-permute-done | bytes 65568 | tf_op jit(solution)/shard_map/ppermute | solution.py:71
  59.2 2.0 %collective-permute-done.6.refs_7_ = bf16[4,8,8,128]{3,2,1,0:T(8,128)(2,1)S(1)} collective-permute-done((bf16[4,8,8,128]{3,2,1,0:T(8,128)(2,1)S(1)}, bf16[4,8,8,128]{3,2,1,0:T(8,128)(2,1)S(1)}, u32[]{:S(2)}, u32[]{:S(2)}) %collective-permute-start.6) | collective-permute-done | bytes 65568 | tf_op jit(solution)/shard_map/ppermute | solution.py:71
  61.2 2.0 %collective-permute-start.7 = (bf16[8,8,8,128]{3,2,1,0:T(8,128)(2,1)S(1)}, bf16[8,8,8,128]{3,2,1,0:T(8,128)(2,1)S(1)}, u32[]{:S(2)}, u32[]{:S(2)}) collective-permute-start(bf16[8,8,8,128]{3,2,1,0:T(8,128)(2,1)S(1)} %get-tuple-element.34), channel_id=1, source_target_pairs={{0,1},{1,0},{2,3},{3,2},{4,5},{5,4},{6,7},{7,6},{8,9},{9,8},{10,11... | collective-permute-start | bytes 393224 | tf_op jit(solution)/shard_map/ppermute | solution.py:71
  63.2 0.7 collective-permute-start.8
  63.9 1.7 %collective-permute-start.9 = (bf16[8,8,8,128]{3,2,1,0:T(8,128)(2,1)S(1)}, bf16[8,8,8,128]{3,2,1,0:T(8,128)(2,1)S(1)}, u32[]{:S(2)}, u32[]{:S(2)}) collective-permute-start(bf16[8,8,8,128]{3,2,1,0:T(8,128)(2,1)S(1)} %get-tuple-element.36), channel_id=1, source_target_pairs={{0,3},{1,2},{2,1},{3,0},{4,7},{5,6},{6,5},{7,4},{8,11},{9,10},{10,... | collective-permute-start | bytes 393224 | tf_op jit(solution)/shard_map/ppermute | solution.py:71
  65.7 1.4 %shard_map.101.refs_0_ = bf16[8,4,8,8,128]{4,3,2,1,0:T(8,128)(2,1)S(1)} custom-call(s32[2]{0:T(128)S(1)} %pad_add_fusion.place_ref, bf16[8,4,17,8,128]{4,3,2,1,0:T(8,128)(2,1)S(1)} %bitcast.7, bf16[128,128]{1,0:T(8,128)(2,1)S(1)} %copy-done.2, bf16[128,1024]{1,0:T(8,128)(2,1)S(1)} %copy-done.1), custom_call_target="tpu_custom_call" | custom-call | tf_op jit(solution)/shard_map/pallas_call | solution.py:46
  67.4 7.8 %collective-permute-done.8.refs_4_ = bf16[8,8,8,128]{3,2,1,0:T(8,128)(2,1)S(1)} collective-permute-done((bf16[8,8,8,128]{3,2,1,0:T(8,128)(2,1)S(1)}, bf16[8,8,8,128]{3,2,1,0:T(8,128)(2,1)S(1)}, u32[]{:S(2)}, u32[]{:S(2)}) %collective-permute-start.8) | collective-permute-done | bytes 131104 | tf_op jit(solution)/shard_map/ppermute | solution.py:71
  75.2 2.6 %shard_map.104 = (bf16[2,8,16,128]{3,2,1,0:T(8,128)(2,1)S(1)}, bf16[2,8,16,128]{3,2,1,0:T(8,128)(2,1)S(1)}, bf16[2,8,16,128]{3,2,1,0:T(8,128)(2,1)S(1)}, bf16[2,...) custom-call(s32[7]{0:T(128)S(1)} %copy-done.3, ...), custom_call_target="tpu_custom_call" | custom-call | tf_op jit(solution)/shard_map/pallas_call | solution.py:46
  77.9 0.8 collective-permute-start.11
  78.7 1.1 %collective-permute-start.12 = (bf16[2,8,16,128]{3,2,1,0:T(8,128)(2,1)S(1)}, bf16[2,8,16,128]{3,2,1,0:T(8,128)(2,1)S(1)}, u32[]{:S(2)}, u32[]{:S(2)}) collective-permute-start(bf16[2,8,16,128]{3,2,1,0:T(8,128)(2,1)S(1)} %get-tuple-element.40), channel_id=1, source_target_pairs={{0,12},{4,8},{8,4},{12,0},{16,28},{20,24},{24,20},{28,16},{1,13},{... | collective-permute-start | bytes 196616 | tf_op jit(solution)/shard_map/ppermute | solution.py:71
  79.8 1.1 %collective-permute-start.13 = (bf16[2,8,16,128]{3,2,1,0:T(8,128)(2,1)S(1)}, bf16[2,8,16,128]{3,2,1,0:T(8,128)(2,1)S(1)}, u32[]{:S(2)}, u32[]{:S(2)}) collective-permute-start(bf16[2,8,16,128]{3,2,1,0:T(8,128)(2,1)S(1)} %get-tuple-element.41), channel_id=1, source_target_pairs={{0,16},{4,20},{8,24},{12,28},{16,0},{20,4},{24,8},{28,12},{1,17},{... | collective-permute-start | bytes 196616 | tf_op jit(solution)/shard_map/ppermute | solution.py:71
  80.9 0.6 collective-permute-start.14
  81.5 1.6 %collective-permute-start.15 = (bf16[2,8,16,128]{3,2,1,0:T(8,128)(2,1)S(1)}, bf16[2,8,16,128]{3,2,1,0:T(8,128)(2,1)S(1)}, u32[]{:S(2)}, u32[]{:S(2)}) collective-permute-start(bf16[2,8,16,128]{3,2,1,0:T(8,128)(2,1)S(1)} %get-tuple-element.43), channel_id=1, source_target_pairs={{0,24},{4,28},{8,16},{12,20},{16,8},{20,12},{24,0},{28,4},{1,25},{... | collective-permute-start | bytes 196616 | tf_op jit(solution)/shard_map/ppermute | solution.py:71
  83.1 1.0 %collective-permute-start.16 = (bf16[2,8,16,128]{3,2,1,0:T(8,128)(2,1)S(1)}, bf16[2,8,16,128]{3,2,1,0:T(8,128)(2,1)S(1)}, u32[]{:S(2)}, u32[]{:S(2)}) collective-permute-start(bf16[2,8,16,128]{3,2,1,0:T(8,128)(2,1)S(1)} %get-tuple-element.44), channel_id=1, source_target_pairs={{0,28},{4,24},{8,20},{12,16},{16,12},{20,8},{24,4},{28,0},{1,29},{... | collective-permute-start | bytes 196616 | tf_op jit(solution)/shard_map/ppermute | solution.py:71
  84.2 2.1 %shard_map.106.refs_9_ = f32[4,2,7,32,256]{4,3,2,1,0:T(8,128)} custom-call(s32[2]{0:T(128)S(1)} %pad_add_fusion.place_ref, bf16[8,2,8,16,128]{4,3,2,1,0:T(8,128)(2,1)S(1)} %all-to-all-done.1.refs_0_, bf16[512,512]{1,0:T(8,128)(2,1)S(1)} %copy-done), custom_call_target="tpu_custom_call" | custom-call | tf_op jit(solution)/shard_map/pallas_call | solution.py:46
  86.3 1.1 %collective-permute-done.15.refs_6_ = bf16[2,8,16,128]{3,2,1,0:T(8,128)(2,1)S(1)} collective-permute-done((bf16[2,8,16,128]{3,2,1,0:T(8,128)(2,1)S(1)}, bf16[2,8,16,128]{3,2,1,0:T(8,128)(2,1)S(1)}, u32[]{:S(2)}, u32[]{:S(2)}) %collective-permute-start.15) | collective-permute-done | bytes 65568 | tf_op jit(solution)/shard_map/ppermute | solution.py:71
  87.4 1.0 %collective-permute-done.16.refs_7_ = bf16[2,8,16,128]{3,2,1,0:T(8,128)(2,1)S(1)} collective-permute-done((bf16[2,8,16,128]{3,2,1,0:T(8,128)(2,1)S(1)}, bf16[2,8,16,128]{3,2,1,0:T(8,128)(2,1)S(1)}, u32[]{:S(2)}, u32[]{:S(2)}) %collective-permute-start.16) | collective-permute-done | bytes 65568 | tf_op jit(solution)/shard_map/ppermute | solution.py:71
  88.4 2.0 %shard_map.107 = f32[4,2,7,32,256]{4,3,2,1,0:T(8,128)} custom-call(s32[2]{0:T(128)S(1)} %pad_add_fusion.place_ref, bf16[2,8,16,128]{3,2,1,0:T(8,128)(2,1)S(1)} %get-tuple-element.37.refs_0_, bf16[2,8,16,128]{3,2,1,0:T(8,128)(2,1)S(1)} %collective-permute-done.10.refs_1_, ...), custom_call_target="tpu_custom_call", output_to_operand_aliasing={{}: (10, {})} | custom-call | tf_op jit(solution)/shard_map/pallas_call | solution.py:46
  (38 shorter events, 1.7 us)
Async XLA Ops:
  4.4 7.8 %copy-start.4 = (s32[7]{0:T(128)S(1)}, s32[7]{0:T(128)}, u32[]{:S(2)}) copy-start(s32[7]{0:T(128)} %param.11) | copy-start | bytes 88
  4.5 33.6 %copy-start.3 = (s32[7]{0:T(128)S(1)}, s32[7]{0:T(128)}, u32[]{:S(2)}) copy-start(s32[7]{0:T(128)} %owner_ref.3) | copy-start | bytes 88
  4.5 33.6 %all-to-all-start = ((bf16[32,17,8,128]{3,2,1,0:T(8,128)(2,1)}), bf16[32,17,8,128]{3,2,1,0:T(8,128)(2,1)S(1)}, u32[]{:S(2)}, u32[]{:S(2)}) async-start(bf16[32,17,8,128]{3,2,1,0:T(8,128)(2,1)} %bitcast.2), calls=%async_computation | async-start | bytes 2228224 | tf_op jit(solution)/shard_map/all_to_all | solution.py:473
  11.8 33.4 %copy-start = (bf16[512,512]{1,0:T(8,128)(2,1)S(1)}, bf16[512,512]{1,0:T(8,128)(2,1)}, u32[]{:S(2)}) copy-start(bf16[512,512]{1,0:T(8,128)(2,1)} %constant.58.clone.swap_hbm.swap.refs_1_.refs_8_) | copy-start | bytes 1572868
  41.2 43.0 %all-to-all-start.1 = ((bf16[8,2,8,16,128]{4,3,2,1,0:T(8,128)(2,1)}), bf16[8,2,8,16,128]{4,3,2,1,0:T(8,128)(2,1)S(1)}, u32[]{:S(2)}, u32[]{:S(2)}) async-start(bf16[8,2,8,16,128]{4,3,2,1,0:T(8,128)(2,1)} %shard_map.105), calls=%async_computation.1 | async-start | bytes 1048576 | tf_op jit(solution)/shard_map/all_to_all | solution.py:478
  45.2 20.5 %copy-start.1 = (bf16[128,1024]{1,0:T(8,128)(2,1)S(1)}, bf16[128,1024]{1,0:T(8,128)(2,1)}, u32[]{:S(2)}) copy-start(bf16[128,1024]{1,0:T(8,128)(2,1)} %constant.61.clone.outer_ref) | copy-start | bytes 786436
  45.2 20.4 %copy-start.2 = (bf16[128,128]{1,0:T(8,128)(2,1)S(1)}, bf16[128,128]{1,0:T(8,128)(2,1)}, u32[]{:S(2)}) copy-start(bf16[128,128]{1,0:T(8,128)(2,1)} %constant.60.clone.inner_ref) | copy-start | bytes 98308
  47.4 4.7 %collective-permute-start = (bf16[4,8,8,128]{3,2,1,0:T(8,128)(2,1)S(1)}, bf16[4,8,8,128]{3,2,1,0:T(8,128)(2,1)S(1)}, u32[]{:S(2)}, u32[]{:S(2)}) collective-permute-start(bf16[4,8,8,128]{3,2,1,0:T(8,128)(2,1)S(1)} %get-tuple-element.26), channel_id=1, source_target_pairs={{0,4},{4,0},{8,12},{12,8},{16,20},{20,16},{24,28},{28,24},{1,5},{5... | collective-permute-start | bytes 196616 | tf_op jit(solution)/shard_map/ppermute | solution.py:71
  48.6 7.4 %collective-permute-start.1 = (bf16[4,8,8,128]{3,2,1,0:T(8,128)(2,1)S(1)}, bf16[4,8,8,128]{3,2,1,0:T(8,128)(2,1)S(1)}, u32[]{:S(2)}, u32[]{:S(2)}) collective-permute-start(bf16[4,8,8,128]{3,2,1,0:T(8,128)(2,1)S(1)} %get-tuple-element.27), channel_id=1, source_target_pairs={{0,8},{4,12},{8,0},{12,4},{16,24},{20,28},{24,16},{28,20},{1,9},{5... | collective-permute-start | bytes 196616 | tf_op jit(solution)/shard_map/ppermute | solution.py:71
  50.0 6.9 %collective-permute-start.2 = (bf16[4,8,8,128]{3,2,1,0:T(8,128)(2,1)S(1)}, bf16[4,8,8,128]{3,2,1,0:T(8,128)(2,1)S(1)}, u32[]{:S(2)}, u32[]{:S(2)}) collective-permute-start(bf16[4,8,8,128]{3,2,1,0:T(8,128)(2,1)S(1)} %get-tuple-element.28), channel_id=1, source_target_pairs={{0,12},{4,8},{8,4},{12,0},{16,28},{20,24},{24,20},{28,16},{1,13},{... | collective-permute-start | bytes 196616 | tf_op jit(solution)/shard_map/ppermute | solution.py:71
  50.0 6.9 %collective-permute-start.3 = (bf16[4,8,8,128]{3,2,1,0:T(8,128)(2,1)S(1)}, bf16[4,8,8,128]{3,2,1,0:T(8,128)(2,1)S(1)}, u32[]{:S(2)}, u32[]{:S(2)}) collective-permute-start(bf16[4,8,8,128]{3,2,1,0:T(8,128)(2,1)S(1)} %get-tuple-element.29), channel_id=1, source_target_pairs={{0,16},{4,20},{8,24},{12,28},{16,0},{20,4},{24,8},{28,12},{1,17},{... | collective-permute-start | bytes 196616 | tf_op jit(solution)/shard_map/ppermute | solution.py:71
  51.5 5.6 %collective-permute-start.4 = (bf16[4,8,8,128]{3,2,1,0:T(8,128)(2,1)S(1)}, bf16[4,8,8,128]{3,2,1,0:T(8,128)(2,1)S(1)}, u32[]{:S(2)}, u32[]{:S(2)}) collective-permute-start(bf16[4,8,8,128]{3,2,1,0:T(8,128)(2,1)S(1)} %get-tuple-element.30), channel_id=1, source_target_pairs={{0,20},{4,16},{8,28},{12,24},{16,4},{20,0},{24,12},{28,8},{1,21},{... | collective-permute-start | bytes 196616 | tf_op jit(solution)/shard_map/ppermute | solution.py:71
  52.1 7.1 %collective-permute-start.5 = (bf16[4,8,8,128]{3,2,1,0:T(8,128)(2,1)S(1)}, bf16[4,8,8,128]{3,2,1,0:T(8,128)(2,1)S(1)}, u32[]{:S(2)}, u32[]{:S(2)}) collective-permute-start(bf16[4,8,8,128]{3,2,1,0:T(8,128)(2,1)S(1)} %get-tuple-element.31), channel_id=1, source_target_pairs={{0,24},{4,28},{8,16},{12,20},{16,8},{20,12},{24,0},{28,4},{1,25},{... | collective-permute-start | bytes 196616 | tf_op jit(solution)/shard_map/ppermute | solution.py:71
  56.0 5.2 %collective-permute-start.6 = (bf16[4,8,8,128]{3,2,1,0:T(8,128)(2,1)S(1)}, bf16[4,8,8,128]{3,2,1,0:T(8,128)(2,1)S(1)}, u32[]{:S(2)}, u32[]{:S(2)}) collective-permute-start(bf16[4,8,8,128]{3,2,1,0:T(8,128)(2,1)S(1)} %get-tuple-element.32), channel_id=1, source_target_pairs={{0,28},{4,24},{8,20},{12,16},{16,12},{20,8},{24,4},{28,0},{1,29},{... | collective-permute-start | bytes 196616 | tf_op jit(solution)/shard_map/ppermute | solution.py:71
  61.2 6.2 %collective-permute-start.7 = (bf16[8,8,8,128]{3,2,1,0:T(8,128)(2,1)S(1)}, bf16[8,8,8,128]{3,2,1,0:T(8,128)(2,1)S(1)}, u32[]{:S(2)}, u32[]{:S(2)}) collective-permute-start(bf16[8,8,8,128]{3,2,1,0:T(8,128)(2,1)S(1)} %get-tuple-element.34), channel_id=1, source_target_pairs={{0,1},{1,0},{2,3},{3,2},{4,5},{5,4},{6,7},{7,6},{8,9},{9,8},{10,11... | collective-permute-start | bytes 393224 | tf_op jit(solution)/shard_map/ppermute | solution.py:71
  63.2 12.0 %collective-permute-start.8 = (bf16[8,8,8,128]{3,2,1,0:T(8,128)(2,1)S(1)}, bf16[8,8,8,128]{3,2,1,0:T(8,128)(2,1)S(1)}, u32[]{:S(2)}, u32[]{:S(2)}) collective-permute-start(bf16[8,8,8,128]{3,2,1,0:T(8,128)(2,1)S(1)} %get-tuple-element.35), channel_id=1, source_target_pairs={{0,2},{1,3},{2,0},{3,1},{4,6},{5,7},{6,4},{7,5},{8,10},{9,11},{10,... | collective-permute-start | bytes 393224 | tf_op jit(solution)/shard_map/ppermute | solution.py:71
  63.9 11.3 %collective-permute-start.9 = (bf16[8,8,8,128]{3,2,1,0:T(8,128)(2,1)S(1)}, bf16[8,8,8,128]{3,2,1,0:T(8,128)(2,1)S(1)}, u32[]{:S(2)}, u32[]{:S(2)}) collective-permute-start(bf16[8,8,8,128]{3,2,1,0:T(8,128)(2,1)S(1)} %get-tuple-element.36), channel_id=1, source_target_pairs={{0,3},{1,2},{2,1},{3,0},{4,7},{5,6},{6,5},{7,4},{8,11},{9,10},{10,... | collective-permute-start | bytes 393224 | tf_op jit(solution)/shard_map/ppermute | solution.py:71
  77.9 3.6 %collective-permute-start.10 = (bf16[2,8,16,128]{3,2,1,0:T(8,128)(2,1)S(1)}, bf16[2,8,16,128]{3,2,1,0:T(8,128)(2,1)S(1)}, u32[]{:S(2)}, u32[]{:S(2)}) collective-permute-start(bf16[2,8,16,128]{3,2,1,0:T(8,128)(2,1)S(1)} %get-tuple-element.38), channel_id=1, source_target_pairs={{0,4},{4,0},{8,12},{12,8},{16,20},{20,16},{24,28},{28,24},{1,5},{5... | collective-permute-start | bytes 196616 | tf_op jit(solution)/shard_map/ppermute | solution.py:71
  77.9 5.2 %collective-permute-start.11 = (bf16[2,8,16,128]{3,2,1,0:T(8,128)(2,1)S(1)}, bf16[2,8,16,128]{3,2,1,0:T(8,128)(2,1)S(1)}, u32[]{:S(2)}, u32[]{:S(2)}) collective-permute-start(bf16[2,8,16,128]{3,2,1,0:T(8,128)(2,1)S(1)} %get-tuple-element.39), channel_id=1, source_target_pairs={{0,8},{4,12},{8,0},{12,4},{16,24},{20,28},{24,16},{28,20},{1,9},{5... | collective-permute-start | bytes 196616 | tf_op jit(solution)/shard_map/ppermute | solution.py:71
  78.7 7.5 %collective-permute-start.12 = (bf16[2,8,16,128]{3,2,1,0:T(8,128)(2,1)S(1)}, bf16[2,8,16,128]{3,2,1,0:T(8,128)(2,1)S(1)}, u32[]{:S(2)}, u32[]{:S(2)}) collective-permute-start(bf16[2,8,16,128]{3,2,1,0:T(8,128)(2,1)S(1)} %get-tuple-element.40), channel_id=1, source_target_pairs={{0,12},{4,8},{8,4},{12,0},{16,28},{20,24},{24,20},{28,16},{1,13},{... | collective-permute-start | bytes 196616 | tf_op jit(solution)/shard_map/ppermute | solution.py:71
  79.8 6.5 %collective-permute-start.13 = (bf16[2,8,16,128]{3,2,1,0:T(8,128)(2,1)S(1)}, bf16[2,8,16,128]{3,2,1,0:T(8,128)(2,1)S(1)}, u32[]{:S(2)}, u32[]{:S(2)}) collective-permute-start(bf16[2,8,16,128]{3,2,1,0:T(8,128)(2,1)S(1)} %get-tuple-element.41), channel_id=1, source_target_pairs={{0,16},{4,20},{8,24},{12,28},{16,0},{20,4},{24,8},{28,12},{1,17},{... | collective-permute-start | bytes 196616 | tf_op jit(solution)/shard_map/ppermute | solution.py:71
  80.9 5.4 %collective-permute-start.14 = (bf16[2,8,16,128]{3,2,1,0:T(8,128)(2,1)S(1)}, bf16[2,8,16,128]{3,2,1,0:T(8,128)(2,1)S(1)}, u32[]{:S(2)}, u32[]{:S(2)}) collective-permute-start(bf16[2,8,16,128]{3,2,1,0:T(8,128)(2,1)S(1)} %get-tuple-element.42), channel_id=1, source_target_pairs={{0,20},{4,16},{8,28},{12,24},{16,4},{20,0},{24,12},{28,8},{1,21},{... | collective-permute-start | bytes 196616 | tf_op jit(solution)/shard_map/ppermute | solution.py:71
  81.5 5.9 %collective-permute-start.15 = (bf16[2,8,16,128]{3,2,1,0:T(8,128)(2,1)S(1)}, bf16[2,8,16,128]{3,2,1,0:T(8,128)(2,1)S(1)}, u32[]{:S(2)}, u32[]{:S(2)}) collective-permute-start(bf16[2,8,16,128]{3,2,1,0:T(8,128)(2,1)S(1)} %get-tuple-element.43), channel_id=1, source_target_pairs={{0,24},{4,28},{8,16},{12,20},{16,8},{20,12},{24,0},{28,4},{1,25},{... | collective-permute-start | bytes 196616 | tf_op jit(solution)/shard_map/ppermute | solution.py:71
  83.1 5.3 %collective-permute-start.16 = (bf16[2,8,16,128]{3,2,1,0:T(8,128)(2,1)S(1)}, bf16[2,8,16,128]{3,2,1,0:T(8,128)(2,1)S(1)}, u32[]{:S(2)}, u32[]{:S(2)}) collective-permute-start(bf16[2,8,16,128]{3,2,1,0:T(8,128)(2,1)S(1)} %get-tuple-element.44), channel_id=1, source_target_pairs={{0,28},{4,24},{8,20},{12,16},{16,12},{20,8},{24,4},{28,0},{1,29},{... | collective-permute-start | bytes 196616 | tf_op jit(solution)/shard_map/ppermute | solution.py:71

commit v3 on v2

--- a/solution.py
+++ b/solution.py
@@ -107,17 +107,23 @@
     return jnp.concatenate(lhs, axis=1)
 
 
-def pack_one(plan, velocity, quantity, place):
-    p = plan
-    shape = (p.ta, p.rg, p.tl, LANES)
+def pack_one(plan, velocity, quantity, packed, place):
+    p = plan
+    shape = (p.ta, p.rg + 1, p.tl, LANES)
     if not p.by_partner or not p.fast:
         x = velocity[quantity].reshape(p.tl, p.groups, p.rg, p.ta, p.blocks, p.cc)
-        x = x.transpose(4, 3, 2, 0, 1, 5).reshape((p.blocks,) + shape)
+        x = x.transpose(4, 3, 2, 0, 1, 5).reshape(p.blocks, p.ta, p.rg, p.tl, LANES)
+        side = velocity[0].reshape(p.tl, p.xb, p.chunks, p.cc)
+        before = jnp.roll(side[..., p.cc - 2 :], 1, axis=2)
+        after = jnp.roll(side[..., :2], -1, axis=2)
+        side = jnp.concatenate([before, after], axis=3).transpose(2, 0, 1, 3)
+        side = side.reshape(p.ta, p.blocks, 1, p.tl, LANES).swapaxes(0, 1)
+        x = jnp.concatenate([x, side], axis=2)
         x = jnp.take(x, jnp.arange(p.ta, dtype=jnp.int32) ^ place[0], axis=1)
         return [jnp.take(x, place[1] ^ n, axis=0) for n in range(p.blocks)] if p.by_partner else [x]
     per_slab = p.cs // LANES
 
-    def body(place_ref, swap, velocity_ref, *rest):
+    def body(place_ref, swap, picks, packed_ref, velocity_ref, *rest):
         outs = rest[: p.blocks]
         x, sems, wide, chunks = rest[p.blocks :]
         copies = []
@@ -127,6 +133,24 @@
                 pltpu.make_async_copy(velocity_ref.at[quantity, :, :, columns], x.at[m], sems.at[m])
             )
             copies[-1].start()
+        acc = jnp.zeros((p.chunks * p.tl, 2 * LANES), jnp.float32)
+        for r in range(p.rg):
+            rows = [
+                packed_ref[c % p.blocks, c // p.blocks, p.rg + r].astype(jnp.float32)
+                for c in range(p.chunks)
+            ]
+            acc = acc + jnp.dot(
+                jnp.concatenate(rows, axis=0).astype(jnp.bfloat16),
+                picks[r * LANES : (r + 1) * LANES, :],
+                preferred_element_type=jnp.float32,
+            )
+        for c in range(p.chunks):
+            before, after = (c + p.chunks - 1) % p.chunks, (c + 1) % p.chunks
+            both = (
+                acc[before * p.tl : (before + 1) * p.tl, :LANES]
+                + acc[after * p.tl : (after + 1) * p.tl, LANES:]
+            )
+            chunks[c % p.blocks, place_ref[0] ^ (c // p.blocks), p.rg] = both.astype(jnp.bfloat16)
         for m in range(p.ta):
             copies[m].wait()
             for i in range(per_slab):
@@ -140,7 +164,7 @@
             m, i = divmod(tile, per_slab)
             for g in range(p.groups):
                 mine = swapped[tile * count : (tile + 1) * count, g * LANES : (g + 1) * LANES]
-                chunks[i * p.groups + g, m] = mine.reshape(p.rg, p.tl, LANES)
+                chunks[i * p.groups + g, m, 0 : p.rg] = mine.reshape(p.rg, p.tl, LANES)
         for n in range(p.blocks):
             outs[n][...] = chunks[place_ref[1] ^ n]
 
@@ -151,7 +175,8 @@
         pltpu.VMEM((p.zb // LANES, p.groups, p.tl * p.rg, LANES), jnp.float32),
         pltpu.VMEM((p.blocks,) + shape, velocity.dtype),
     ]
-    return on_chip(body, [group_swap(p), velocity], outs, scratch, (place,), in_hbm=1)
+    inputs = [group_swap(p), side_picks(p), packed, velocity]
+    return on_chip(body, inputs, outs, scratch, (place,), in_hbm=1)
 
 
 def regroup(plan, arrays):
@@ -164,33 +189,25 @@
             for m in range(p.ta):
                 refs[p.blocks + m][n] = refs[n][m]
 
-    outs = [pltpu.VMEM((p.blocks, p.rg, p.tl, LANES), arrays[0].dtype) for _ in range(p.ta)]
+    outs = [pltpu.VMEM((p.blocks,) + arrays[0].shape[1:], arrays[0].dtype) for _ in range(p.ta)]
     return on_chip(body, list(arrays), outs, [])
 
 
 def pack_all(plan, velocity):
     p = plan
-    shape = (p.blocks, p.ta, 2 * p.rg + 1, p.tl, LANES)
+    shape = (p.blocks, p.ta, 2 * p.rg, p.tl, LANES)
     if not p.fast:
         out = []
         for quantity in (2, 0):
             x = velocity[quantity].reshape(p.tl, p.groups, p.rg, p.ta, p.blocks, p.cc)
             out.append(x.transpose(4, 3, 2, 0, 1, 5).reshape(p.blocks, p.ta, p.rg, p.tl, LANES))
-        x = velocity[0].reshape(p.tl, p.xb, p.chunks, p.cc)
-        before = jnp.roll(x[..., p.cc - 2 :], 1, axis=2)
-        after = jnp.roll(x[..., :2], -1, axis=2)
-        side = jnp.concatenate([before, after], axis=3).transpose(2, 0, 1, 3)
-        out.append(side.reshape(p.ta, p.blocks, 1, p.tl, LANES).swapaxes(0, 1))
         return jnp.concatenate(out, axis=2)
     per_slab = p.cs // LANES
     half = max(p.ta // 2, 1)
 
-    def body(swap_hbm, picks_hbm, velocity_ref, out, x, sems, table_sems, wide, swap, picks, chunks):
-        tables = [
-            pltpu.make_async_copy(swap_hbm, swap, table_sems.at[0]),
-            pltpu.make_async_copy(picks_hbm, picks, table_sems.at[1]),
-        ]
-        tables[0].start()
+    def body(swap_hbm, velocity_ref, out, x, sems, table_sems, wide, swap):
+        table = pltpu.make_async_copy(swap_hbm, swap, table_sems.at[0])
+        table.start()
         copies = {}
         for n, quantity in enumerate((2, 0)):
             for start in range(0, p.ta, half):
@@ -199,8 +216,7 @@
                     velocity_ref.at[quantity, :, :, columns], x.at[n, :, :, columns], sems.at[n, start]
                 )
                 copies[n, start].start()
-        tables[1].start()
-        tables[0].wait()
+        table.wait()
         count = p.rg * p.tl
         for n in range(2):
             for start in range(0, p.ta, half):
@@ -216,40 +232,20 @@
                     m, i = divmod(tile, per_slab)
                     for g in range(p.groups):
                         mine = swapped[at : at + count, g * LANES : (g + 1) * LANES]
-                        if n == 1:
-                            chunks[tile * p.groups + g] = mine
                         out[i * p.groups + g, m, n * p.rg : (n + 1) * p.rg] = mine.reshape(
                             p.rg, p.tl, LANES
                         ).astype(jnp.bfloat16)
-        tables[1].wait()
-        acc = jnp.zeros((p.chunks * p.tl, 2 * LANES), jnp.float32)
-        for r in range(p.rg):
-            rows = [chunks[c, r * p.tl : (r + 1) * p.tl, :] for c in range(p.chunks)]
-            acc = acc + jnp.dot(
-                jnp.concatenate(rows, axis=0).astype(jnp.bfloat16),
-                picks[r * LANES : (r + 1) * LANES, :],
-                preferred_element_type=jnp.float32,
-            )
-        for c in range(p.chunks):
-            before, after = (c + p.chunks - 1) % p.chunks, (c + 1) % p.chunks
-            both = (
-                acc[before * p.tl : (before + 1) * p.tl, :LANES]
-                + acc[after * p.tl : (after + 1) * p.tl, LANES:]
-            )
-            out[c % p.blocks, c // p.blocks, 2 * p.rg] = both.astype(jnp.bfloat16)
-
-    swap, picks = group_swap(p), side_picks(p)
+
+    swap = group_swap(p)
     scratch = [
         pltpu.VMEM((2, p.tl, p.xb, p.zb), velocity.dtype),
         pltpu.SemaphoreType.DMA((2, p.ta)),
-        pltpu.SemaphoreType.DMA((2,)),
+        pltpu.SemaphoreType.DMA((1,)),
         pltpu.VMEM((p.zb // LANES, p.groups, p.tl * p.rg, LANES), jnp.float32),
         pltpu.VMEM(swap.shape, swap.dtype),
-        pltpu.VMEM(picks.shape, picks.dtype),
-        pltpu.VMEM((p.chunks, p.rg * p.tl, LANES), jnp.float32),
     ]
     outs = pltpu.VMEM(shape, velocity.dtype)
-    return on_chip(body, [swap, picks, velocity], outs, scratch, in_hbm=3)
+    return on_chip(body, [swap, velocity], outs, scratch, in_hbm=2)
 
 
 def slope_taps(plan):
@@ -276,11 +272,19 @@
     return jnp.concatenate(x, axis=0)
 
 
-def vorticity(plan, both, place):
+def vorticity(plan, both, wall, place):
     p = plan
     inner, outer = slope_taps(p)
 
-    def body(place_ref, x, inner_ref, outer_ref, out, sides, slope):
+    def body(place_ref, x, inner_ref, outer_ref, *rest):
+        arrived, (out, sides, slope, beside) = rest[: p.ta], rest[p.ta :]
+        for m in range(p.ta):
+            beside[m] = arrived[m][:, p.rg].astype(jnp.float32)
+
+        def side_of(b):
+            at = place_ref[1] ^ b if p.by_partner else b
+            return jnp.concatenate([beside[place_ref[0] ^ t, at] for t in range(p.ta)], axis=0)
+
         chunk = place_ref[0] * p.blocks + place_ref[1]
         first = (chunk == 0).astype(jnp.int32)
         last = (chunk == p.chunks - 1).astype(jnp.int32)
@@ -289,8 +293,7 @@
             for z in range(p.gz):
                 before = a * p.gz + lax.rem(z + p.gz - first, p.gz)
                 after = a * p.gz + lax.rem(z + last, p.gz)
-                left = series_of(x, before, 2 * p.rg)
-                right = series_of(x, after, 2 * p.rg)
+                left, right = side_of(before), side_of(after)
                 b = a * p.gz + z
                 side = jnp.where(lane % 4 < 2, left, right).astype(jnp.bfloat16)
                 sides[b * p.nt : (b + 1) * p.nt, :] = side
@@ -324,8 +327,9 @@
     scratch = [
         pltpu.VMEM((p.blocks * p.nt, LANES), jnp.bfloat16),
         pltpu.VMEM((p.blocks * p.nt, p.rg * LANES), jnp.float32),
+        pltpu.VMEM((p.ta, p.blocks, p.tl, LANES), jnp.float32),
     ]
-    return on_chip(body, [both, inner, outer], outs, scratch, (place,))
+    return on_chip(body, [both, inner, outer, *wall], outs, scratch, (place,))
 
 
 def cross(plan, jobs, owner, place, by_partner):
@@ -468,8 +472,8 @@
     time = lax.axis_index("ta").astype(jnp.int32)
     place = jnp.stack([time, lax.axis_index(block_axes).astype(jnp.int32)])
 
-    both = pack_all(plan, velocity)
-    both = both.reshape((-1,) + both.shape[2:])
+    packed = pack_all(plan, velocity)
+    both = packed.reshape((-1,) + packed.shape[2:])
     both = lax.all_to_all(both, block_axes + ("ta",), split_axis=0, concat_axis=0, tiled=True)
     both = both.reshape((plan.blocks, plan.ta) + both.shape[1:])
 
@@ -478,7 +482,7 @@
             return [lax.all_to_all(arrays[0], block_axes, split_axis=0, concat_axis=0, tiled=True)]
         return [arrays[0]] + [trade(arrays[n], block_axes, n, plan.blocks) for n in range(1, plan.blocks)]
 
-    wall = pack_one(plan, velocity, 1, place)
+    wall = pack_one(plan, velocity, 1, packed, place)
     wall = over_blocks(wall)
     wall = regroup(plan, wall)
     wall = [wall[0]] + [trade(wall[m], "ta", m, plan.ta) for m in range(1, plan.ta)]
@@ -489,7 +493,7 @@
     table = dft_rows(offsets, (turn * plan.tl + times).reshape(-1))
     early = cross(plan, [([both], 0, table), ([both], plan.rg, table)], owner, place, False)
     early = over_blocks(early)
-    spin = vorticity(plan, both, place)
+    spin = vorticity(plan, both, wall, place)
     late = cross(plan, [([spin], 0, table), (wall, 0, table_wall)], owner, place, plan.by_partner)
     late = over_blocks(late)
     out = assemble(plan, None, (2, 0), early, place)

time: 90.8 us -> 92.3 us (1.017)
    ppermute x17, waiting for transfers between devices: 16.9 us -> 18.7 us  [trade(): return lax.ppermute(x, axis, [(i, i ^ step) for i in range(count)])]
    all_to_all x1, waiting for transfers between devices: 25.2 us -> 23.8 us  [shards(): lax.all_to_all(both, block_axes + ('ta',), split_axis=0, concat_axis=0, t...]
  transfers between devices with their start and end apart: 19 -> 19, of which waited for: 10 -> 10; matrix products, arithmetic and copies ran while one was open for 1% -> 1% of each run, Pallas kernels for 9% -> 11%
where the time goes in v3:
time: 92.3 us; the launch traced here: 91.8 us
  waiting for transfers between devices  42.5 us (46%)
  starting transfers between devices  29.6 us (32%)
  Pallas kernels  18.3 us (20%)
    all_to_all x1, waiting for transfers between devices, shards(): lax.all_to_all(both, block_axes + ('ta',), split_axis=0, concat_axis=0, t...  23.8 us
    ppermute x17, waiting for transfers between devices, trade(): return lax.ppermute(x, axis, [(i, i ^ step) for i in range(count)])  18.7 us
    pallas_call x8, Pallas kernels, on_chip(): pl.pallas_call(body, in_specs=[smem] * len(scalars) + [vmem] * count + [h...  18.3 us
    ppermute x17, starting transfers between devices, trade(): return lax.ppermute(x, axis, [(i, i ^ step) for i in range(count)])  18.3 us
    all_to_all x1, starting transfers between devices, shards(): lax.all_to_all(both, block_axes + ('ta',), split_axis=0, concat_axis=0, t...  7.33 us
    all_to_all x1, starting transfers between devices, over_blocks(): lax.all_to_all(arrays[0], block_axes, split_axis=0, concat_axis=0, tiled=...  4.04 us
  transfers between devices with their start and end apart: 19, of which 10 were waited for; matrix products, arithmetic and copies ran while one was open for 1% of the time, Pallas kernels for 11%

profile of v3, /device:TPU:0, one launch (start us, length us, event | category | flops | bytes accessed | tf_op | source)
XLA Modules:
  0.0 91.8 jit_solution(13789301590169732932)
XLA Ops:
  0.0 3.6 %shard_map.100.packed_ref = bf16[8,4,16,8,128]{4,3,2,1,0:T(8,128)(2,1)} custom-call(bf16[512,512]{1,0:T(8,128)(2,1)} %constant.58.clone.swap_hbm.swap.refs_1_.refs_8_, bf16[3,8,32,1024]{3,2,1,0:T(8,128)(2,1)} %velocity_ref.3), custom_call_target="tpu_custom_call" | custom-call | tf_op jit(solution)/shard_map/pallas_call | solution.py:46
  3.6 7.3 %all-to-all-start = ((bf16[32,16,8,128]{3,2,1,0:T(8,128)(2,1)}), bf16[32,16,8,128]{3,2,1,0:T(8,128)(2,1)S(1)}, u32[]{:S(2)}, u32[]{:S(2)}) async-start(bf16[32,16,8,128]{3,2,1,0:T(8,128)(2,1)} %bitcast.2), calls=%async_computation | async-start | bytes 2097152 | tf_op jit(solution)/shard_map/all_to_all | solution.py:477
  12.0 23.8 %all-to-all-done = bf16[32,16,8,128]{3,2,1,0:T(8,128)(2,1)S(1)} async-done(((bf16[32,16,8,128]{3,2,1,0:T(8,128)(2,1)}), bf16[32,16,8,128]{3,2,1,0:T(8,128)(2,1)S(1)}, u32[]{:S(2)}, u32[]{:S(2)}) %all-to-all-start) | async-done | bytes 1048608 | tf_op jit(solution)/shard_map/all_to_all | solution.py:477
  35.9 3.1 %shard_map.105 = bf16[8,2,8,16,128]{4,3,2,1,0:T(8,128)(2,1)} custom-call(s32[7]{0:T(128)S(1)} %copy-done.4, s32[2]{0:T(128)S(1)} %pad_add_fusion.place_ref, bf16[8,4,16,8,128]{4,3,2,1,0:T(8,128)(2,1)S(1)} %bitcast.6, bf16[112,32]{1,0:T(8,128)(2,1)S(1)} %bitcast.8), custom_call_target="tpu_custom_call" | custom-call | tf_op jit(solution)/shard_map/pallas_call | solution.py:46
  39.0 4.0 %all-to-all-start.1 = ((bf16[8,2,8,16,128]{4,3,2,1,0:T(8,128)(2,1)}), bf16[8,2,8,16,128]{4,3,2,1,0:T(8,128)(2,1)S(1)}, u32[]{:S(2)}, u32[]{:S(2)}) async-start(bf16[8,2,8,16,128]{4,3,2,1,0:T(8,128)(2,1)} %shard_map.105), calls=%async_computation.1 | async-start | bytes 1048576 | tf_op jit(solution)/shard_map/all_to_all | solution.py:482
  43.1 3.5 %shard_map.101 = (bf16[4,9,8,128]{3,2,1,0:T(8,128)(2,1)S(1)}, bf16[4,9,8,128]{3,2,1,0:T(8,128)(2,1)S(1)}, bf16[4,9,8,128]{3,2,1,0:T(8,128)(2,1)S(1)}, bf16[4,9,8...) custom-call(s32[2]{0:T(128)S(1)} %pad_add_fusion.place_ref, ...), custom_call_target="tpu_custom_call" | custom-call | tf_op jit(solution)/shard_map/pallas_call | solution.py:46
  46.6 1.2 %collective-permute-start = (bf16[4,9,8,128]{3,2,1,0:T(8,128)(2,1)S(1)}, bf16[4,9,8,128]{3,2,1,0:T(8,128)(2,1)S(1)}, u32[]{:S(2)}, u32[]{:S(2)}) collective-permute-start(bf16[4,9,8,128]{3,2,1,0:T(8,128)(2,1)S(1)} %get-tuple-element.26), channel_id=1, source_target_pairs={{0,4},{4,0},{8,12},{12,8},{16,20},{20,16},{24,28},{28,24},{1,5},{5... | collective-permute-start | bytes 221192 | tf_op jit(solution)/shard_map/ppermute | solution.py:71
  47.7 1.4 %collective-permute-start.1 = (bf16[4,9,8,128]{3,2,1,0:T(8,128)(2,1)S(1)}, bf16[4,9,8,128]{3,2,1,0:T(8,128)(2,1)S(1)}, u32[]{:S(2)}, u32[]{:S(2)}) collective-permute-start(bf16[4,9,8,128]{3,2,1,0:T(8,128)(2,1)S(1)} %get-tuple-element.27), channel_id=1, source_target_pairs={{0,8},{4,12},{8,0},{12,4},{16,24},{20,28},{24,16},{28,20},{1,9},{5... | collective-permute-start | bytes 221192 | tf_op jit(solution)/shard_map/ppermute | solution.py:71
  49.2 1.5 %collective-permute-start.3 = (bf16[4,9,8,128]{3,2,1,0:T(8,128)(2,1)S(1)}, bf16[4,9,8,128]{3,2,1,0:T(8,128)(2,1)S(1)}, u32[]{:S(2)}, u32[]{:S(2)}) collective-permute-start(bf16[4,9,8,128]{3,2,1,0:T(8,128)(2,1)S(1)} %get-tuple-element.29), channel_id=1, source_target_pairs={{0,16},{4,20},{8,24},{12,28},{16,0},{20,4},{24,8},{28,12},{1,17},{... | collective-permute-start | bytes 221192 | tf_op jit(solution)/shard_map/ppermute | solution.py:71
  50.6 0.6 collective-permute-start.4
  51.2 1.9 %collective-permute-start.5 = (bf16[4,9,8,128]{3,2,1,0:T(8,128)(2,1)S(1)}, bf16[4,9,8,128]{3,2,1,0:T(8,128)(2,1)S(1)}, u32[]{:S(2)}, u32[]{:S(2)}) collective-permute-start(bf16[4,9,8,128]{3,2,1,0:T(8,128)(2,1)S(1)} %get-tuple-element.31), channel_id=1, source_target_pairs={{0,24},{4,28},{8,16},{12,20},{16,8},{20,12},{24,0},{28,4},{1,25},{... | collective-permute-start | bytes 221192 | tf_op jit(solution)/shard_map/ppermute | solution.py:71
  53.2 0.8 collective-permute-done.1.refs_2_
  54.0 0.6 collective-permute-start.6
  54.5 0.6 collective-permute-done.2.refs_3_
  55.4 3.0 %collective-permute-done.5.refs_6_ = bf16[4,9,8,128]{3,2,1,0:T(8,128)(2,1)S(1)} collective-permute-done((bf16[4,9,8,128]{3,2,1,0:T(8,128)(2,1)S(1)}, bf16[4,9,8,128]{3,2,1,0:T(8,128)(2,1)S(1)}, u32[]{:S(2)}, u32[]{:S(2)}) %collective-permute-start.5) | collective-permute-done | bytes 73760 | tf_op jit(solution)/shard_map/ppermute | solution.py:71
  58.3 1.1 %collective-permute-done.6.refs_7_ = bf16[4,9,8,128]{3,2,1,0:T(8,128)(2,1)S(1)} collective-permute-done((bf16[4,9,8,128]{3,2,1,0:T(8,128)(2,1)S(1)}, bf16[4,9,8,128]{3,2,1,0:T(8,128)(2,1)S(1)}, u32[]{:S(2)}, u32[]{:S(2)}) %collective-permute-start.6) | collective-permute-done | bytes 73760 | tf_op jit(solution)/shard_map/ppermute | solution.py:71
  59.5 2.4 %collective-permute-start.7 = (bf16[8,9,8,128]{3,2,1,0:T(8,128)(2,1)S(1)}, bf16[8,9,8,128]{3,2,1,0:T(8,128)(2,1)S(1)}, u32[]{:S(2)}, u32[]{:S(2)}) collective-permute-start(bf16[8,9,8,128]{3,2,1,0:T(8,128)(2,1)S(1)} %get-tuple-element.34), channel_id=1, source_target_pairs={{0,1},{1,0},{2,3},{3,2},{4,5},{5,4},{6,7},{7,6},{8,9},{9,8},{10,11... | collective-permute-start | bytes 442376 | tf_op jit(solution)/shard_map/ppermute | solution.py:71
  61.9 0.7 collective-permute-start.8
  62.6 1.7 %collective-permute-start.9 = (bf16[8,9,8,128]{3,2,1,0:T(8,128)(2,1)S(1)}, bf16[8,9,8,128]{3,2,1,0:T(8,128)(2,1)S(1)}, u32[]{:S(2)}, u32[]{:S(2)}) collective-permute-start(bf16[8,9,8,128]{3,2,1,0:T(8,128)(2,1)S(1)} %get-tuple-element.36), channel_id=1, source_target_pairs={{0,3},{1,2},{2,1},{3,0},{4,7},{5,6},{6,5},{7,4},{8,11},{9,10},{10,... | collective-permute-start | bytes 442376 | tf_op jit(solution)/shard_map/ppermute | solution.py:71
  64.3 2.4 %collective-permute-done.7.rest_1_.refs_3_ = bf16[8,9,8,128]{3,2,1,0:T(8,128)(2,1)S(1)} collective-permute-done((bf16[8,9,8,128]{3,2,1,0:T(8,128)(2,1)S(1)}, bf16[8,9,8,128]{3,2,1,0:T(8,128)(2,1)S(1)}, u32[]{:S(2)}, u32[]{:S(2)}) %collective-permute-start.7) | collective-permute-done | bytes 147488 | tf_op jit(solution)/shard_map/ppermute | solution.py:71
  66.7 8.5 %collective-permute-done.8.rest_2_.refs_4_ = bf16[8,9,8,128]{3,2,1,0:T(8,128)(2,1)S(1)} collective-permute-done((bf16[8,9,8,128]{3,2,1,0:T(8,128)(2,1)S(1)}, bf16[8,9,8,128]{3,2,1,0:T(8,128)(2,1)S(1)}, u32[]{:S(2)}, u32[]{:S(2)}) %collective-permute-start.8) | collective-permute-done | bytes 147488 | tf_op jit(solution)/shard_map/ppermute | solution.py:71
  75.2 1.4 %shard_map.103.refs_0_ = bf16[8,4,8,8,128]{4,3,2,1,0:T(8,128)(2,1)S(1)} custom-call(s32[2]{0:T(128)S(1)} %pad_add_fusion.place_ref, bf16[8,4,16,8,128]{4,3,2,1,0:T(8,128)(2,1)S(1)} %bitcast.7, bf16[128,128]{1,0:T(8,128)(2,1)S(1)} %copy-done.3, bf16[128,1024]{1,0:T(8,128)(2,1)S(1)} %copy-done.2, bf16[8,9,8,128]{3,2,1,0:T(8,128)(2,1)S(1)} %get-tuple-element.33.rest_0_.refs_2_, ...), custom_call_target="tpu_custom_call" | custom-call | tf_op jit(solution)/shard_map/pallas_call | solution.py:46
  76.6 2.6 %shard_map.104 = (bf16[2,8,16,128]{3,2,1,0:T(8,128)(2,1)S(1)}, bf16[2,8,16,128]{3,2,1,0:T(8,128)(2,1)S(1)}, bf16[2,8,16,128]{3,2,1,0:T(8,128)(2,1)S(1)}, bf16[2,...) custom-call(s32[7]{0:T(128)S(1)} %copy-done.4, ...), custom_call_target="tpu_custom_call" | custom-call | tf_op jit(solution)/shard_map/pallas_call | solution.py:46
  79.3 0.4 collective-permute-start.11
  79.7 1.4 %collective-permute-start.12 = (bf16[2,8,16,128]{3,2,1,0:T(8,128)(2,1)S(1)}, bf16[2,8,16,128]{3,2,1,0:T(8,128)(2,1)S(1)}, u32[]{:S(2)}, u32[]{:S(2)}) collective-permute-start(bf16[2,8,16,128]{3,2,1,0:T(8,128)(2,1)S(1)} %get-tuple-element.40), channel_id=1, source_target_pairs={{0,12},{4,8},{8,4},{12,0},{16,28},{20,24},{24,20},{28,16},{1,13},{... | collective-permute-start | bytes 196616 | tf_op jit(solution)/shard_map/ppermute | solution.py:71
  81.2 1.5 %collective-permute-start.13 = (bf16[2,8,16,128]{3,2,1,0:T(8,128)(2,1)S(1)}, bf16[2,8,16,128]{3,2,1,0:T(8,128)(2,1)S(1)}, u32[]{:S(2)}, u32[]{:S(2)}) collective-permute-start(bf16[2,8,16,128]{3,2,1,0:T(8,128)(2,1)S(1)} %get-tuple-element.41), channel_id=1, source_target_pairs={{0,16},{4,20},{8,24},{12,28},{16,0},{20,4},{24,8},{28,12},{1,17},{... | collective-permute-start | bytes 196616 | tf_op jit(solution)/shard_map/ppermute | solution.py:71
  82.9 1.6 %collective-permute-start.15 = (bf16[2,8,16,128]{3,2,1,0:T(8,128)(2,1)S(1)}, bf16[2,8,16,128]{3,2,1,0:T(8,128)(2,1)S(1)}, u32[]{:S(2)}, u32[]{:S(2)}) collective-permute-start(bf16[2,8,16,128]{3,2,1,0:T(8,128)(2,1)S(1)} %get-tuple-element.43), channel_id=1, source_target_pairs={{0,24},{4,28},{8,16},{12,20},{16,8},{20,12},{24,0},{28,4},{1,25},{... | collective-permute-start | bytes 196616 | tf_op jit(solution)/shard_map/ppermute | solution.py:71
  84.4 1.1 %collective-permute-start.16 = (bf16[2,8,16,128]{3,2,1,0:T(8,128)(2,1)S(1)}, bf16[2,8,16,128]{3,2,1,0:T(8,128)(2,1)S(1)}, u32[]{:S(2)}, u32[]{:S(2)}) collective-permute-start(bf16[2,8,16,128]{3,2,1,0:T(8,128)(2,1)S(1)} %get-tuple-element.44), channel_id=1, source_target_pairs={{0,28},{4,24},{8,20},{12,16},{16,12},{20,8},{24,4},{28,0},{1,29},{... | collective-permute-start | bytes 196616 | tf_op jit(solution)/shard_map/ppermute | solution.py:71
  85.6 2.1 %shard_map.106.refs_9_ = f32[4,2,7,32,256]{4,3,2,1,0:T(8,128)} custom-call(s32[2]{0:T(128)S(1)} %pad_add_fusion.place_ref, bf16[8,2,8,16,128]{4,3,2,1,0:T(8,128)(2,1)S(1)} %all-to-all-done.1.refs_0_, bf16[512,512]{1,0:T(8,128)(2,1)S(1)} %copy-done), custom_call_target="tpu_custom_call" | custom-call | tf_op jit(solution)/shard_map/pallas_call | solution.py:46
  87.7 1.0 %collective-permute-done.15.refs_6_ = bf16[2,8,16,128]{3,2,1,0:T(8,128)(2,1)S(1)} collective-permute-done((bf16[2,8,16,128]{3,2,1,0:T(8,128)(2,1)S(1)}, bf16[2,8,16,128]{3,2,1,0:T(8,128)(2,1)S(1)}, u32[]{:S(2)}, u32[]{:S(2)}) %collective-permute-start.15) | collective-permute-done | bytes 65568 | tf_op jit(solution)/shard_map/ppermute | solution.py:71
  88.7 1.0 %collective-permute-done.16.refs_7_ = bf16[2,8,16,128]{3,2,1,0:T(8,128)(2,1)S(1)} collective-permute-done((bf16[2,8,16,128]{3,2,1,0:T(8,128)(2,1)S(1)}, bf16[2,8,16,128]{3,2,1,0:T(8,128)(2,1)S(1)}, u32[]{:S(2)}, u32[]{:S(2)}) %collective-permute-start.16) | collective-permute-done | bytes 65568 | tf_op jit(solution)/shard_map/ppermute | solution.py:71
  89.7 2.0 %shard_map.107 = f32[4,2,7,32,256]{4,3,2,1,0:T(8,128)} custom-call(s32[2]{0:T(128)S(1)} %pad_add_fusion.place_ref, bf16[2,8,16,128]{3,2,1,0:T(8,128)(2,1)S(1)} %get-tuple-element.37.refs_0_, bf16[2,8,16,128]{3,2,1,0:T(8,128)(2,1)S(1)} %collective-permute-done.10.refs_1_, ...), custom_call_target="tpu_custom_call", output_to_operand_aliasing={{}: (10, {})} | custom-call | tf_op jit(solution)/shard_map/pallas_call | solution.py:46
  (40 shorter events, 1.6 us)
Async XLA Ops:
  3.6 7.8 %copy-start.5 = (s32[7]{0:T(128)S(1)}, s32[7]{0:T(128)}, u32[]{:S(2)}) copy-start(s32[7]{0:T(128)} %param.11) | copy-start | bytes 88
  3.6 32.3 %copy-start.4 = (s32[7]{0:T(128)S(1)}, s32[7]{0:T(128)}, u32[]{:S(2)}) copy-start(s32[7]{0:T(128)} %owner_ref.3) | copy-start | bytes 88
  3.6 32.3 %all-to-all-start = ((bf16[32,16,8,128]{3,2,1,0:T(8,128)(2,1)}), bf16[32,16,8,128]{3,2,1,0:T(8,128)(2,1)S(1)}, u32[]{:S(2)}, u32[]{:S(2)}) async-start(bf16[32,16,8,128]{3,2,1,0:T(8,128)(2,1)} %bitcast.2), calls=%async_computation | async-start | bytes 2097152 | tf_op jit(solution)/shard_map/all_to_all | solution.py:477
  11.0 32.1 %copy-start = (bf16[512,512]{1,0:T(8,128)(2,1)S(1)}, bf16[512,512]{1,0:T(8,128)(2,1)}, u32[]{:S(2)}) copy-start(bf16[512,512]{1,0:T(8,128)(2,1)} %constant.58.clone.swap_hbm.swap.refs_1_.refs_8_) | copy-start | bytes 1572868
  11.0 32.1 %copy-start.1 = (bf16[1024,256]{1,0:T(8,128)(2,1)S(1)}, bf16[1024,256]{1,0:T(8,128)(2,1)}, u32[]{:S(2)}) copy-start(bf16[1024,256]{1,0:T(8,128)(2,1)} %constant.59.clone.picks) | copy-start | bytes 1572868
  39.0 46.6 %all-to-all-start.1 = ((bf16[8,2,8,16,128]{4,3,2,1,0:T(8,128)(2,1)}), bf16[8,2,8,16,128]{4,3,2,1,0:T(8,128)(2,1)S(1)}, u32[]{:S(2)}, u32[]{:S(2)}) async-start(bf16[8,2,8,16,128]{4,3,2,1,0:T(8,128)(2,1)} %shard_map.105), calls=%async_computation.1 | async-start | bytes 1048576 | tf_op jit(solution)/shard_map/all_to_all | solution.py:482
  43.0 32.2 %copy-start.2 = (bf16[128,1024]{1,0:T(8,128)(2,1)S(1)}, bf16[128,1024]{1,0:T(8,128)(2,1)}, u32[]{:S(2)}) copy-start(bf16[128,1024]{1,0:T(8,128)(2,1)} %constant.61.clone.outer_ref) | copy-start | bytes 786436
  43.0 32.2 %copy-start.3 = (bf16[128,128]{1,0:T(8,128)(2,1)S(1)}, bf16[128,128]{1,0:T(8,128)(2,1)}, u32[]{:S(2)}) copy-start(bf16[128,128]{1,0:T(8,128)(2,1)} %constant.60.clone.inner_ref) | copy-start | bytes 98308
  46.6 4.7 %collective-permute-start = (bf16[4,9,8,128]{3,2,1,0:T(8,128)(2,1)S(1)}, bf16[4,9,8,128]{3,2,1,0:T(8,128)(2,1)S(1)}, u32[]{:S(2)}, u32[]{:S(2)}) collective-permute-start(bf16[4,9,8,128]{3,2,1,0:T(8,128)(2,1)S(1)} %get-tuple-element.26), channel_id=1, source_target_pairs={{0,4},{4,0},{8,12},{12,8},{16,20},{20,16},{24,28},{28,24},{1,5},{5... | collective-permute-start | bytes 221192 | tf_op jit(solution)/shard_map/ppermute | solution.py:71
  47.7 6.2 %collective-permute-start.1 = (bf16[4,9,8,128]{3,2,1,0:T(8,128)(2,1)S(1)}, bf16[4,9,8,128]{3,2,1,0:T(8,128)(2,1)S(1)}, u32[]{:S(2)}, u32[]{:S(2)}) collective-permute-start(bf16[4,9,8,128]{3,2,1,0:T(8,128)(2,1)S(1)} %get-tuple-element.27), channel_id=1, source_target_pairs={{0,8},{4,12},{8,0},{12,4},{16,24},{20,28},{24,16},{28,20},{1,9},{5... | collective-permute-start | bytes 221192 | tf_op jit(solution)/shard_map/ppermute | solution.py:71
  49.2 5.9 %collective-permute-start.2 = (bf16[4,9,8,128]{3,2,1,0:T(8,128)(2,1)S(1)}, bf16[4,9,8,128]{3,2,1,0:T(8,128)(2,1)S(1)}, u32[]{:S(2)}, u32[]{:S(2)}) collective-permute-start(bf16[4,9,8,128]{3,2,1,0:T(8,128)(2,1)S(1)} %get-tuple-element.28), channel_id=1, source_target_pairs={{0,12},{4,8},{8,4},{12,0},{16,28},{20,24},{24,20},{28,16},{1,13},{... | collective-permute-start | bytes 221192 | tf_op jit(solution)/shard_map/ppermute | solution.py:71
  49.2 5.9 %collective-permute-start.3 = (bf16[4,9,8,128]{3,2,1,0:T(8,128)(2,1)S(1)}, bf16[4,9,8,128]{3,2,1,0:T(8,128)(2,1)S(1)}, u32[]{:S(2)}, u32[]{:S(2)}) collective-permute-start(bf16[4,9,8,128]{3,2,1,0:T(8,128)(2,1)S(1)} %get-tuple-element.29), channel_id=1, source_target_pairs={{0,16},{4,20},{8,24},{12,28},{16,0},{20,4},{24,8},{28,12},{1,17},{... | collective-permute-start | bytes 221192 | tf_op jit(solution)/shard_map/ppermute | solution.py:71
  50.6 4.7 %collective-permute-start.4 = (bf16[4,9,8,128]{3,2,1,0:T(8,128)(2,1)S(1)}, bf16[4,9,8,128]{3,2,1,0:T(8,128)(2,1)S(1)}, u32[]{:S(2)}, u32[]{:S(2)}) collective-permute-start(bf16[4,9,8,128]{3,2,1,0:T(8,128)(2,1)S(1)} %get-tuple-element.30), channel_id=1, source_target_pairs={{0,20},{4,16},{8,28},{12,24},{16,4},{20,0},{24,12},{28,8},{1,21},{... | collective-permute-start | bytes 221192 | tf_op jit(solution)/shard_map/ppermute | solution.py:71
  51.2 7.1 %collective-permute-start.5 = (bf16[4,9,8,128]{3,2,1,0:T(8,128)(2,1)S(1)}, bf16[4,9,8,128]{3,2,1,0:T(8,128)(2,1)S(1)}, u32[]{:S(2)}, u32[]{:S(2)}) collective-permute-start(bf16[4,9,8,128]{3,2,1,0:T(8,128)(2,1)S(1)} %get-tuple-element.31), channel_id=1, source_target_pairs={{0,24},{4,28},{8,16},{12,20},{16,8},{20,12},{24,0},{28,4},{1,25},{... | collective-permute-start | bytes 221192 | tf_op jit(solution)/shard_map/ppermute | solution.py:71
  54.0 5.5 %collective-permute-start.6 = (bf16[4,9,8,128]{3,2,1,0:T(8,128)(2,1)S(1)}, bf16[4,9,8,128]{3,2,1,0:T(8,128)(2,1)S(1)}, u32[]{:S(2)}, u32[]{:S(2)}) collective-permute-start(bf16[4,9,8,128]{3,2,1,0:T(8,128)(2,1)S(1)} %get-tuple-element.32), channel_id=1, source_target_pairs={{0,28},{4,24},{8,20},{12,16},{16,12},{20,8},{24,4},{28,0},{1,29},{... | collective-permute-start | bytes 221192 | tf_op jit(solution)/shard_map/ppermute | solution.py:71
  59.5 7.2 %collective-permute-start.7 = (bf16[8,9,8,128]{3,2,1,0:T(8,128)(2,1)S(1)}, bf16[8,9,8,128]{3,2,1,0:T(8,128)(2,1)S(1)}, u32[]{:S(2)}, u32[]{:S(2)}) collective-permute-start(bf16[8,9,8,128]{3,2,1,0:T(8,128)(2,1)S(1)} %get-tuple-element.34), channel_id=1, source_target_pairs={{0,1},{1,0},{2,3},{3,2},{4,5},{5,4},{6,7},{7,6},{8,9},{9,8},{10,11... | collective-permute-start | bytes 442376 | tf_op jit(solution)/shard_map/ppermute | solution.py:71
  61.9 13.3 %collective-permute-start.8 = (bf16[8,9,8,128]{3,2,1,0:T(8,128)(2,1)S(1)}, bf16[8,9,8,128]{3,2,1,0:T(8,128)(2,1)S(1)}, u32[]{:S(2)}, u32[]{:S(2)}) collective-permute-start(bf16[8,9,8,128]{3,2,1,0:T(8,128)(2,1)S(1)} %get-tuple-element.35), channel_id=1, source_target_pairs={{0,2},{1,3},{2,0},{3,1},{4,6},{5,7},{6,4},{7,5},{8,10},{9,11},{10,... | collective-permute-start | bytes 442376 | tf_op jit(solution)/shard_map/ppermute | solution.py:71
  62.6 12.6 %collective-permute-start.9 = (bf16[8,9,8,128]{3,2,1,0:T(8,128)(2,1)S(1)}, bf16[8,9,8,128]{3,2,1,0:T(8,128)(2,1)S(1)}, u32[]{:S(2)}, u32[]{:S(2)}) collective-permute-start(bf16[8,9,8,128]{3,2,1,0:T(8,128)(2,1)S(1)} %get-tuple-element.36), channel_id=1, source_target_pairs={{0,3},{1,2},{2,1},{3,0},{4,7},{5,6},{6,5},{7,4},{8,11},{9,10},{10,... | collective-permute-start | bytes 442376 | tf_op jit(solution)/shard_map/ppermute | solution.py:71
  79.2 3.6 %collective-permute-start.10 = (bf16[2,8,16,128]{3,2,1,0:T(8,128)(2,1)S(1)}, bf16[2,8,16,128]{3,2,1,0:T(8,128)(2,1)S(1)}, u32[]{:S(2)}, u32[]{:S(2)}) collective-permute-start(bf16[2,8,16,128]{3,2,1,0:T(8,128)(2,1)S(1)} %get-tuple-element.38), channel_id=1, source_target_pairs={{0,4},{4,0},{8,12},{12,8},{16,20},{20,16},{24,28},{28,24},{1,5},{5... | collective-permute-start | bytes 196616 | tf_op jit(solution)/shard_map/ppermute | solution.py:71
  79.3 5.1 %collective-permute-start.11 = (bf16[2,8,16,128]{3,2,1,0:T(8,128)(2,1)S(1)}, bf16[2,8,16,128]{3,2,1,0:T(8,128)(2,1)S(1)}, u32[]{:S(2)}, u32[]{:S(2)}) collective-permute-start(bf16[2,8,16,128]{3,2,1,0:T(8,128)(2,1)S(1)} %get-tuple-element.39), channel_id=1, source_target_pairs={{0,8},{4,12},{8,0},{12,4},{16,24},{20,28},{24,16},{28,20},{1,9},{5... | collective-permute-start | bytes 196616 | tf_op jit(solution)/shard_map/ppermute | solution.py:71
  79.7 7.9 %collective-permute-start.12 = (bf16[2,8,16,128]{3,2,1,0:T(8,128)(2,1)S(1)}, bf16[2,8,16,128]{3,2,1,0:T(8,128)(2,1)S(1)}, u32[]{:S(2)}, u32[]{:S(2)}) collective-permute-start(bf16[2,8,16,128]{3,2,1,0:T(8,128)(2,1)S(1)} %get-tuple-element.40), channel_id=1, source_target_pairs={{0,12},{4,8},{8,4},{12,0},{16,28},{20,24},{24,20},{28,16},{1,13},{... | collective-permute-start | bytes 196616 | tf_op jit(solution)/shard_map/ppermute | solution.py:71
  81.2 6.5 %collective-permute-start.13 = (bf16[2,8,16,128]{3,2,1,0:T(8,128)(2,1)S(1)}, bf16[2,8,16,128]{3,2,1,0:T(8,128)(2,1)S(1)}, u32[]{:S(2)}, u32[]{:S(2)}) collective-permute-start(bf16[2,8,16,128]{3,2,1,0:T(8,128)(2,1)S(1)} %get-tuple-element.41), channel_id=1, source_target_pairs={{0,16},{4,20},{8,24},{12,28},{16,0},{20,4},{24,8},{28,12},{1,17},{... | collective-permute-start | bytes 196616 | tf_op jit(solution)/shard_map/ppermute | solution.py:71
  82.7 5.0 %collective-permute-start.14 = (bf16[2,8,16,128]{3,2,1,0:T(8,128)(2,1)S(1)}, bf16[2,8,16,128]{3,2,1,0:T(8,128)(2,1)S(1)}, u32[]{:S(2)}, u32[]{:S(2)}) collective-permute-start(bf16[2,8,16,128]{3,2,1,0:T(8,128)(2,1)S(1)} %get-tuple-element.42), channel_id=1, source_target_pairs={{0,20},{4,16},{8,28},{12,24},{16,4},{20,0},{24,12},{28,8},{1,21},{... | collective-permute-start | bytes 196616 | tf_op jit(solution)/shard_map/ppermute | solution.py:71
  82.9 5.8 %collective-permute-start.15 = (bf16[2,8,16,128]{3,2,1,0:T(8,128)(2,1)S(1)}, bf16[2,8,16,128]{3,2,1,0:T(8,128)(2,1)S(1)}, u32[]{:S(2)}, u32[]{:S(2)}) collective-permute-start(bf16[2,8,16,128]{3,2,1,0:T(8,128)(2,1)S(1)} %get-tuple-element.43), channel_id=1, source_target_pairs={{0,24},{4,28},{8,16},{12,20},{16,8},{20,12},{24,0},{28,4},{1,25},{... | collective-permute-start | bytes 196616 | tf_op jit(solution)/shard_map/ppermute | solution.py:71
  84.4 5.3 %collective-permute-start.16 = (bf16[2,8,16,128]{3,2,1,0:T(8,128)(2,1)S(1)}, bf16[2,8,16,128]{3,2,1,0:T(8,128)(2,1)S(1)}, u32[]{:S(2)}, u32[]{:S(2)}) collective-permute-start(bf16[2,8,16,128]{3,2,1,0:T(8,128)(2,1)S(1)} %get-tuple-element.44), channel_id=1, source_target_pairs={{0,28},{4,24},{8,20},{12,16},{16,12},{20,8},{24,4},{28,0},{1,29},{... | collective-permute-start | bytes 196616 | tf_op jit(solution)/shard_map/ppermute | solution.py:71

commit v4 on v3

--- a/solution.py
+++ b/solution.py
@@ -272,32 +272,12 @@
     return jnp.concatenate(x, axis=0)
 
 
-def vorticity(plan, both, wall, place):
-    p = plan
-    inner, outer = slope_taps(p)
-
-    def body(place_ref, x, inner_ref, outer_ref, *rest):
-        arrived, (out, sides, slope, beside) = rest[: p.ta], rest[p.ta :]
-        for m in range(p.ta):
-            beside[m] = arrived[m][:, p.rg].astype(jnp.float32)
-
-        def side_of(b):
-            at = place_ref[1] ^ b if p.by_partner else b
-            return jnp.concatenate([beside[place_ref[0] ^ t, at] for t in range(p.ta)], axis=0)
-
-        chunk = place_ref[0] * p.blocks + place_ref[1]
-        first = (chunk == 0).astype(jnp.int32)
-        last = (chunk == p.chunks - 1).astype(jnp.int32)
+def inner_vorticity(plan, both):
+    p = plan
+    inner, _ = slope_taps(p)
+
+    def body(x, inner_ref, out):
         lane = lax.broadcasted_iota(jnp.int32, (p.nt, LANES), 1)
-        for a in range(p.gx):
-            for z in range(p.gz):
-                before = a * p.gz + lax.rem(z + p.gz - first, p.gz)
-                after = a * p.gz + lax.rem(z + last, p.gz)
-                left, right = side_of(before), side_of(after)
-                b = a * p.gz + z
-                side = jnp.where(lane % 4 < 2, left, right).astype(jnp.bfloat16)
-                sides[b * p.nt : (b + 1) * p.nt, :] = side
-        slope[...] = jnp.dot(sides[...], outer_ref[...], preferred_element_type=jnp.float32)
 
         def row_of(a, z, r):
             shift, r = divmod(r, p.rg)
@@ -318,21 +298,47 @@
                     across = 8.0 * (rows[r + 1] - rows[r - 1]) - (rows[r + 2] - rows[r - 2])
                     mine = series_of(x, b, p.rg + r).astype(jnp.bfloat16)
                     along = jnp.dot(mine, inner_ref[...], preferred_element_type=jnp.float32)
-                    along = along + slope[b * p.nt : (b + 1) * p.nt, r * LANES : (r + 1) * LANES]
-                    spin = (along - across) / 12.0
-                    for m in range(p.ta):
-                        out[b, m, r] = spin[m * p.tl : (m + 1) * p.tl].astype(jnp.bfloat16)
-
-    outs = pltpu.VMEM((p.blocks, p.ta, p.rg, p.tl, LANES), jnp.bfloat16)
+                    out[b, r] = along - across
+
+    outs = pltpu.VMEM((p.blocks, p.rg, p.nt, LANES), jnp.float32)
+    return on_chip(body, [both, inner], outs, [])
+
+
+def cross_spin_and(plan, base, wall, table, table_wall, owner, place, by_partner):
+    p = plan
+    _, outer = slope_taps(p)
+
+    def prepare(place_ref, outer_ref, arrived, sides, slope, beside):
+        chunk = place_ref[0] * p.blocks + place_ref[1]
+        first = (chunk == 0).astype(jnp.int32)
+        last = (chunk == p.chunks - 1).astype(jnp.int32)
+        is_left = (lax.broadcasted_iota(jnp.int32, (p.nt, LANES), 1) & 3) < 2
+        for m in range(p.ta):
+            beside[m] = arrived[m][:, p.rg].astype(jnp.float32)
+
+        def side_of(b):
+            at = place_ref[1] ^ b if p.by_partner else b
+            return jnp.concatenate([beside[place_ref[0] ^ t, at] for t in range(p.ta)], axis=0)
+
+        for a in range(p.gx):
+            for z in range(p.gz):
+                before = a * p.gz + lax.rem(z + p.gz - first, p.gz)
+                after = a * p.gz + lax.rem(z + last, p.gz)
+                b = a * p.gz + z
+                side = jnp.where(is_left, side_of(before), side_of(after))
+                sides[b * p.nt : (b + 1) * p.nt, :] = side.astype(jnp.bfloat16)
+        slope[...] = jnp.dot(sides[...], outer_ref[...], preferred_element_type=jnp.float32)
+
     scratch = [
         pltpu.VMEM((p.blocks * p.nt, LANES), jnp.bfloat16),
         pltpu.VMEM((p.blocks * p.nt, p.rg * LANES), jnp.float32),
         pltpu.VMEM((p.ta, p.blocks, p.tl, LANES), jnp.float32),
     ]
-    return on_chip(body, [both, inner, outer, *wall], outs, scratch, (place,))
-
-
-def cross(plan, jobs, owner, place, by_partner):
+    jobs = [(wall, 0, table_wall), ([base], 0, table)]
+    return cross(plan, jobs, owner, place, by_partner, (outer, prepare, scratch))
+
+
+def cross(plan, jobs, owner, place, by_partner, spin=None):
     p = plan
     scaling = 8.0 / (3.0 * SEG * NSEG)
     pair = 2 if p.rg % 2 == 0 else 1
@@ -346,39 +352,57 @@
         first = next(i for i, x in enumerate(inputs) if x is series[0])
         where.append((first, len(series), start, next(i for i, x in enumerate(inputs) if x is table)))
 
+    if spin is not None:
+        outer, prepare, more_scratch = spin
+        inputs.append(outer)
+
     def body(owner_ref, place_ref, *refs):
-        outs, (spec, ref_spec) = refs[len(inputs) : -2], refs[-2:]
+        outs = refs[len(inputs) : len(inputs) + n_outs]
+        if by_partner:
+            spec_0, spec_1, ref_0, ref_1 = refs[len(inputs) + n_outs :][:4]
+            turns = ((spec_0, ref_0), (spec_1, ref_1))
+        else:
+            specs, ref_specs = refs[len(inputs) + n_outs :][:2]
+            turns = tuple((specs.at[i], ref_specs.at[i]) for i in range(2))
+        more = refs[len(refs) - 3 :]
         turn = 0
         for q, (first, count, start, table) in enumerate(where):
+            whole = inputs[first].dtype == jnp.float32
+            if whole:
+                arrived = refs[where[0][0] : where[0][0] + where[0][1]]
+                prepare(place_ref, refs[len(inputs) - 1], arrived, *more)
             for r in range(0, p.rg, pair):
-                slot = turn % 2
+                spec, ref_spec = turns[turn % 2]
                 turn += 1
                 for n in range(p.blocks):
                     rows = []
                     for i in range(pair):
                         at = start + r + i
-                        if count > 1:
+                        if whole:
+                            slope = more[1][n * p.nt : (n + 1) * p.nt, at * LANES : (at + 1) * LANES]
+                            rows.append((refs[first][n, at] + slope) / 12.0)
+                        elif count > 1:
                             x = [refs[first + m][n, at].astype(jnp.float32) for m in range(count)]
                             rows.append(jnp.concatenate(x, axis=0))
                         else:
                             rows.append(series_of(refs[first], n, at))
                     b = place_ref[1] ^ n if count > 1 and p.by_partner else n
-                    spec[slot, b] = jnp.dot(
+                    spec[b] = jnp.dot(
                         refs[table][...],
                         jnp.concatenate(rows, axis=1).astype(jnp.bfloat16),
                         preferred_element_type=jnp.float32,
                     )
                 for s in range(NSEG):
                     at = s * ROWS
-                    ref_spec[slot, at : at + ROWS, :] = spec[slot, owner_ref[s], at : at + ROWS, :]
+                    ref_spec[at : at + ROWS, :] = spec[owner_ref[s], at : at + ROWS, :]
                 for n in range(p.blocks):
                     b = place_ref[1] ^ n if by_partner else n
                     co = jnp.zeros((8, width), jnp.float32)
                     quad = jnp.zeros((8, width), jnp.float32)
                     for s in range(NSEG):
                         at = s * ROWS
-                        rc, rs = ref_spec[slot, at : at + 8, :], ref_spec[slot, at + 8 : at + 16, :]
-                        qc, qs = spec[slot, b, at : at + 8, :], spec[slot, b, at + 8 : at + 16, :]
+                        rc, rs = ref_spec[at : at + 8, :], ref_spec[at + 8 : at + 16, :]
+                        qc, qs = spec[b, at : at + 8, :], spec[b, at + 8 : at + 16, :]
                         co = co + (rc * qc + rs * qs)
                         quad = quad + (rc * qs - rs * qc)
                     both = (jnp.concatenate([co, quad], axis=0) * scaling).astype(jnp.bfloat16)
@@ -394,10 +418,13 @@
         outs = [pltpu.VMEM(shape, jnp.bfloat16) for _ in range(p.blocks)]
     else:
         outs = [pltpu.VMEM((p.blocks,) + shape, jnp.bfloat16)]
-    scratch = [
-        pltpu.VMEM((2, p.blocks, NSEG * ROWS, width), jnp.float32),
-        pltpu.VMEM((2, NSEG * ROWS, width), jnp.float32),
-    ]
+    n_outs = len(outs)
+    spec_shape, ref_shape = (p.blocks, NSEG * ROWS, width), (NSEG * ROWS, width)
+    if by_partner:
+        scratch = [pltpu.VMEM(x, jnp.float32) for x in (spec_shape, spec_shape, ref_shape, ref_shape)]
+    else:
+        scratch = [pltpu.VMEM((2,) + x, jnp.float32) for x in (spec_shape, ref_shape)]
+    scratch += more_scratch if spin is not None else []
     return on_chip(body, inputs, outs, scratch, (owner, place))
 
 
@@ -480,7 +507,8 @@
     def over_blocks(arrays):
         if len(arrays) == 1:
             return [lax.all_to_all(arrays[0], block_axes, split_axis=0, concat_axis=0, tiled=True)]
-        return [arrays[0]] + [trade(arrays[n], block_axes, n, plan.blocks) for n in range(1, plan.blocks)]
+        traded = {n: trade(arrays[n], block_axes, n, plan.blocks) for n in range(1, plan.blocks)}
+        return [arrays[0]] + [traded[n] for n in range(1, plan.blocks)]
 
     wall = pack_one(plan, velocity, 1, packed, place)
     wall = over_blocks(wall)
@@ -493,11 +521,11 @@
     table = dft_rows(offsets, (turn * plan.tl + times).reshape(-1))
     early = cross(plan, [([both], 0, table), ([both], plan.rg, table)], owner, place, False)
     early = over_blocks(early)
-    spin = vorticity(plan, both, wall, place)
-    late = cross(plan, [([spin], 0, table), (wall, 0, table_wall)], owner, place, plan.by_partner)
+    base = inner_vorticity(plan, both)
+    late = cross_spin_and(plan, base, wall, table, table_wall, owner, place, plan.by_partner)
     late = over_blocks(late)
     out = assemble(plan, None, (2, 0), early, place)
-    return assemble(plan, out, (3, 1), late, place)
+    return assemble(plan, out, (1, 3), late, place)
 
 
 def solution(mesh):

time: 92.3 us -> 90.9 us (0.985)
  transfers between devices with their start and end apart: 19 -> 19, of which waited for: 10 -> 10; matrix products, arithmetic and copies ran while one was open for 1% -> 1% of each run, Pallas kernels for 11% -> 10%
where the time goes in v4:
time: 90.9 us; the launch traced here: 90.3 us
  waiting for transfers between devices  41.9 us (46%)
  starting transfers between devices  29.6 us (33%)
  Pallas kernels  17.5 us (19%)
    all_to_all x1, waiting for transfers between devices, shards(): lax.all_to_all(both, block_axes + ('ta',), split_axis=0, concat_axis=0, t...  23.8 us
    ppermute x17, starting transfers between devices, trade(): return lax.ppermute(x, axis, [(i, i ^ step) for i in range(count)])  18.2 us
    ppermute x17, waiting for transfers between devices, trade(): return lax.ppermute(x, axis, [(i, i ^ step) for i in range(count)])  18.1 us
    pallas_call x8, Pallas kernels, on_chip(): pl.pallas_call(body, in_specs=[smem] * len(scalars) + [vmem] * count + [h...  17.5 us
    all_to_all x1, starting transfers between devices, shards(): lax.all_to_all(both, block_axes + ('ta',), split_axis=0, concat_axis=0, t...  7.33 us
    all_to_all x1, starting transfers between devices, over_blocks(): lax.all_to_all(arrays[0], block_axes, split_axis=0, concat_axis=0, tiled=...  4.04 us
  transfers between devices with their start and end apart: 19, of which 10 were waited for; matrix products, arithmetic and copies ran while one was open for 1% of the time, Pallas kernels for 10%

profile of v4, /device:TPU:0, one launch (start us, length us, event | category | flops | bytes accessed | tf_op | source)
XLA Modules:
  0.0 90.3 jit_solution(7205500370984949886)
XLA Ops:
  0.0 3.6 %shard_map.100.packed_ref = bf16[8,4,16,8,128]{4,3,2,1,0:T(8,128)(2,1)} custom-call(bf16[512,512]{1,0:T(8,128)(2,1)} %constant.58.clone.swap_hbm.swap.refs_1_.refs_8_, bf16[3,8,32,1024]{3,2,1,0:T(8,128)(2,1)} %velocity_ref.3), custom_call_target="tpu_custom_call" | custom-call | tf_op jit(solution)/shard_map/pallas_call | solution.py:46
  3.6 7.3 %all-to-all-start = ((bf16[32,16,8,128]{3,2,1,0:T(8,128)(2,1)}), bf16[32,16,8,128]{3,2,1,0:T(8,128)(2,1)S(1)}, u32[]{:S(2)}, u32[]{:S(2)}) async-start(bf16[32,16,8,128]{3,2,1,0:T(8,128)(2,1)} %bitcast.3), calls=%async_computation | async-start | bytes 2097152 | tf_op jit(solution)/shard_map/all_to_all | solution.py:504
  12.0 23.8 %all-to-all-done = bf16[32,16,8,128]{3,2,1,0:T(8,128)(2,1)S(1)} async-done(((bf16[32,16,8,128]{3,2,1,0:T(8,128)(2,1)}), bf16[32,16,8,128]{3,2,1,0:T(8,128)(2,1)S(1)}, u32[]{:S(2)}, u32[]{:S(2)}) %all-to-all-start) | async-done | bytes 1048608 | tf_op jit(solution)/shard_map/all_to_all | solution.py:504
  35.9 3.1 %shard_map.105 = bf16[8,2,8,16,128]{4,3,2,1,0:T(8,128)(2,1)} custom-call(s32[7]{0:T(128)S(1)} %copy-done.4, s32[2]{0:T(128)S(1)} %pad_add_fusion.place_ref, bf16[8,4,16,8,128]{4,3,2,1,0:T(8,128)(2,1)S(1)} %bitcast.6, bf16[112,32]{1,0:T(8,128)(2,1)S(1)} %bitcast.8), custom_call_target="tpu_custom_call" | custom-call | tf_op jit(solution)/shard_map/pallas_call | solution.py:46
  39.0 4.0 %all-to-all-start.1 = ((bf16[8,2,8,16,128]{4,3,2,1,0:T(8,128)(2,1)}), bf16[8,2,8,16,128]{4,3,2,1,0:T(8,128)(2,1)S(1)}, u32[]{:S(2)}, u32[]{:S(2)}) async-start(bf16[8,2,8,16,128]{4,3,2,1,0:T(8,128)(2,1)} %shard_map.105), calls=%async_computation.1 | async-start | bytes 1048576 | tf_op jit(solution)/shard_map/all_to_all | solution.py:509
  43.0 3.5 %shard_map.101 = (bf16[4,9,8,128]{3,2,1,0:T(8,128)(2,1)S(1)}, bf16[4,9,8,128]{3,2,1,0:T(8,128)(2,1)S(1)}, bf16[4,9,8,128]{3,2,1,0:T(8,128)(2,1)S(1)}, bf16[4,9,8...) custom-call(s32[2]{0:T(128)S(1)} %pad_add_fusion.place_ref, ...), custom_call_target="tpu_custom_call" | custom-call | tf_op jit(solution)/shard_map/pallas_call | solution.py:46
  46.5 1.2 %collective-permute-start = (bf16[4,9,8,128]{3,2,1,0:T(8,128)(2,1)S(1)}, bf16[4,9,8,128]{3,2,1,0:T(8,128)(2,1)S(1)}, u32[]{:S(2)}, u32[]{:S(2)}) collective-permute-start(bf16[4,9,8,128]{3,2,1,0:T(8,128)(2,1)S(1)} %get-tuple-element.26), channel_id=1, source_target_pairs={{0,4},{4,0},{8,12},{12,8},{16,20},{20,16},{24,28},{28,24},{1,5},{5... | collective-permute-start | bytes 221192 | tf_op jit(solution)/shard_map/ppermute | solution.py:71
  47.7 1.4 %collective-permute-start.1 = (bf16[4,9,8,128]{3,2,1,0:T(8,128)(2,1)S(1)}, bf16[4,9,8,128]{3,2,1,0:T(8,128)(2,1)S(1)}, u32[]{:S(2)}, u32[]{:S(2)}) collective-permute-start(bf16[4,9,8,128]{3,2,1,0:T(8,128)(2,1)S(1)} %get-tuple-element.27), channel_id=1, source_target_pairs={{0,8},{4,12},{8,0},{12,4},{16,24},{20,28},{24,16},{28,20},{1,9},{5... | collective-permute-start | bytes 221192 | tf_op jit(solution)/shard_map/ppermute | solution.py:71
  49.1 1.5 %collective-permute-start.3 = (bf16[4,9,8,128]{3,2,1,0:T(8,128)(2,1)S(1)}, bf16[4,9,8,128]{3,2,1,0:T(8,128)(2,1)S(1)}, u32[]{:S(2)}, u32[]{:S(2)}) collective-permute-start(bf16[4,9,8,128]{3,2,1,0:T(8,128)(2,1)S(1)} %get-tuple-element.29), channel_id=1, source_target_pairs={{0,16},{4,20},{8,24},{12,28},{16,0},{20,4},{24,8},{28,12},{1,17},{... | collective-permute-start | bytes 221192 | tf_op jit(solution)/shard_map/ppermute | solution.py:71
  50.6 0.6 collective-permute-start.4
  51.2 1.9 %collective-permute-start.5 = (bf16[4,9,8,128]{3,2,1,0:T(8,128)(2,1)S(1)}, bf16[4,9,8,128]{3,2,1,0:T(8,128)(2,1)S(1)}, u32[]{:S(2)}, u32[]{:S(2)}) collective-permute-start(bf16[4,9,8,128]{3,2,1,0:T(8,128)(2,1)S(1)} %get-tuple-element.31), channel_id=1, source_target_pairs={{0,24},{4,28},{8,16},{12,20},{16,8},{20,12},{24,0},{28,4},{1,25},{... | collective-permute-start | bytes 221192 | tf_op jit(solution)/shard_map/ppermute | solution.py:71
  53.1 0.8 collective-permute-done.1.refs_2_
  54.0 0.6 collective-permute-start.6
  54.5 0.6 collective-permute-done.2.refs_3_
  55.3 2.9 %collective-permute-done.5.refs_6_ = bf16[4,9,8,128]{3,2,1,0:T(8,128)(2,1)S(1)} collective-permute-done((bf16[4,9,8,128]{3,2,1,0:T(8,128)(2,1)S(1)}, bf16[4,9,8,128]{3,2,1,0:T(8,128)(2,1)S(1)}, u32[]{:S(2)}, u32[]{:S(2)}) %collective-permute-start.5) | collective-permute-done | bytes 73760 | tf_op jit(solution)/shard_map/ppermute | solution.py:71
  58.2 1.2 %collective-permute-done.6.refs_7_ = bf16[4,9,8,128]{3,2,1,0:T(8,128)(2,1)S(1)} collective-permute-done((bf16[4,9,8,128]{3,2,1,0:T(8,128)(2,1)S(1)}, bf16[4,9,8,128]{3,2,1,0:T(8,128)(2,1)S(1)}, u32[]{:S(2)}, u32[]{:S(2)}) %collective-permute-start.6) | collective-permute-done | bytes 73760 | tf_op jit(solution)/shard_map/ppermute | solution.py:71
  59.5 2.3 %collective-permute-start.7 = (bf16[8,9,8,128]{3,2,1,0:T(8,128)(2,1)S(1)}, bf16[8,9,8,128]{3,2,1,0:T(8,128)(2,1)S(1)}, u32[]{:S(2)}, u32[]{:S(2)}) collective-permute-start(bf16[8,9,8,128]{3,2,1,0:T(8,128)(2,1)S(1)} %get-tuple-element.34), channel_id=1, source_target_pairs={{0,1},{1,0},{2,3},{3,2},{4,5},{5,4},{6,7},{7,6},{8,9},{9,8},{10,11... | collective-permute-start | bytes 442376 | tf_op jit(solution)/shard_map/ppermute | solution.py:71
  61.8 0.7 collective-permute-start.8
  62.6 1.7 %collective-permute-start.9 = (bf16[8,9,8,128]{3,2,1,0:T(8,128)(2,1)S(1)}, bf16[8,9,8,128]{3,2,1,0:T(8,128)(2,1)S(1)}, u32[]{:S(2)}, u32[]{:S(2)}) collective-permute-start(bf16[8,9,8,128]{3,2,1,0:T(8,128)(2,1)S(1)} %get-tuple-element.36), channel_id=1, source_target_pairs={{0,3},{1,2},{2,1},{3,0},{4,7},{5,6},{6,5},{7,4},{8,11},{9,10},{10,... | collective-permute-start | bytes 442376 | tf_op jit(solution)/shard_map/ppermute | solution.py:71
  64.3 0.7 shard_map.103.refs_5_
  64.9 1.7 %collective-permute-done.7.refs_1_ = bf16[8,9,8,128]{3,2,1,0:T(8,128)(2,1)S(1)} collective-permute-done((bf16[8,9,8,128]{3,2,1,0:T(8,128)(2,1)S(1)}, bf16[8,9,8,128]{3,2,1,0:T(8,128)(2,1)S(1)}, u32[]{:S(2)}, u32[]{:S(2)}) %collective-permute-start.7) | collective-permute-done | bytes 147488 | tf_op jit(solution)/shard_map/ppermute | solution.py:71
  66.6 8.5 %collective-permute-done.8.refs_2_ = bf16[8,9,8,128]{3,2,1,0:T(8,128)(2,1)S(1)} collective-permute-done((bf16[8,9,8,128]{3,2,1,0:T(8,128)(2,1)S(1)}, bf16[8,9,8,128]{3,2,1,0:T(8,128)(2,1)S(1)}, u32[]{:S(2)}, u32[]{:S(2)}) %collective-permute-start.8) | collective-permute-done | bytes 147488 | tf_op jit(solution)/shard_map/ppermute | solution.py:71
  75.1 2.6 %shard_map.104 = (bf16[2,8,16,128]{3,2,1,0:T(8,128)(2,1)S(1)}, bf16[2,8,16,128]{3,2,1,0:T(8,128)(2,1)S(1)}, bf16[2,8,16,128]{3,2,1,0:T(8,128)(2,1)S(1)}, bf16[2,...) custom-call(s32[7]{0:T(128)S(1)} %copy-done.4, ...), custom_call_target="tpu_custom_call" | custom-call | tf_op jit(solution)/shard_map/pallas_call | solution.py:46
  77.8 0.4 collective-permute-start.11
  78.3 1.4 %collective-permute-start.12 = (bf16[2,8,16,128]{3,2,1,0:T(8,128)(2,1)S(1)}, bf16[2,8,16,128]{3,2,1,0:T(8,128)(2,1)S(1)}, u32[]{:S(2)}, u32[]{:S(2)}) collective-permute-start(bf16[2,8,16,128]{3,2,1,0:T(8,128)(2,1)S(1)} %get-tuple-element.40), channel_id=1, source_target_pairs={{0,12},{4,8},{8,4},{12,0},{16,28},{20,24},{24,20},{28,16},{1,13},{... | collective-permute-start | bytes 196616 | tf_op jit(solution)/shard_map/ppermute | solution.py:71
  79.7 1.5 %collective-permute-start.13 = (bf16[2,8,16,128]{3,2,1,0:T(8,128)(2,1)S(1)}, bf16[2,8,16,128]{3,2,1,0:T(8,128)(2,1)S(1)}, u32[]{:S(2)}, u32[]{:S(2)}) collective-permute-start(bf16[2,8,16,128]{3,2,1,0:T(8,128)(2,1)S(1)} %get-tuple-element.41), channel_id=1, source_target_pairs={{0,16},{4,20},{8,24},{12,28},{16,0},{20,4},{24,8},{28,12},{1,17},{... | collective-permute-start | bytes 196616 | tf_op jit(solution)/shard_map/ppermute | solution.py:71
  81.4 1.6 %collective-permute-start.15 = (bf16[2,8,16,128]{3,2,1,0:T(8,128)(2,1)S(1)}, bf16[2,8,16,128]{3,2,1,0:T(8,128)(2,1)S(1)}, u32[]{:S(2)}, u32[]{:S(2)}) collective-permute-start(bf16[2,8,16,128]{3,2,1,0:T(8,128)(2,1)S(1)} %get-tuple-element.43), channel_id=1, source_target_pairs={{0,24},{4,28},{8,16},{12,20},{16,8},{20,12},{24,0},{28,4},{1,25},{... | collective-permute-start | bytes 196616 | tf_op jit(solution)/shard_map/ppermute | solution.py:71
  83.0 1.1 %collective-permute-start.16 = (bf16[2,8,16,128]{3,2,1,0:T(8,128)(2,1)S(1)}, bf16[2,8,16,128]{3,2,1,0:T(8,128)(2,1)S(1)}, u32[]{:S(2)}, u32[]{:S(2)}) collective-permute-start(bf16[2,8,16,128]{3,2,1,0:T(8,128)(2,1)S(1)} %get-tuple-element.44), channel_id=1, source_target_pairs={{0,28},{4,24},{8,20},{12,16},{16,12},{20,8},{24,4},{28,0},{1,29},{... | collective-permute-start | bytes 196616 | tf_op jit(solution)/shard_map/ppermute | solution.py:71
  84.1 2.1 %shard_map.106.refs_9_ = f32[4,2,7,32,256]{4,3,2,1,0:T(8,128)} custom-call(s32[2]{0:T(128)S(1)} %pad_add_fusion.place_ref, bf16[8,2,8,16,128]{4,3,2,1,0:T(8,128)(2,1)S(1)} %all-to-all-done.1.refs_0_, bf16[512,512]{1,0:T(8,128)(2,1)S(1)} %copy-done), custom_call_target="tpu_custom_call" | custom-call | tf_op jit(solution)/shard_map/pallas_call | solution.py:46
  86.2 1.1 %collective-permute-done.15.refs_6_ = bf16[2,8,16,128]{3,2,1,0:T(8,128)(2,1)S(1)} collective-permute-done((bf16[2,8,16,128]{3,2,1,0:T(8,128)(2,1)S(1)}, bf16[2,8,16,128]{3,2,1,0:T(8,128)(2,1)S(1)}, u32[]{:S(2)}, u32[]{:S(2)}) %collective-permute-start.15) | collective-permute-done | bytes 65568 | tf_op jit(solution)/shard_map/ppermute | solution.py:71
  87.3 1.0 %collective-permute-done.16.refs_7_ = bf16[2,8,16,128]{3,2,1,0:T(8,128)(2,1)S(1)} collective-permute-done((bf16[2,8,16,128]{3,2,1,0:T(8,128)(2,1)S(1)}, bf16[2,8,16,128]{3,2,1,0:T(8,128)(2,1)S(1)}, u32[]{:S(2)}, u32[]{:S(2)}) %collective-permute-start.16) | collective-permute-done | bytes 65568 | tf_op jit(solution)/shard_map/ppermute | solution.py:71
  88.3 2.0 %shard_map.107 = f32[4,2,7,32,256]{4,3,2,1,0:T(8,128)} custom-call(s32[2]{0:T(128)S(1)} %pad_add_fusion.place_ref, bf16[2,8,16,128]{3,2,1,0:T(8,128)(2,1)S(1)} %get-tuple-element.37.refs_0_, bf16[2,8,16,128]{3,2,1,0:T(8,128)(2,1)S(1)} %collective-permute-done.10.refs_1_, ...), custom_call_target="tpu_custom_call", output_to_operand_aliasing={{}: (10, {})} | custom-call | tf_op jit(solution)/shard_map/pallas_call | solution.py:46
  (40 shorter events, 1.6 us)
Async XLA Ops:
  3.6 7.8 %copy-start.5 = (s32[7]{0:T(128)S(1)}, s32[7]{0:T(128)}, u32[]{:S(2)}) copy-start(s32[7]{0:T(128)} %param.11) | copy-start | bytes 88
  3.6 32.3 %copy-start.4 = (s32[7]{0:T(128)S(1)}, s32[7]{0:T(128)}, u32[]{:S(2)}) copy-start(s32[7]{0:T(128)} %owner_ref.3) | copy-start | bytes 88
  3.6 32.3 %all-to-all-start = ((bf16[32,16,8,128]{3,2,1,0:T(8,128)(2,1)}), bf16[32,16,8,128]{3,2,1,0:T(8,128)(2,1)S(1)}, u32[]{:S(2)}, u32[]{:S(2)}) async-start(bf16[32,16,8,128]{3,2,1,0:T(8,128)(2,1)} %bitcast.3), calls=%async_computation | async-start | bytes 2097152 | tf_op jit(solution)/shard_map/all_to_all | solution.py:504
  11.0 32.1 %copy-start = (bf16[512,512]{1,0:T(8,128)(2,1)S(1)}, bf16[512,512]{1,0:T(8,128)(2,1)}, u32[]{:S(2)}) copy-start(bf16[512,512]{1,0:T(8,128)(2,1)} %constant.58.clone.swap_hbm.swap.refs_1_.refs_8_) | copy-start | bytes 1572868
  11.0 32.1 %copy-start.1 = (bf16[1024,256]{1,0:T(8,128)(2,1)S(1)}, bf16[1024,256]{1,0:T(8,128)(2,1)}, u32[]{:S(2)}) copy-start(bf16[1024,256]{1,0:T(8,128)(2,1)} %constant.59.clone.picks) | copy-start | bytes 1572868
  39.0 45.1 %all-to-all-start.1 = ((bf16[8,2,8,16,128]{4,3,2,1,0:T(8,128)(2,1)}), bf16[8,2,8,16,128]{4,3,2,1,0:T(8,128)(2,1)S(1)}, u32[]{:S(2)}, u32[]{:S(2)}) async-start(bf16[8,2,8,16,128]{4,3,2,1,0:T(8,128)(2,1)} %shard_map.105), calls=%async_computation.1 | async-start | bytes 1048576 | tf_op jit(solution)/shard_map/all_to_all | solution.py:509
  43.0 21.2 %copy-start.3 = (bf16[128,128]{1,0:T(8,128)(2,1)S(1)}, bf16[128,128]{1,0:T(8,128)(2,1)}, u32[]{:S(2)}) copy-start(bf16[128,128]{1,0:T(8,128)(2,1)} %constant.60.clone.inner_ref) | copy-start | bytes 98308
  46.5 28.6 %copy-start.2 = (bf16[128,1024]{1,0:T(8,128)(2,1)S(1)}, bf16[128,1024]{1,0:T(8,128)(2,1)}, u32[]{:S(2)}) copy-start(bf16[128,1024]{1,0:T(8,128)(2,1)} %constant.61.clone.refs_7_) | copy-start | bytes 786436
  46.5 4.7 %collective-permute-start = (bf16[4,9,8,128]{3,2,1,0:T(8,128)(2,1)S(1)}, bf16[4,9,8,128]{3,2,1,0:T(8,128)(2,1)S(1)}, u32[]{:S(2)}, u32[]{:S(2)}) collective-permute-start(bf16[4,9,8,128]{3,2,1,0:T(8,128)(2,1)S(1)} %get-tuple-element.26), channel_id=1, source_target_pairs={{0,4},{4,0},{8,12},{12,8},{16,20},{20,16},{24,28},{28,24},{1,5},{5... | collective-permute-start | bytes 221192 | tf_op jit(solution)/shard_map/ppermute | solution.py:71
  47.7 6.3 %collective-permute-start.1 = (bf16[4,9,8,128]{3,2,1,0:T(8,128)(2,1)S(1)}, bf16[4,9,8,128]{3,2,1,0:T(8,128)(2,1)S(1)}, u32[]{:S(2)}, u32[]{:S(2)}) collective-permute-start(bf16[4,9,8,128]{3,2,1,0:T(8,128)(2,1)S(1)} %get-tuple-element.27), channel_id=1, source_target_pairs={{0,8},{4,12},{8,0},{12,4},{16,24},{20,28},{24,16},{28,20},{1,9},{5... | collective-permute-start | bytes 221192 | tf_op jit(solution)/shard_map/ppermute | solution.py:71
  49.1 6.0 %collective-permute-start.2 = (bf16[4,9,8,128]{3,2,1,0:T(8,128)(2,1)S(1)}, bf16[4,9,8,128]{3,2,1,0:T(8,128)(2,1)S(1)}, u32[]{:S(2)}, u32[]{:S(2)}) collective-permute-start(bf16[4,9,8,128]{3,2,1,0:T(8,128)(2,1)S(1)} %get-tuple-element.28), channel_id=1, source_target_pairs={{0,12},{4,8},{8,4},{12,0},{16,28},{20,24},{24,20},{28,16},{1,13},{... | collective-permute-start | bytes 221192 | tf_op jit(solution)/shard_map/ppermute | solution.py:71
  49.1 6.0 %collective-permute-start.3 = (bf16[4,9,8,128]{3,2,1,0:T(8,128)(2,1)S(1)}, bf16[4,9,8,128]{3,2,1,0:T(8,128)(2,1)S(1)}, u32[]{:S(2)}, u32[]{:S(2)}) collective-permute-start(bf16[4,9,8,128]{3,2,1,0:T(8,128)(2,1)S(1)} %get-tuple-element.29), channel_id=1, source_target_pairs={{0,16},{4,20},{8,24},{12,28},{16,0},{20,4},{24,8},{28,12},{1,17},{... | collective-permute-start | bytes 221192 | tf_op jit(solution)/shard_map/ppermute | solution.py:71
  50.6 4.7 %collective-permute-start.4 = (bf16[4,9,8,128]{3,2,1,0:T(8,128)(2,1)S(1)}, bf16[4,9,8,128]{3,2,1,0:T(8,128)(2,1)S(1)}, u32[]{:S(2)}, u32[]{:S(2)}) collective-permute-start(bf16[4,9,8,128]{3,2,1,0:T(8,128)(2,1)S(1)} %get-tuple-element.30), channel_id=1, source_target_pairs={{0,20},{4,16},{8,28},{12,24},{16,4},{20,0},{24,12},{28,8},{1,21},{... | collective-permute-start | bytes 221192 | tf_op jit(solution)/shard_map/ppermute | solution.py:71
  51.2 7.0 %collective-permute-start.5 = (bf16[4,9,8,128]{3,2,1,0:T(8,128)(2,1)S(1)}, bf16[4,9,8,128]{3,2,1,0:T(8,128)(2,1)S(1)}, u32[]{:S(2)}, u32[]{:S(2)}) collective-permute-start(bf16[4,9,8,128]{3,2,1,0:T(8,128)(2,1)S(1)} %get-tuple-element.31), channel_id=1, source_target_pairs={{0,24},{4,28},{8,16},{12,20},{16,8},{20,12},{24,0},{28,4},{1,25},{... | collective-permute-start | bytes 221192 | tf_op jit(solution)/shard_map/ppermute | solution.py:71
  54.0 5.5 %collective-permute-start.6 = (bf16[4,9,8,128]{3,2,1,0:T(8,128)(2,1)S(1)}, bf16[4,9,8,128]{3,2,1,0:T(8,128)(2,1)S(1)}, u32[]{:S(2)}, u32[]{:S(2)}) collective-permute-start(bf16[4,9,8,128]{3,2,1,0:T(8,128)(2,1)S(1)} %get-tuple-element.32), channel_id=1, source_target_pairs={{0,28},{4,24},{8,20},{12,16},{16,12},{20,8},{24,4},{28,0},{1,29},{... | collective-permute-start | bytes 221192 | tf_op jit(solution)/shard_map/ppermute | solution.py:71
  59.5 7.1 %collective-permute-start.7 = (bf16[8,9,8,128]{3,2,1,0:T(8,128)(2,1)S(1)}, bf16[8,9,8,128]{3,2,1,0:T(8,128)(2,1)S(1)}, u32[]{:S(2)}, u32[]{:S(2)}) collective-permute-start(bf16[8,9,8,128]{3,2,1,0:T(8,128)(2,1)S(1)} %get-tuple-element.34), channel_id=1, source_target_pairs={{0,1},{1,0},{2,3},{3,2},{4,5},{5,4},{6,7},{7,6},{8,9},{9,8},{10,11... | collective-permute-start | bytes 442376 | tf_op jit(solution)/shard_map/ppermute | solution.py:71
  61.8 13.3 %collective-permute-start.8 = (bf16[8,9,8,128]{3,2,1,0:T(8,128)(2,1)S(1)}, bf16[8,9,8,128]{3,2,1,0:T(8,128)(2,1)S(1)}, u32[]{:S(2)}, u32[]{:S(2)}) collective-permute-start(bf16[8,9,8,128]{3,2,1,0:T(8,128)(2,1)S(1)} %get-tuple-element.35), channel_id=1, source_target_pairs={{0,2},{1,3},{2,0},{3,1},{4,6},{5,7},{6,4},{7,5},{8,10},{9,11},{10,... | collective-permute-start | bytes 442376 | tf_op jit(solution)/shard_map/ppermute | solution.py:71
  62.6 12.6 %collective-permute-start.9 = (bf16[8,9,8,128]{3,2,1,0:T(8,128)(2,1)S(1)}, bf16[8,9,8,128]{3,2,1,0:T(8,128)(2,1)S(1)}, u32[]{:S(2)}, u32[]{:S(2)}) collective-permute-start(bf16[8,9,8,128]{3,2,1,0:T(8,128)(2,1)S(1)} %get-tuple-element.36), channel_id=1, source_target_pairs={{0,3},{1,2},{2,1},{3,0},{4,7},{5,6},{6,5},{7,4},{8,11},{9,10},{10,... | collective-permute-start | bytes 442376 | tf_op jit(solution)/shard_map/ppermute | solution.py:71
  77.7 3.6 %collective-permute-start.10 = (bf16[2,8,16,128]{3,2,1,0:T(8,128)(2,1)S(1)}, bf16[2,8,16,128]{3,2,1,0:T(8,128)(2,1)S(1)}, u32[]{:S(2)}, u32[]{:S(2)}) collective-permute-start(bf16[2,8,16,128]{3,2,1,0:T(8,128)(2,1)S(1)} %get-tuple-element.38), channel_id=1, source_target_pairs={{0,4},{4,0},{8,12},{12,8},{16,20},{20,16},{24,28},{28,24},{1,5},{5... | collective-permute-start | bytes 196616 | tf_op jit(solution)/shard_map/ppermute | solution.py:71
  77.8 5.2 %collective-permute-start.11 = (bf16[2,8,16,128]{3,2,1,0:T(8,128)(2,1)S(1)}, bf16[2,8,16,128]{3,2,1,0:T(8,128)(2,1)S(1)}, u32[]{:S(2)}, u32[]{:S(2)}) collective-permute-start(bf16[2,8,16,128]{3,2,1,0:T(8,128)(2,1)S(1)} %get-tuple-element.39), channel_id=1, source_target_pairs={{0,8},{4,12},{8,0},{12,4},{16,24},{20,28},{24,16},{28,20},{1,9},{5... | collective-permute-start | bytes 196616 | tf_op jit(solution)/shard_map/ppermute | solution.py:71
  78.3 7.9 %collective-permute-start.12 = (bf16[2,8,16,128]{3,2,1,0:T(8,128)(2,1)S(1)}, bf16[2,8,16,128]{3,2,1,0:T(8,128)(2,1)S(1)}, u32[]{:S(2)}, u32[]{:S(2)}) collective-permute-start(bf16[2,8,16,128]{3,2,1,0:T(8,128)(2,1)S(1)} %get-tuple-element.40), channel_id=1, source_target_pairs={{0,12},{4,8},{8,4},{12,0},{16,28},{20,24},{24,20},{28,16},{1,13},{... | collective-permute-start | bytes 196616 | tf_op jit(solution)/shard_map/ppermute | solution.py:71
  79.7 6.5 %collective-permute-start.13 = (bf16[2,8,16,128]{3,2,1,0:T(8,128)(2,1)S(1)}, bf16[2,8,16,128]{3,2,1,0:T(8,128)(2,1)S(1)}, u32[]{:S(2)}, u32[]{:S(2)}) collective-permute-start(bf16[2,8,16,128]{3,2,1,0:T(8,128)(2,1)S(1)} %get-tuple-element.41), channel_id=1, source_target_pairs={{0,16},{4,20},{8,24},{12,28},{16,0},{20,4},{24,8},{28,12},{1,17},{... | collective-permute-start | bytes 196616 | tf_op jit(solution)/shard_map/ppermute | solution.py:71
  81.2 5.0 %collective-permute-start.14 = (bf16[2,8,16,128]{3,2,1,0:T(8,128)(2,1)S(1)}, bf16[2,8,16,128]{3,2,1,0:T(8,128)(2,1)S(1)}, u32[]{:S(2)}, u32[]{:S(2)}) collective-permute-start(bf16[2,8,16,128]{3,2,1,0:T(8,128)(2,1)S(1)} %get-tuple-element.42), channel_id=1, source_target_pairs={{0,20},{4,16},{8,28},{12,24},{16,4},{20,0},{24,12},{28,8},{1,21},{... | collective-permute-start | bytes 196616 | tf_op jit(solution)/shard_map/ppermute | solution.py:71
  81.4 5.9 %collective-permute-start.15 = (bf16[2,8,16,128]{3,2,1,0:T(8,128)(2,1)S(1)}, bf16[2,8,16,128]{3,2,1,0:T(8,128)(2,1)S(1)}, u32[]{:S(2)}, u32[]{:S(2)}) collective-permute-start(bf16[2,8,16,128]{3,2,1,0:T(8,128)(2,1)S(1)} %get-tuple-element.43), channel_id=1, source_target_pairs={{0,24},{4,28},{8,16},{12,20},{16,8},{20,12},{24,0},{28,4},{1,25},{... | collective-permute-start | bytes 196616 | tf_op jit(solution)/shard_map/ppermute | solution.py:71
  83.0 5.3 %collective-permute-start.16 = (bf16[2,8,16,128]{3,2,1,0:T(8,128)(2,1)S(1)}, bf16[2,8,16,128]{3,2,1,0:T(8,128)(2,1)S(1)}, u32[]{:S(2)}, u32[]{:S(2)}) collective-permute-start(bf16[2,8,16,128]{3,2,1,0:T(8,128)(2,1)S(1)} %get-tuple-element.44), channel_id=1, source_target_pairs={{0,28},{4,24},{8,20},{12,16},{16,12},{20,8},{24,4},{28,0},{1,29},{... | collective-permute-start | bytes 196616 | tf_op jit(solution)/shard_map/ppermute | solution.py:71

commit v5 on v4

--- a/solution.py
+++ b/solution.py
@@ -203,43 +203,37 @@
             out.append(x.transpose(4, 3, 2, 0, 1, 5).reshape(p.blocks, p.ta, p.rg, p.tl, LANES))
         return jnp.concatenate(out, axis=2)
     per_slab = p.cs // LANES
-    half = max(p.ta // 2, 1)
 
     def body(swap_hbm, velocity_ref, out, x, sems, table_sems, wide, swap):
         table = pltpu.make_async_copy(swap_hbm, swap, table_sems.at[0])
-        table.start()
-        copies = {}
+        copies = []
         for n, quantity in enumerate((2, 0)):
-            for start in range(0, p.ta, half):
-                columns = slice(start * p.cs, (start + half) * p.cs)
-                copies[n, start] = pltpu.make_async_copy(
-                    velocity_ref.at[quantity, :, :, columns], x.at[n, :, :, columns], sems.at[n, start]
-                )
-                copies[n, start].start()
+            copies.append(pltpu.make_async_copy(velocity_ref.at[quantity], x.at[n], sems.at[n]))
+            copies[-1].start()
+            if n == 0:
+                table.start()
         table.wait()
         count = p.rg * p.tl
+        tiles = range(p.zb // LANES)
         for n in range(2):
-            for start in range(0, p.ta, half):
-                copies[n, start].wait()
-                tiles = range(start * per_slab, (start + half) * per_slab)
-                for tile in tiles:
-                    spread_rows(p, wide, tile, x[n, :, :, tile * LANES : (tile + 1) * LANES])
-                swapped = jnp.dot(
-                    rows_by_snapshot(p, wide, tiles), swap[...], preferred_element_type=jnp.float32
-                )
-                for tile in tiles:
-                    at = (tile - tiles[0]) * count
-                    m, i = divmod(tile, per_slab)
-                    for g in range(p.groups):
-                        mine = swapped[at : at + count, g * LANES : (g + 1) * LANES]
-                        out[i * p.groups + g, m, n * p.rg : (n + 1) * p.rg] = mine.reshape(
-                            p.rg, p.tl, LANES
-                        ).astype(jnp.bfloat16)
+            copies[n].wait()
+            for tile in tiles:
+                spread_rows(p, wide, tile, x[n, :, :, tile * LANES : (tile + 1) * LANES])
+            swapped = jnp.dot(
+                rows_by_snapshot(p, wide, tiles), swap[...], preferred_element_type=jnp.float32
+            )
+            for tile in tiles:
+                m, i = divmod(tile, per_slab)
+                for g in range(p.groups):
+                    mine = swapped[tile * count : (tile + 1) * count, g * LANES : (g + 1) * LANES]
+                    out[i * p.groups + g, m, n * p.rg : (n + 1) * p.rg] = mine.reshape(
+                        p.rg, p.tl, LANES
+                    ).astype(jnp.bfloat16)
 
     swap = group_swap(p)
     scratch = [
         pltpu.VMEM((2, p.tl, p.xb, p.zb), velocity.dtype),
-        pltpu.SemaphoreType.DMA((2, p.ta)),
+        pltpu.SemaphoreType.DMA((2,)),
         pltpu.SemaphoreType.DMA((1,)),
         pltpu.VMEM((p.zb // LANES, p.groups, p.tl * p.rg, LANES), jnp.float32),
         pltpu.VMEM(swap.shape, swap.dtype),
@@ -447,25 +441,29 @@
     def body(place_ref, *refs):
         xs, swap = refs[: len(pieces)], refs[len(pieces)]
         out, by_chunk, wide, held, sems = refs[-5:]
-        copies = []
-        for n, quantity in enumerate(quantities):
+        copies, lhs = [], []
+        tiles = p.cs // LANES
+        for n in range(len(quantities)):
             for j in range(p.blocks):
                 if len(pieces) > 1:
-                    by_chunk[place_ref[1] ^ j] = xs[j][n].reshape(p.rg * ROWS, LANES)
+                    by_chunk[n, place_ref[1] ^ j] = xs[j][n].reshape(p.rg * ROWS, LANES)
                 else:
-                    by_chunk[j] = xs[0][j, n].reshape(p.rg * ROWS, LANES)
-            for tile in range(p.cs // LANES):
-                lhs = [by_chunk[tile * p.groups + i] for i in range(p.groups)]
-                swapped = jnp.dot(
-                    jnp.concatenate(lhs, axis=1), swap[...], preferred_element_type=jnp.float32
-                )
+                    by_chunk[n, j] = xs[0][j, n].reshape(p.rg * ROWS, LANES)
+            for tile in range(tiles):
+                columns = [by_chunk[n, tile * p.groups + i] for i in range(p.groups)]
+                lhs.append(jnp.concatenate(columns, axis=1))
+        swapped = jnp.dot(jnp.concatenate(lhs, axis=0), swap[...], preferred_element_type=jnp.float32)
+        count = p.rg * ROWS
+        for n, quantity in enumerate(quantities):
+            for tile in range(tiles):
+                at = (n * tiles + tile) * count
                 for g in range(p.groups):
-                    wide[tile, g] = swapped[:, g * LANES : (g + 1) * LANES]
+                    wide[n, tile, g] = swapped[at : at + count, g * LANES : (g + 1) * LANES]
             for part in range(2):
                 for k in range(F):
-                    for tile in range(p.cs // LANES):
+                    for tile in range(tiles):
                         for g in range(p.groups):
-                            block = wide[tile, g, pl.ds(part * 8 + k, p.rg, stride=ROWS), :]
+                            block = wide[n, tile, g, pl.ds(part * 8 + k, p.rg, stride=ROWS), :]
                             rows = slice(g * p.rg, (g + 1) * p.rg)
                             held[n, part, k, rows, tile * LANES : (tile + 1) * LANES] = block
                 copies.append(
@@ -477,8 +475,8 @@
 
     before = [] if so_far is None else [so_far]
     scratch = [
-        pltpu.VMEM((p.blocks, p.rg * ROWS, LANES), jnp.bfloat16),
-        pltpu.VMEM((p.cs // LANES, p.groups, p.rg * ROWS, LANES), jnp.float32),
+        pltpu.VMEM((len(quantities), p.blocks, p.rg * ROWS, LANES), jnp.bfloat16),
+        pltpu.VMEM((len(quantities), p.cs // LANES, p.groups, p.rg * ROWS, LANES), jnp.float32),
         pltpu.VMEM((len(quantities),) + shape[1:], jnp.float32),
         pltpu.SemaphoreType.DMA((len(quantities), 2)),
     ]

time: 90.9 us -> 90.4 us (level)
  no operation moved by 1% of the time
where the time goes in v5:
time: 90.4 us; the launch traced here: 89.8 us
  waiting for transfers between devices  42 us (46%)
  starting transfers between devices  29.6 us (33%)
  Pallas kernels  17 us (19%)
    all_to_all x1, waiting for transfers between devices, shards(): lax.all_to_all(both, block_axes + ('ta',), split_axis=0, concat_axis=0, t...  23.8 us
    ppermute x17, starting transfers between devices, trade(): return lax.ppermute(x, axis, [(i, i ^ step) for i in range(count)])  18.2 us
    ppermute x17, waiting for transfers between devices, trade(): return lax.ppermute(x, axis, [(i, i ^ step) for i in range(count)])  18.2 us
    pallas_call x8, Pallas kernels, on_chip(): pl.pallas_call(body, in_specs=[smem] * len(scalars) + [vmem] * count + [h...  17 us
    all_to_all x1, starting transfers between devices, shards(): lax.all_to_all(both, block_axes + ('ta',), split_axis=0, concat_axis=0, t...  7.33 us
    all_to_all x1, starting transfers between devices, over_blocks(): lax.all_to_all(arrays[0], block_axes, split_axis=0, concat_axis=0, tiled=...  4.03 us
  transfers between devices with their start and end apart: 19, of which 10 were waited for; matrix products, arithmetic and copies ran while one was open for 1% of the time, Pallas kernels for 10%

profile of v5, /device:TPU:0, one launch (start us, length us, event | category | flops | bytes accessed | tf_op | source)
XLA Modules:
  0.0 89.8 jit_solution(8474529776274352325)
XLA Ops:
  0.0 3.1 %shard_map.100.packed_ref = bf16[8,4,16,8,128]{4,3,2,1,0:T(8,128)(2,1)} custom-call(bf16[512,512]{1,0:T(8,128)(2,1)} %constant.58.clone.swap_hbm.swap.refs_1_.refs_8_, bf16[3,8,32,1024]{3,2,1,0:T(8,128)(2,1)} %velocity_ref.3), custom_call_target="tpu_custom_call" | custom-call | tf_op jit(solution)/shard_map/pallas_call | solution.py:46
  3.1 7.3 %all-to-all-start = ((bf16[32,16,8,128]{3,2,1,0:T(8,128)(2,1)}), bf16[32,16,8,128]{3,2,1,0:T(8,128)(2,1)S(1)}, u32[]{:S(2)}, u32[]{:S(2)}) async-start(bf16[32,16,8,128]{3,2,1,0:T(8,128)(2,1)} %bitcast.3), calls=%async_computation | async-start | bytes 2097152 | tf_op jit(solution)/shard_map/all_to_all | solution.py:502
  11.6 23.8 %all-to-all-done = bf16[32,16,8,128]{3,2,1,0:T(8,128)(2,1)S(1)} async-done(((bf16[32,16,8,128]{3,2,1,0:T(8,128)(2,1)}), bf16[32,16,8,128]{3,2,1,0:T(8,128)(2,1)S(1)}, u32[]{:S(2)}, u32[]{:S(2)}) %all-to-all-start) | async-done | bytes 1048608 | tf_op jit(solution)/shard_map/all_to_all | solution.py:502
  35.4 3.1 %shard_map.105 = bf16[8,2,8,16,128]{4,3,2,1,0:T(8,128)(2,1)} custom-call(s32[7]{0:T(128)S(1)} %copy-done.4, s32[2]{0:T(128)S(1)} %pad_add_fusion.place_ref, bf16[8,4,16,8,128]{4,3,2,1,0:T(8,128)(2,1)S(1)} %bitcast.6, bf16[112,32]{1,0:T(8,128)(2,1)S(1)} %bitcast.8), custom_call_target="tpu_custom_call" | custom-call | tf_op jit(solution)/shard_map/pallas_call | solution.py:46
  38.5 4.0 %all-to-all-start.1 = ((bf16[8,2,8,16,128]{4,3,2,1,0:T(8,128)(2,1)}), bf16[8,2,8,16,128]{4,3,2,1,0:T(8,128)(2,1)S(1)}, u32[]{:S(2)}, u32[]{:S(2)}) async-start(bf16[8,2,8,16,128]{4,3,2,1,0:T(8,128)(2,1)} %shard_map.105), calls=%async_computation.1 | async-start | bytes 1048576 | tf_op jit(solution)/shard_map/all_to_all | solution.py:507
  42.6 3.5 %shard_map.101 = (bf16[4,9,8,128]{3,2,1,0:T(8,128)(2,1)S(1)}, bf16[4,9,8,128]{3,2,1,0:T(8,128)(2,1)S(1)}, bf16[4,9,8,128]{3,2,1,0:T(8,128)(2,1)S(1)}, bf16[4,9,8...) custom-call(s32[2]{0:T(128)S(1)} %pad_add_fusion.place_ref, ...), custom_call_target="tpu_custom_call" | custom-call | tf_op jit(solution)/shard_map/pallas_call | solution.py:46
  46.1 1.2 %collective-permute-start = (bf16[4,9,8,128]{3,2,1,0:T(8,128)(2,1)S(1)}, bf16[4,9,8,128]{3,2,1,0:T(8,128)(2,1)S(1)}, u32[]{:S(2)}, u32[]{:S(2)}) collective-permute-start(bf16[4,9,8,128]{3,2,1,0:T(8,128)(2,1)S(1)} %get-tuple-element.26), channel_id=1, source_target_pairs={{0,4},{4,0},{8,12},{12,8},{16,20},{20,16},{24,28},{28,24},{1,5},{5... | collective-permute-start | bytes 221192 | tf_op jit(solution)/shard_map/ppermute | solution.py:71
  47.2 1.4 %collective-permute-start.1 = (bf16[4,9,8,128]{3,2,1,0:T(8,128)(2,1)S(1)}, bf16[4,9,8,128]{3,2,1,0:T(8,128)(2,1)S(1)}, u32[]{:S(2)}, u32[]{:S(2)}) collective-permute-start(bf16[4,9,8,128]{3,2,1,0:T(8,128)(2,1)S(1)} %get-tuple-element.27), channel_id=1, source_target_pairs={{0,8},{4,12},{8,0},{12,4},{16,24},{20,28},{24,16},{28,20},{1,9},{5... | collective-permute-start | bytes 221192 | tf_op jit(solution)/shard_map/ppermute | solution.py:71
  48.7 1.5 %collective-permute-start.3 = (bf16[4,9,8,128]{3,2,1,0:T(8,128)(2,1)S(1)}, bf16[4,9,8,128]{3,2,1,0:T(8,128)(2,1)S(1)}, u32[]{:S(2)}, u32[]{:S(2)}) collective-permute-start(bf16[4,9,8,128]{3,2,1,0:T(8,128)(2,1)S(1)} %get-tuple-element.29), channel_id=1, source_target_pairs={{0,16},{4,20},{8,24},{12,28},{16,0},{20,4},{24,8},{28,12},{1,17},{... | collective-permute-start | bytes 221192 | tf_op jit(solution)/shard_map/ppermute | solution.py:71
  50.1 0.6 collective-permute-start.4
  50.7 1.9 %collective-permute-start.5 = (bf16[4,9,8,128]{3,2,1,0:T(8,128)(2,1)S(1)}, bf16[4,9,8,128]{3,2,1,0:T(8,128)(2,1)S(1)}, u32[]{:S(2)}, u32[]{:S(2)}) collective-permute-start(bf16[4,9,8,128]{3,2,1,0:T(8,128)(2,1)S(1)} %get-tuple-element.31), channel_id=1, source_target_pairs={{0,24},{4,28},{8,16},{12,20},{16,8},{20,12},{24,0},{28,4},{1,25},{... | collective-permute-start | bytes 221192 | tf_op jit(solution)/shard_map/ppermute | solution.py:71
  52.7 0.8 collective-permute-done.1.refs_2_
  53.5 0.6 collective-permute-start.6
  54.1 0.6 collective-permute-done.2.refs_3_
  54.8 2.9 %collective-permute-done.5.refs_6_ = bf16[4,9,8,128]{3,2,1,0:T(8,128)(2,1)S(1)} collective-permute-done((bf16[4,9,8,128]{3,2,1,0:T(8,128)(2,1)S(1)}, bf16[4,9,8,128]{3,2,1,0:T(8,128)(2,1)S(1)}, u32[]{:S(2)}, u32[]{:S(2)}) %collective-permute-start.5) | collective-permute-done | bytes 73760 | tf_op jit(solution)/shard_map/ppermute | solution.py:71
  57.8 1.2 %collective-permute-done.6.refs_7_ = bf16[4,9,8,128]{3,2,1,0:T(8,128)(2,1)S(1)} collective-permute-done((bf16[4,9,8,128]{3,2,1,0:T(8,128)(2,1)S(1)}, bf16[4,9,8,128]{3,2,1,0:T(8,128)(2,1)S(1)}, u32[]{:S(2)}, u32[]{:S(2)}) %collective-permute-start.6) | collective-permute-done | bytes 73760 | tf_op jit(solution)/shard_map/ppermute | solution.py:71
  59.0 2.3 %collective-permute-start.7 = (bf16[8,9,8,128]{3,2,1,0:T(8,128)(2,1)S(1)}, bf16[8,9,8,128]{3,2,1,0:T(8,128)(2,1)S(1)}, u32[]{:S(2)}, u32[]{:S(2)}) collective-permute-start(bf16[8,9,8,128]{3,2,1,0:T(8,128)(2,1)S(1)} %get-tuple-element.34), channel_id=1, source_target_pairs={{0,1},{1,0},{2,3},{3,2},{4,5},{5,4},{6,7},{7,6},{8,9},{9,8},{10,11... | collective-permute-start | bytes 442376 | tf_op jit(solution)/shard_map/ppermute | solution.py:71
  61.4 0.7 collective-permute-start.8
  62.1 1.7 %collective-permute-start.9 = (bf16[8,9,8,128]{3,2,1,0:T(8,128)(2,1)S(1)}, bf16[8,9,8,128]{3,2,1,0:T(8,128)(2,1)S(1)}, u32[]{:S(2)}, u32[]{:S(2)}) collective-permute-start(bf16[8,9,8,128]{3,2,1,0:T(8,128)(2,1)S(1)} %get-tuple-element.36), channel_id=1, source_target_pairs={{0,3},{1,2},{2,1},{3,0},{4,7},{5,6},{6,5},{7,4},{8,11},{9,10},{10,... | collective-permute-start | bytes 442376 | tf_op jit(solution)/shard_map/ppermute | solution.py:71
  63.8 0.7 shard_map.103.refs_5_
  64.5 1.7 %collective-permute-done.7.refs_1_ = bf16[8,9,8,128]{3,2,1,0:T(8,128)(2,1)S(1)} collective-permute-done((bf16[8,9,8,128]{3,2,1,0:T(8,128)(2,1)S(1)}, bf16[8,9,8,128]{3,2,1,0:T(8,128)(2,1)S(1)}, u32[]{:S(2)}, u32[]{:S(2)}) %collective-permute-start.7) | collective-permute-done | bytes 147488 | tf_op jit(solution)/shard_map/ppermute | solution.py:71
  66.1 8.5 %collective-permute-done.8.refs_2_ = bf16[8,9,8,128]{3,2,1,0:T(8,128)(2,1)S(1)} collective-permute-done((bf16[8,9,8,128]{3,2,1,0:T(8,128)(2,1)S(1)}, bf16[8,9,8,128]{3,2,1,0:T(8,128)(2,1)S(1)}, u32[]{:S(2)}, u32[]{:S(2)}) %collective-permute-start.8) | collective-permute-done | bytes 147488 | tf_op jit(solution)/shard_map/ppermute | solution.py:71
  74.7 2.6 %shard_map.104 = (bf16[2,8,16,128]{3,2,1,0:T(8,128)(2,1)S(1)}, bf16[2,8,16,128]{3,2,1,0:T(8,128)(2,1)S(1)}, bf16[2,8,16,128]{3,2,1,0:T(8,128)(2,1)S(1)}, bf16[2,...) custom-call(s32[7]{0:T(128)S(1)} %copy-done.4, ...), custom_call_target="tpu_custom_call" | custom-call | tf_op jit(solution)/shard_map/pallas_call | solution.py:46
  77.3 0.4 collective-permute-start.11
  77.8 1.4 %collective-permute-start.12 = (bf16[2,8,16,128]{3,2,1,0:T(8,128)(2,1)S(1)}, bf16[2,8,16,128]{3,2,1,0:T(8,128)(2,1)S(1)}, u32[]{:S(2)}, u32[]{:S(2)}) collective-permute-start(bf16[2,8,16,128]{3,2,1,0:T(8,128)(2,1)S(1)} %get-tuple-element.40), channel_id=1, source_target_pairs={{0,12},{4,8},{8,4},{12,0},{16,28},{20,24},{24,20},{28,16},{1,13},{... | collective-permute-start | bytes 196616 | tf_op jit(solution)/shard_map/ppermute | solution.py:71
  79.2 1.5 %collective-permute-start.13 = (bf16[2,8,16,128]{3,2,1,0:T(8,128)(2,1)S(1)}, bf16[2,8,16,128]{3,2,1,0:T(8,128)(2,1)S(1)}, u32[]{:S(2)}, u32[]{:S(2)}) collective-permute-start(bf16[2,8,16,128]{3,2,1,0:T(8,128)(2,1)S(1)} %get-tuple-element.41), channel_id=1, source_target_pairs={{0,16},{4,20},{8,24},{12,28},{16,0},{20,4},{24,8},{28,12},{1,17},{... | collective-permute-start | bytes 196616 | tf_op jit(solution)/shard_map/ppermute | solution.py:71
  80.9 1.6 %collective-permute-start.15 = (bf16[2,8,16,128]{3,2,1,0:T(8,128)(2,1)S(1)}, bf16[2,8,16,128]{3,2,1,0:T(8,128)(2,1)S(1)}, u32[]{:S(2)}, u32[]{:S(2)}) collective-permute-start(bf16[2,8,16,128]{3,2,1,0:T(8,128)(2,1)S(1)} %get-tuple-element.43), channel_id=1, source_target_pairs={{0,24},{4,28},{8,16},{12,20},{16,8},{20,12},{24,0},{28,4},{1,25},{... | collective-permute-start | bytes 196616 | tf_op jit(solution)/shard_map/ppermute | solution.py:71
  82.6 1.0 %collective-permute-start.16 = (bf16[2,8,16,128]{3,2,1,0:T(8,128)(2,1)S(1)}, bf16[2,8,16,128]{3,2,1,0:T(8,128)(2,1)S(1)}, u32[]{:S(2)}, u32[]{:S(2)}) collective-permute-start(bf16[2,8,16,128]{3,2,1,0:T(8,128)(2,1)S(1)} %get-tuple-element.44), channel_id=1, source_target_pairs={{0,28},{4,24},{8,20},{12,16},{16,12},{20,8},{24,4},{28,0},{1,29},{... | collective-permute-start | bytes 196616 | tf_op jit(solution)/shard_map/ppermute | solution.py:71
  83.6 2.0 %shard_map.106.refs_9_ = f32[4,2,7,32,256]{4,3,2,1,0:T(8,128)} custom-call(s32[2]{0:T(128)S(1)} %pad_add_fusion.place_ref, bf16[8,2,8,16,128]{4,3,2,1,0:T(8,128)(2,1)S(1)} %all-to-all-done.1.refs_0_, bf16[512,512]{1,0:T(8,128)(2,1)S(1)} %copy-done), custom_call_target="tpu_custom_call" | custom-call | tf_op jit(solution)/shard_map/pallas_call | solution.py:46
  85.6 1.2 %collective-permute-done.15.refs_6_ = bf16[2,8,16,128]{3,2,1,0:T(8,128)(2,1)S(1)} collective-permute-done((bf16[2,8,16,128]{3,2,1,0:T(8,128)(2,1)S(1)}, bf16[2,8,16,128]{3,2,1,0:T(8,128)(2,1)S(1)}, u32[]{:S(2)}, u32[]{:S(2)}) %collective-permute-start.15) | collective-permute-done | bytes 65568 | tf_op jit(solution)/shard_map/ppermute | solution.py:71
  86.8 1.0 %collective-permute-done.16.refs_7_ = bf16[2,8,16,128]{3,2,1,0:T(8,128)(2,1)S(1)} collective-permute-done((bf16[2,8,16,128]{3,2,1,0:T(8,128)(2,1)S(1)}, bf16[2,8,16,128]{3,2,1,0:T(8,128)(2,1)S(1)}, u32[]{:S(2)}, u32[]{:S(2)}) %collective-permute-start.16) | collective-permute-done | bytes 65568 | tf_op jit(solution)/shard_map/ppermute | solution.py:71
  87.8 2.0 %shard_map.107 = f32[4,2,7,32,256]{4,3,2,1,0:T(8,128)} custom-call(s32[2]{0:T(128)S(1)} %pad_add_fusion.place_ref, bf16[2,8,16,128]{3,2,1,0:T(8,128)(2,1)S(1)} %get-tuple-element.37.refs_0_, bf16[2,8,16,128]{3,2,1,0:T(8,128)(2,1)S(1)} %collective-permute-done.10.refs_1_, ...), custom_call_target="tpu_custom_call", output_to_operand_aliasing={{}: (10, {})} | custom-call | tf_op jit(solution)/shard_map/pallas_call | solution.py:46
  (40 shorter events, 1.6 us)
Async XLA Ops:
  3.1 7.8 %copy-start.5 = (s32[7]{0:T(128)S(1)}, s32[7]{0:T(128)}, u32[]{:S(2)}) copy-start(s32[7]{0:T(128)} %param.11) | copy-start | bytes 88
  3.1 32.3 %copy-start.4 = (s32[7]{0:T(128)S(1)}, s32[7]{0:T(128)}, u32[]{:S(2)}) copy-start(s32[7]{0:T(128)} %owner_ref.3) | copy-start | bytes 88
  3.1 32.3 %all-to-all-start = ((bf16[32,16,8,128]{3,2,1,0:T(8,128)(2,1)}), bf16[32,16,8,128]{3,2,1,0:T(8,128)(2,1)S(1)}, u32[]{:S(2)}, u32[]{:S(2)}) async-start(bf16[32,16,8,128]{3,2,1,0:T(8,128)(2,1)} %bitcast.3), calls=%async_computation | async-start | bytes 2097152 | tf_op jit(solution)/shard_map/all_to_all | solution.py:502
  10.5 32.1 %copy-start = (bf16[512,512]{1,0:T(8,128)(2,1)S(1)}, bf16[512,512]{1,0:T(8,128)(2,1)}, u32[]{:S(2)}) copy-start(bf16[512,512]{1,0:T(8,128)(2,1)} %constant.58.clone.swap_hbm.swap.refs_1_.refs_8_) | copy-start | bytes 1572868
  10.5 32.1 %copy-start.1 = (bf16[1024,256]{1,0:T(8,128)(2,1)S(1)}, bf16[1024,256]{1,0:T(8,128)(2,1)}, u32[]{:S(2)}) copy-start(bf16[1024,256]{1,0:T(8,128)(2,1)} %constant.59.clone.picks) | copy-start | bytes 1572868
  38.5 45.1 %all-to-all-start.1 = ((bf16[8,2,8,16,128]{4,3,2,1,0:T(8,128)(2,1)}), bf16[8,2,8,16,128]{4,3,2,1,0:T(8,128)(2,1)S(1)}, u32[]{:S(2)}, u32[]{:S(2)}) async-start(bf16[8,2,8,16,128]{4,3,2,1,0:T(8,128)(2,1)} %shard_map.105), calls=%async_computation.1 | async-start | bytes 1048576 | tf_op jit(solution)/shard_map/all_to_all | solution.py:507
  42.6 21.2 %copy-start.3 = (bf16[128,128]{1,0:T(8,128)(2,1)S(1)}, bf16[128,128]{1,0:T(8,128)(2,1)}, u32[]{:S(2)}) copy-start(bf16[128,128]{1,0:T(8,128)(2,1)} %constant.60.clone.inner_ref) | copy-start | bytes 98308
  46.0 28.6 %copy-start.2 = (bf16[128,1024]{1,0:T(8,128)(2,1)S(1)}, bf16[128,1024]{1,0:T(8,128)(2,1)}, u32[]{:S(2)}) copy-start(bf16[128,1024]{1,0:T(8,128)(2,1)} %constant.61.clone.refs_7_) | copy-start | bytes 786436
  46.1 4.7 %collective-permute-start = (bf16[4,9,8,128]{3,2,1,0:T(8,128)(2,1)S(1)}, bf16[4,9,8,128]{3,2,1,0:T(8,128)(2,1)S(1)}, u32[]{:S(2)}, u32[]{:S(2)}) collective-permute-start(bf16[4,9,8,128]{3,2,1,0:T(8,128)(2,1)S(1)} %get-tuple-element.26), channel_id=1, source_target_pairs={{0,4},{4,0},{8,12},{12,8},{16,20},{20,16},{24,28},{28,24},{1,5},{5... | collective-permute-start | bytes 221192 | tf_op jit(solution)/shard_map/ppermute | solution.py:71
  47.2 6.3 %collective-permute-start.1 = (bf16[4,9,8,128]{3,2,1,0:T(8,128)(2,1)S(1)}, bf16[4,9,8,128]{3,2,1,0:T(8,128)(2,1)S(1)}, u32[]{:S(2)}, u32[]{:S(2)}) collective-permute-start(bf16[4,9,8,128]{3,2,1,0:T(8,128)(2,1)S(1)} %get-tuple-element.27), channel_id=1, source_target_pairs={{0,8},{4,12},{8,0},{12,4},{16,24},{20,28},{24,16},{28,20},{1,9},{5... | collective-permute-start | bytes 221192 | tf_op jit(solution)/shard_map/ppermute | solution.py:71
  48.7 6.0 %collective-permute-start.2 = (bf16[4,9,8,128]{3,2,1,0:T(8,128)(2,1)S(1)}, bf16[4,9,8,128]{3,2,1,0:T(8,128)(2,1)S(1)}, u32[]{:S(2)}, u32[]{:S(2)}) collective-permute-start(bf16[4,9,8,128]{3,2,1,0:T(8,128)(2,1)S(1)} %get-tuple-element.28), channel_id=1, source_target_pairs={{0,12},{4,8},{8,4},{12,0},{16,28},{20,24},{24,20},{28,16},{1,13},{... | collective-permute-start | bytes 221192 | tf_op jit(solution)/shard_map/ppermute | solution.py:71
  48.7 6.0 %collective-permute-start.3 = (bf16[4,9,8,128]{3,2,1,0:T(8,128)(2,1)S(1)}, bf16[4,9,8,128]{3,2,1,0:T(8,128)(2,1)S(1)}, u32[]{:S(2)}, u32[]{:S(2)}) collective-permute-start(bf16[4,9,8,128]{3,2,1,0:T(8,128)(2,1)S(1)} %get-tuple-element.29), channel_id=1, source_target_pairs={{0,16},{4,20},{8,24},{12,28},{16,0},{20,4},{24,8},{28,12},{1,17},{... | collective-permute-start | bytes 221192 | tf_op jit(solution)/shard_map/ppermute | solution.py:71
  50.1 4.7 %collective-permute-start.4 = (bf16[4,9,8,128]{3,2,1,0:T(8,128)(2,1)S(1)}, bf16[4,9,8,128]{3,2,1,0:T(8,128)(2,1)S(1)}, u32[]{:S(2)}, u32[]{:S(2)}) collective-permute-start(bf16[4,9,8,128]{3,2,1,0:T(8,128)(2,1)S(1)} %get-tuple-element.30), channel_id=1, source_target_pairs={{0,20},{4,16},{8,28},{12,24},{16,4},{20,0},{24,12},{28,8},{1,21},{... | collective-permute-start | bytes 221192 | tf_op jit(solution)/shard_map/ppermute | solution.py:71
  50.7 7.0 %collective-permute-start.5 = (bf16[4,9,8,128]{3,2,1,0:T(8,128)(2,1)S(1)}, bf16[4,9,8,128]{3,2,1,0:T(8,128)(2,1)S(1)}, u32[]{:S(2)}, u32[]{:S(2)}) collective-permute-start(bf16[4,9,8,128]{3,2,1,0:T(8,128)(2,1)S(1)} %get-tuple-element.31), channel_id=1, source_target_pairs={{0,24},{4,28},{8,16},{12,20},{16,8},{20,12},{24,0},{28,4},{1,25},{... | collective-permute-start | bytes 221192 | tf_op jit(solution)/shard_map/ppermute | solution.py:71
  53.5 5.5 %collective-permute-start.6 = (bf16[4,9,8,128]{3,2,1,0:T(8,128)(2,1)S(1)}, bf16[4,9,8,128]{3,2,1,0:T(8,128)(2,1)S(1)}, u32[]{:S(2)}, u32[]{:S(2)}) collective-permute-start(bf16[4,9,8,128]{3,2,1,0:T(8,128)(2,1)S(1)} %get-tuple-element.32), channel_id=1, source_target_pairs={{0,28},{4,24},{8,20},{12,16},{16,12},{20,8},{24,4},{28,0},{1,29},{... | collective-permute-start | bytes 221192 | tf_op jit(solution)/shard_map/ppermute | solution.py:71
  59.0 7.1 %collective-permute-start.7 = (bf16[8,9,8,128]{3,2,1,0:T(8,128)(2,1)S(1)}, bf16[8,9,8,128]{3,2,1,0:T(8,128)(2,1)S(1)}, u32[]{:S(2)}, u32[]{:S(2)}) collective-permute-start(bf16[8,9,8,128]{3,2,1,0:T(8,128)(2,1)S(1)} %get-tuple-element.34), channel_id=1, source_target_pairs={{0,1},{1,0},{2,3},{3,2},{4,5},{5,4},{6,7},{7,6},{8,9},{9,8},{10,11... | collective-permute-start | bytes 442376 | tf_op jit(solution)/shard_map/ppermute | solution.py:71
  61.4 13.3 %collective-permute-start.8 = (bf16[8,9,8,128]{3,2,1,0:T(8,128)(2,1)S(1)}, bf16[8,9,8,128]{3,2,1,0:T(8,128)(2,1)S(1)}, u32[]{:S(2)}, u32[]{:S(2)}) collective-permute-start(bf16[8,9,8,128]{3,2,1,0:T(8,128)(2,1)S(1)} %get-tuple-element.35), channel_id=1, source_target_pairs={{0,2},{1,3},{2,0},{3,1},{4,6},{5,7},{6,4},{7,5},{8,10},{9,11},{10,... | collective-permute-start | bytes 442376 | tf_op jit(solution)/shard_map/ppermute | solution.py:71
  62.1 12.6 %collective-permute-start.9 = (bf16[8,9,8,128]{3,2,1,0:T(8,128)(2,1)S(1)}, bf16[8,9,8,128]{3,2,1,0:T(8,128)(2,1)S(1)}, u32[]{:S(2)}, u32[]{:S(2)}) collective-permute-start(bf16[8,9,8,128]{3,2,1,0:T(8,128)(2,1)S(1)} %get-tuple-element.36), channel_id=1, source_target_pairs={{0,3},{1,2},{2,1},{3,0},{4,7},{5,6},{6,5},{7,4},{8,11},{9,10},{10,... | collective-permute-start | bytes 442376 | tf_op jit(solution)/shard_map/ppermute | solution.py:71
  77.3 3.6 %collective-permute-start.10 = (bf16[2,8,16,128]{3,2,1,0:T(8,128)(2,1)S(1)}, bf16[2,8,16,128]{3,2,1,0:T(8,128)(2,1)S(1)}, u32[]{:S(2)}, u32[]{:S(2)}) collective-permute-start(bf16[2,8,16,128]{3,2,1,0:T(8,128)(2,1)S(1)} %get-tuple-element.38), channel_id=1, source_target_pairs={{0,4},{4,0},{8,12},{12,8},{16,20},{20,16},{24,28},{28,24},{1,5},{5... | collective-permute-start | bytes 196616 | tf_op jit(solution)/shard_map/ppermute | solution.py:71
  77.3 5.2 %collective-permute-start.11 = (bf16[2,8,16,128]{3,2,1,0:T(8,128)(2,1)S(1)}, bf16[2,8,16,128]{3,2,1,0:T(8,128)(2,1)S(1)}, u32[]{:S(2)}, u32[]{:S(2)}) collective-permute-start(bf16[2,8,16,128]{3,2,1,0:T(8,128)(2,1)S(1)} %get-tuple-element.39), channel_id=1, source_target_pairs={{0,8},{4,12},{8,0},{12,4},{16,24},{20,28},{24,16},{28,20},{1,9},{5... | collective-permute-start | bytes 196616 | tf_op jit(solution)/shard_map/ppermute | solution.py:71
  77.8 7.8 %collective-permute-start.12 = (bf16[2,8,16,128]{3,2,1,0:T(8,128)(2,1)S(1)}, bf16[2,8,16,128]{3,2,1,0:T(8,128)(2,1)S(1)}, u32[]{:S(2)}, u32[]{:S(2)}) collective-permute-start(bf16[2,8,16,128]{3,2,1,0:T(8,128)(2,1)S(1)} %get-tuple-element.40), channel_id=1, source_target_pairs={{0,12},{4,8},{8,4},{12,0},{16,28},{20,24},{24,20},{28,16},{1,13},{... | collective-permute-start | bytes 196616 | tf_op jit(solution)/shard_map/ppermute | solution.py:71
  79.2 6.4 %collective-permute-start.13 = (bf16[2,8,16,128]{3,2,1,0:T(8,128)(2,1)S(1)}, bf16[2,8,16,128]{3,2,1,0:T(8,128)(2,1)S(1)}, u32[]{:S(2)}, u32[]{:S(2)}) collective-permute-start(bf16[2,8,16,128]{3,2,1,0:T(8,128)(2,1)S(1)} %get-tuple-element.41), channel_id=1, source_target_pairs={{0,16},{4,20},{8,24},{12,28},{16,0},{20,4},{24,8},{28,12},{1,17},{... | collective-permute-start | bytes 196616 | tf_op jit(solution)/shard_map/ppermute | solution.py:71
  80.7 4.9 %collective-permute-start.14 = (bf16[2,8,16,128]{3,2,1,0:T(8,128)(2,1)S(1)}, bf16[2,8,16,128]{3,2,1,0:T(8,128)(2,1)S(1)}, u32[]{:S(2)}, u32[]{:S(2)}) collective-permute-start(bf16[2,8,16,128]{3,2,1,0:T(8,128)(2,1)S(1)} %get-tuple-element.42), channel_id=1, source_target_pairs={{0,20},{4,16},{8,28},{12,24},{16,4},{20,0},{24,12},{28,8},{1,21},{... | collective-permute-start | bytes 196616 | tf_op jit(solution)/shard_map/ppermute | solution.py:71
  80.9 5.9 %collective-permute-start.15 = (bf16[2,8,16,128]{3,2,1,0:T(8,128)(2,1)S(1)}, bf16[2,8,16,128]{3,2,1,0:T(8,128)(2,1)S(1)}, u32[]{:S(2)}, u32[]{:S(2)}) collective-permute-start(bf16[2,8,16,128]{3,2,1,0:T(8,128)(2,1)S(1)} %get-tuple-element.43), channel_id=1, source_target_pairs={{0,24},{4,28},{8,16},{12,20},{16,8},{20,12},{24,0},{28,4},{1,25},{... | collective-permute-start | bytes 196616 | tf_op jit(solution)/shard_map/ppermute | solution.py:71
  82.6 5.3 %collective-permute-start.16 = (bf16[2,8,16,128]{3,2,1,0:T(8,128)(2,1)S(1)}, bf16[2,8,16,128]{3,2,1,0:T(8,128)(2,1)S(1)}, u32[]{:S(2)}, u32[]{:S(2)}) collective-permute-start(bf16[2,8,16,128]{3,2,1,0:T(8,128)(2,1)S(1)} %get-tuple-element.44), channel_id=1, source_target_pairs={{0,28},{4,24},{8,20},{12,16},{16,12},{20,8},{24,4},{28,0},{1,29},{... | collective-permute-start | bytes 196616 | tf_op jit(solution)/shard_map/ppermute | solution.py:71
